TPU v7x, 256 devices: a whole 4x4x8 slice. The times are simulated.
256 devices in a mesh: dp: 128 (over z, x, y_hi, core), mp: 2 (over y_lo).
Axes of the slice: x: 4, y: 4 (y_hi: 2, y_lo: 2; y = y_hi * 2 + y_lo), z: 8, core: 2. Of those that a mesh axis runs over, the one named last changes fastest.
Arguments:
- features: bfloat16 [16384, 512], P('dp'), may hold values from -6 to 6
- w_in: bfloat16 [512, 512], P(None, 'mp'), may hold values from -0.25 to 0.25
- b_in: float32 [512], P('mp'), may hold values from -1 to 1
- w_out: bfloat16 [512, 128], P('mp'), may hold values from -0.25 to 0.25
- partner: int32 [16384], P('dp'), may hold values from 0 to 16383, as said below
- window: int32 [128], replicated, may hold values from 0 to 3
Outputs:
- row_loss: float32 [4096], P('dp')
- grad_w_in: float32 [512, 512], P(None, 'mp')
- grad_b_in: float32 [512], P('mp')
- grad_w_out: float32 [512, 128], P('mp')
Inputs may be any that keep to these rules, and one draw needn't show every extreme that they name: partner pairs the rows: partner[partner[i]] = i and partner[i] != i for every row i.
All inputs are finite; a program needn't handle non-finite values.
Results may differ from a plain program's by a relative error of at most 0.0027.
Values may be sent and summed in bfloat16 or wider, within the bound.
No kernel may reach another device: no remote copies, remote signals or barrier semaphores. Data moves between devices by JAX's collectives and lax.ppermute only.
A program may use at most 64 MiB of HBM per device.

v0:
```python
import math

import jax
import jax.numpy as jnp
from jax import lax
from jax.sharding import Mesh
from jax.sharding import PartitionSpec as P

A_DEV = 32
DP = ("dp_0", "dp_1", "dp_2", "dp_3")


INV_TEMP = 10.0
SHIFT = 10.0
EPS = 1e-06


def copy_for_each(value, axis):
    length = lax.axis_size(axis)
    return lax.all_to_all(
        jnp.broadcast_to(value[None], (length, *value.shape)), axis, 0, 0, tiled=True
    )


def of_everyone(value, axis):
    return copy_for_each(value, axis).sum(axis=0)


def in_order(parts, dim):
    parts = jnp.moveaxis(parts, 0, dim)
    lengths = parts.shape
    return parts.reshape(*lengths[:dim], lengths[dim] * lengths[dim + 1], *lengths[dim + 2 :])


def whole_of(value, axes, dim):
    far, near = axes
    first = copy_for_each(value, far)
    parts = jnp.swapaxes(copy_for_each(first, near), 0, 1)
    return in_order(parts.reshape(-1, *value.shape), dim)


def packed_total(arrays, axis):
    ends = [0]
    for a in arrays:
        ends.append(ends[-1] + a.size)
    subtotal = of_everyone(jnp.concatenate([a.ravel() for a in arrays]), axis)
    return tuple((subtotal[b:e].reshape(a.shape) for a, b, e in zip(arrays, ends, ends[1:])))


def cut_along(value, dim, length):
    before, after = (value.shape[:dim], value.shape[dim + 1 :])
    return jnp.moveaxis(value.reshape(*before, length, -1, *after), dim, 0)


def sum_at_owner(value, axis, dim):
    parts = cut_along(value, dim, lax.axis_size(axis))
    arrived = lax.all_to_all(parts, axis, split_axis=0, concat_axis=0, tiled=True)
    return arrived.sum(axis=0)


def sum_by_axis(value, axes, dim):
    far, near = axes
    parts = cut_along(value, dim, lax.axis_size(far))
    nearer = sum_at_owner(parts, near, dim + 1)
    arrived = lax.all_to_all(nearer, far, split_axis=0, concat_axis=0, tiled=True)
    return arrived.sum(axis=0)


def padded_to(lines, length):
    spare = -len(lines) % length
    return jnp.pad(lines, [(0, spare)] + [(0, 0)] * (lines.ndim - 1))


def total_of(value, axes):
    own = sum_by_axis(padded_to(value, lax.axis_size(axes[0]) * lax.axis_size(axes[1])), axes, 0)
    whole = whole_of(own, axes, 0)
    return whole[: len(value)].reshape(value.shape)


def in_one(arrays, axis):
    ravelled, at, finished = (jnp.concatenate([a.reshape(-1) for a in arrays]), 0, [])
    subtotal = total_of(ravelled, axis)
    for a in arrays:
        finished.append(subtotal[at : at + a.size].reshape(a.shape))
        at += a.size
    return tuple(finished)


def contract_rows(left, right):
    return lax.dot_general(
        left, right, (((0,), (0,)), ((), ())), preferred_element_type=jnp.float32
    )


def on_device(features, w_in, b_in, w_out, partner, window):
    rows = features.shape[0]
    parts = lax.axis_size("mp")
    part = lax.axis_index("mp")
    shards = lax.axis_size(DP)
    shard = lax.axis_index(DP)
    width = rows // parts
    anchor_rows = A_DEV
    anchor_all = anchor_rows * shards
    pre = jnp.dot(features, w_in, preferred_element_type=jnp.float32) + b_in
    hidden = jax.nn.silu(pre).astype(jnp.bfloat16)
    proj = of_everyone(jnp.dot(hidden, w_out, preferred_element_type=jnp.float32), "mp")
    norm = jnp.sqrt(jnp.sum(proj * proj, axis=1, keepdims=True) + EPS)
    emb = (proj / norm).astype(jnp.bfloat16)
    embed = emb.shape[1]
    own_cols = lax.dynamic_slice_in_dim(emb, part * width, width, 0)
    columns = whole_of(own_cols, (("dp_0", "dp_1", "dp_2"), "dp_3"), 0)
    col_total = columns.shape[0]
    shard_ids = jnp.arange(shards, dtype=jnp.int32)
    my_block = jnp.sum(jnp.where(shard_ids == shard, window, 0))
    my_start = my_block * anchor_rows
    anchors = lax.dynamic_slice_in_dim(emb, my_start, anchor_rows, 0)
    anchor_partner = lax.dynamic_slice_in_dim(partner, my_start, anchor_rows, 0)
    anchor_ids = shard * rows + my_start + jnp.arange(anchor_rows, dtype=jnp.int32)

    def column_ids(start, count):
        local = start + jnp.arange(count, dtype=jnp.int32)
        return local // width * rows + part * width + local % width

    blk = math.gcd(col_total, 2048)
    nblk = col_total // blk
    col_blocks = columns.reshape(nblk, blk, embed)
    starts = jnp.arange(nblk, dtype=jnp.int32) * blk

    def forward(carry, item):
        total, hit = carry
        block, start = item
        s = jnp.dot(anchors, block.T, preferred_element_type=jnp.float32) * INV_TEMP
        ids = column_ids(start, blk)
        ex = jnp.where(ids[None, :] == anchor_ids[:, None], 0.0, jnp.exp(s - SHIFT))
        hit = hit + jnp.sum(jnp.where(ids[None, :] == anchor_partner[:, None], s, 0.0), axis=1)
        return ((total + jnp.sum(ex, axis=1), hit), None)

    zero_rows = jnp.zeros((anchor_rows,), jnp.float32)
    (total, hit), _ = lax.scan(forward, (zero_rows, zero_rows), (col_blocks, starts))
    total, hit = packed_total((total, hit), "mp")
    row_loss = jnp.log(total) + SHIFT - hit

    def row_weights(s, ids):
        prob = jnp.where(
            ids[None, :] == anchor_ids[:, None], 0.0, jnp.exp(s - SHIFT) / total[:, None]
        )
        onehot = (ids[None, :] == anchor_partner[:, None]).astype(jnp.float32)
        return (prob - onehot).astype(jnp.bfloat16)

    def backward(acc, item):
        block, start = item
        s = jnp.dot(anchors, block.T, preferred_element_type=jnp.float32) * INV_TEMP
        weights = row_weights(s, column_ids(start, blk))
        return (acc + jnp.dot(weights, block, preferred_element_type=jnp.float32), None)

    row_part, _ = lax.scan(
        backward, jnp.zeros((anchor_rows, embed), jnp.float32), (col_blocks, starts)
    )
    totals = whole_of(total, (("dp_0", "dp_1", "dp_2"), "dp_3"), 0)
    own_ids = shard * rows + part * width + jnp.arange(width, dtype=jnp.int32)
    own_partner = lax.dynamic_slice_in_dim(partner, part * width, width, 0)
    piece = whole_of(anchors, (("dp_0", "dp_1", "dp_2"), "dp_3"), 0)
    count = piece.shape[0]
    inner = math.gcd(count, 2048)
    sub_pieces = piece.reshape(count // inner, inner, embed)
    offsets = jnp.arange(count // inner, dtype=jnp.int32) * inner

    def one_block(inner_acc, item):
        block, offset = item
        block_totals = lax.dynamic_slice_in_dim(totals, offset, inner, 0)
        flat = offset + jnp.arange(inner, dtype=jnp.int32)
        owner = flat // anchor_rows
        owner_block = jnp.sum(
            jnp.where(owner[:, None] == shard_ids[None, :], window[None, :], 0), axis=1
        )
        ids = owner * rows + owner_block * anchor_rows + flat % anchor_rows
        s = jnp.dot(own_cols, block.T, preferred_element_type=jnp.float32) * INV_TEMP
        prob = jnp.where(
            ids[None, :] == own_ids[:, None], 0.0, jnp.exp(s - SHIFT) / block_totals[None, :]
        )
        onehot = (ids[None, :] == own_partner[:, None]).astype(jnp.float32)
        weights = (prob - onehot).astype(jnp.bfloat16)
        return (inner_acc + jnp.dot(weights, block, preferred_element_type=jnp.float32), None)

    result, _ = lax.scan(one_block, jnp.zeros((width, embed), jnp.float32), (sub_pieces, offsets))
    placed = lax.dynamic_update_slice_in_dim(
        jnp.zeros((rows, embed), jnp.float32), result, part * width, 0
    )
    row_placed = lax.dynamic_update_slice_in_dim(
        jnp.zeros((rows, embed), jnp.float32), row_part, my_start, 0
    )
    grad_emb = of_everyone(row_placed + placed, "mp") * (INV_TEMP / anchor_all)
    unit = proj / norm
    grad_proj = ((grad_emb - unit * jnp.sum(unit * grad_emb, axis=1, keepdims=True)) / norm).astype(
        jnp.bfloat16
    )
    grad_w_out = contract_rows(hidden, grad_proj)
    grad_hidden = lax.dot_general(
        grad_proj, w_out, (((1,), (1,)), ((), ())), preferred_element_type=jnp.float32
    )
    sig = jax.nn.sigmoid(pre)
    grad_pre = (grad_hidden * sig * (1.0 + pre * (1.0 - sig))).astype(jnp.bfloat16)
    grad_w_in = contract_rows(features, grad_pre)
    grad_b_in = jnp.sum(grad_pre.astype(jnp.float32), axis=0)
    grad_w_in, grad_b_in, grad_w_out = in_one(
        (grad_w_in, grad_b_in, grad_w_out), (("dp_0", "dp_1", "dp_2"), "dp_3")
    )
    return (row_loss, grad_w_in, grad_b_in, grad_w_out)


def solution(mesh):
    finer = Mesh(
        mesh.devices.reshape(8, 4, 2, 2, mesh.shape["mp"]), ("dp_0", "dp_1", "dp_2", "dp_3", "mp")
    )
    placed = (P(DP, None), P(None, "mp"), P("mp"), P("mp", None), P(DP), P())
    return jax.shard_map(
        on_device,
        mesh=finer,
        in_specs=placed,
        out_specs=(P(DP), P(None, "mp"), P("mp"), P("mp", None)),
        check_vma=False,
    )
```

profile of v0, /device:TPU:1, one launch (start us, length us, event | category | flops | bytes accessed | tf_op | source)
XLA Modules:
  0.0 235.6 jit_solution(1263698015841084937)
XLA Ops:
  1.6 1.8 multiply_convert_fusion
  5.6 3.4 %all-to-all-start = ((f32[2,128,128]{2,1,0:T(8,128)}), f32[2,128,128]{2,1,0:T(8,128)S(1)}, u32[]{:S(2)}, u32[]{:S(2)}) async-start(f32[2,128,128]{2,1,0:T(8,128)} %broadcast_in_dim.95), calls=%async_computation | async-start | bytes 262144 | tf_op jit(solution)/shard_map/all_to_all | solution.py:20
  11.0 2.0 all-to-all-done
  14.1 14.6 %all-to-all-start.4 = ((bf16[64,32,128]{2,1,0:T(8,128)(2,1)}), bf16[64,32,128]{2,1,0:T(8,128)(2,1)S(1)}, u32[]{:S(2)}, u32[]{:S(2)}) async-start(bf16[64,32,128]{2,1,0:T(8,128)(2,1)} %broadcast_in_dim.151), calls=%async_computation.4 | async-start | bytes 1048576 | tf_op jit(solution)/shard_map/all_to_all | solution.py:20
  28.7 15.7 %all-to-all-done.4 = bf16[64,32,128]{2,1,0:T(8,128)(2,1)S(1)} async-done(((bf16[64,32,128]{2,1,0:T(8,128)(2,1)}), bf16[64,32,128]{2,1,0:T(8,128)(2,1)S(1)}, u32[]{:S(2)}, u32[]{:S(2)}) %all-to-all-start.4) | async-done | bytes 524320 | tf_op jit(solution)/shard_map/all_to_all | solution.py:20
  45.7 7.8 %all-to-all-start.1 = ((bf16[64,64,128]{2,1,0:T(8,128)(2,1)}), bf16[64,64,128]{2,1,0:T(8,128)(2,1)S(1)}, u32[]{:S(2)}, u32[]{:S(2)}) async-start(bf16[64,64,128]{2,1,0:T(8,128)(2,1)} %broadcast_in_dim.96), calls=%async_computation.1 | async-start | bytes 2097152 | tf_op jit(solution)/shard_map/all_to_all | solution.py:20
  55.2 24.6 %all-to-all-done.1 = bf16[64,64,128]{2,1,0:T(8,128)(2,1)S(1)} async-done(((bf16[64,64,128]{2,1,0:T(8,128)(2,1)}), bf16[64,64,128]{2,1,0:T(8,128)(2,1)S(1)}, u32[]{:S(2)}, u32[]{:S(2)}) %all-to-all-start.1) | async-done | bytes 1048608 | tf_op jit(solution)/shard_map/all_to_all | solution.py:20
  80.4 10.1 %all_to_all.72 = bf16[2,64,64,128]{3,2,1,0:T(8,128)(2,1)S(1)} all-to-all(bf16[2,64,64,128]{3,2,1,0:T(8,128)(2,1)S(1)} %broadcast_in_dim.97), channel_id=1, replica_groups=mesh['dp_0'=8,'dp_1'=4,'dp_2'=2,'dp_3'=2,'mp'=2] {'dp_3'}, dimensions={0} | all-to-all | bytes 4194304 | tf_op jit(solution)/shard_map/all_to_all | solution.py:20
  91.6 3.9 %all-to-all-start.5 = ((bf16[2,64,32,128]{3,2,1,0:T(8,128)(2,1)}), bf16[2,64,32,128]{3,2,1,0:T(8,128)(2,1)S(1)}, u32[]{:S(2)}, u32[]{:S(2)}) async-start(bf16[2,64,32,128]{3,2,1,0:T(8,128)(2,1)} %broadcast_in_dim.152), calls=%async_computation.5 | async-start | bytes 2097152 | tf_op jit(solution)/shard_map/all_to_all | solution.py:20
  95.5 1.5 copy.32
  97.1 13.7 %while.41 = (s32[]{:T(128)}, f32[32]{0:T(128)S(1)}, f32[32]{0:T(128)S(1)}, s32[4]{0:T(128)}, s32[]{:T(128)}, /*index=5*/bf16[4,2048,128]{2,1,0:T(8,128)(2,1)}, b...) while((s32[]{:T(128)}, f32[32]{0:T(128)S(1)}, ...), condition=%wide.region_6.7_spmd.clone, body=%wide.region_3.6_spmd.clone.sunk | while | flops 17348704 | bytes 550927 | solution.py:139
  102.4 1.5 select_reduce_fusion.5
  111.4 3.2 %all-to-all-start.3 = ((f32[2,1,64]{2,1,0:T(1,128)}), f32[2,1,64]{2,1,0:T(1,128)S(1)}, u32[]{:S(2)}, u32[]{:S(2)}) async-start(f32[2,1,64]{2,1,0:T(1,128)} %broadcast_in_dim.98), calls=%async_computation.3 | async-start | bytes 2048 | tf_op jit(solution)/shard_map/all_to_all | solution.py:20
  118.4 5.6 %all-to-all-start.6 = ((f32[64,1,32]{2,1,0:T(1,128)}), f32[64,1,32]{2,1,0:T(1,128)S(1)}, u32[]{:S(2)}, u32[]{:S(2)}) async-start(f32[64,1,32]{2,1,0:T(1,128)} %broadcast_in_dim.153), calls=%async_computation.6 | async-start | bytes 65536 | tf_op jit(solution)/shard_map/all_to_all | solution.py:20
  124.0 15.4 %while.42 = (s32[]{:T(128)}, f32[32,128]{1,0:T(8,128)S(1)}, s32[4]{0:T(128)}, s32[]{:T(128)}, bf16[4,2048,128]{2,1,0:T(8,128)(2,1)S(1)}, /*index=5*/bf16[32,128]...) while((s32[]{:T(128)}, f32[32,128]{1,0:T(8,128)S(1)}, ...), condition=%wide.region_9.10_spmd.clone, body=%wide.region_8.9_spmd.clone.sunk | while | flops 34199584 | bytes 1108751 | solution.py:156
  139.6 4.8 %all_to_all.73 = f32[2,1,2048]{2,1,0:T(1,128)S(1)} all-to-all(f32[2,1,2048]{2,1,0:T(1,128)S(1)} %reshape.182), channel_id=1, replica_groups=mesh['dp_0'=8,'dp_1'=4,'dp_2'=2,'dp_3'=2,'mp'=2] {'dp_3'}, dimensions={0} | all-to-all | bytes 32768 | tf_op jit(solution)/shard_map/all_to_all | solution.py:20
  146.0 15.4 %while.43 = (s32[]{:T(128)}, f32[64,128]{1,0:T(8,128)}, s32[2]{0:T(128)}, s32[128]{0:T(128)}, bf16[2,2048,128]{2,1,0:T(8,128)(2,1)S(1)}, /*index=5*/bf16[64,128]...) while((s32[]{:T(128)}, f32[64,128]{1,0:T(8,128)}, ...), condition=%wide.region_12.13_spmd.clone, body=%wide.region_10.12_spmd.clone.sunk | while | flops 69171272 | bytes 1206973 | solution.py:185
  151.9 1.7 fusion.134
  159.5 1.9 fusion.134
  162.2 5.7 %all_to_all.74 = f32[2,128,128]{2,1,0:T(8,128)S(1)} all-to-all(f32[2,128,128]{2,1,0:T(8,128)S(1)} %broadcast_in_dim.156), channel_id=1, replica_groups=mesh['dp_0'=8,'dp_1'=4,'dp_2'=2,'dp_3'=2,'mp'=2] {'mp'}, dimensions={0} | all-to-all | bytes 262144 | tf_op jit(solution)/shard_map/all_to_all | solution.py:20
  170.3 5.4 %all_to_all.75 = f32[2,64,1282]{2,1,0:T(8,128)S(1)} all-to-all(f32[2,64,1282]{2,1,0:T(8,128)S(1)} %copy.38), channel_id=1, replica_groups=mesh['dp_0'=8,'dp_1'=4,'dp_2'=2,'dp_3'=2,'mp'=2] {'dp_3'}, dimensions={0} | all-to-all | bytes 1312768 | tf_op jit(solution)/shard_map/all_to_all | solution.py:57
  176.1 26.3 %all_to_all.76 = f32[64,1,1282]{2,1,0:T(1,128)S(1)} all-to-all(f32[64,1,1282]{2,1,0:T(1,128)S(1)} %all_to_all.55), channel_id=1, replica_groups=mesh['dp_0'=8,'dp_1'=4,'dp_2'=2,'dp_3'=2,'mp'=2] {'dp_0','dp_1','dp_2'}, dimensions={0} | all-to-all | bytes 656384 | tf_op jit(solution)/shard_map/all_to_all | solution.py:65
  202.8 19.9 %all_to_all.77 = f32[64,1,1282]{2,1,0:T(1,128)S(1)} all-to-all(f32[64,1,1282]{2,1,0:T(1,128)S(1)} %broadcast_in_dim.157), channel_id=1, replica_groups=mesh['dp_0'=8,'dp_1'=4,'dp_2'=2,'dp_3'=2,'mp'=2] {'dp_0','dp_1','dp_2'}, dimensions={0} | all-to-all | bytes 656384 | tf_op jit(solution)/shard_map/all_to_all | solution.py:20
  222.7 7.9 %all_to_all.78 = f32[2,64,1282]{2,1,0:T(8,128)S(1)} all-to-all(f32[2,64,1282]{2,1,0:T(8,128)S(1)} %broadcast_in_dim.159), channel_id=1, replica_groups=mesh['dp_0'=8,'dp_1'=4,'dp_2'=2,'dp_3'=2,'mp'=2] {'dp_3'}, dimensions={0} | all-to-all | bytes 1312768 | tf_op jit(solution)/shard_map/all_to_all | solution.py:20
  (143 shorter events, 60.4 us)
Async XLA Ops:
  0.6 1.0 copy-start
  3.3 0.6 copy-start.7
  5.6 7.3 %all-to-all-start = ((f32[2,128,128]{2,1,0:T(8,128)}), f32[2,128,128]{2,1,0:T(8,128)S(1)}, u32[]{:S(2)}, u32[]{:S(2)}) async-start(f32[2,128,128]{2,1,0:T(8,128)} %broadcast_in_dim.95), calls=%async_computation | async-start | bytes 262144 | tf_op jit(solution)/shard_map/all_to_all | solution.py:20
  13.1 15.6 %copy-start.9 = (f32[128]{0:T(128)}, f32[128]{0:T(128)S(1)}, u32[]{:S(2)}) copy-start(f32[128]{0:T(128)S(1)} %add_sqrt_fusion) | copy-start | bytes 1540
  14.1 39.3 %copy-start.12 = (s32[128]{0:T(128)S(1)}, s32[128]{0:T(128)}, u32[]{:S(2)}) copy-start(s32[128]{0:T(128)} %param.16) | copy-start | bytes 1540
  14.1 30.3 %all-to-all-start.4 = ((bf16[64,32,128]{2,1,0:T(8,128)(2,1)}), bf16[64,32,128]{2,1,0:T(8,128)(2,1)S(1)}, u32[]{:S(2)}, u32[]{:S(2)}) async-start(bf16[64,32,128]{2,1,0:T(8,128)(2,1)} %broadcast_in_dim.151), calls=%async_computation.4 | async-start | bytes 1048576 | tf_op jit(solution)/shard_map/all_to_all | solution.py:20
  44.4 1.2 copy-start.1
  45.7 34.2 %all-to-all-start.1 = ((bf16[64,64,128]{2,1,0:T(8,128)(2,1)}), bf16[64,64,128]{2,1,0:T(8,128)(2,1)S(1)}, u32[]{:S(2)}, u32[]{:S(2)}) async-start(bf16[64,64,128]{2,1,0:T(8,128)(2,1)} %broadcast_in_dim.96), calls=%async_computation.1 | async-start | bytes 2097152 | tf_op jit(solution)/shard_map/all_to_all | solution.py:20
  80.4 10.1 %copy-start.2 = (bf16[64,32,128]{2,1,0:T(8,128)(2,1)S(1)}, bf16[64,32,128]{2,1,0:T(8,128)(2,1)}, u32[]{:S(2)}) copy-start(bf16[64,32,128]{2,1,0:T(8,128)(2,1)} %copy-done.1) | copy-start | bytes 1572868
  91.6 19.2 %all-to-all-start.5 = ((bf16[2,64,32,128]{3,2,1,0:T(8,128)(2,1)}), bf16[2,64,32,128]{3,2,1,0:T(8,128)(2,1)S(1)}, u32[]{:S(2)}, u32[]{:S(2)}) async-start(bf16[2,64,32,128]{3,2,1,0:T(8,128)(2,1)} %broadcast_in_dim.152), calls=%async_computation.5 | async-start | bytes 2097152 | tf_op jit(solution)/shard_map/all_to_all | solution.py:20
  110.7 3.9 %copy-start.13 = (s32[32]{0:T(128)}, s32[32]{0:T(128)S(1)}, u32[]{:S(2)}) copy-start(s32[32]{0:T(128)S(1)} %get-tuple-element.826) | copy-start | bytes 388
  110.7 13.2 %copy-start.3 = (bf16[4,2048,128]{2,1,0:T(8,128)(2,1)S(1)}, bf16[4,2048,128]{2,1,0:T(8,128)(2,1)}, u32[]{:S(2)}) copy-start(bf16[4,2048,128]{2,1,0:T(8,128)(2,1)} %get-tuple-element.821) | copy-start | bytes 6291460
  111.4 5.7 %all-to-all-start.3 = ((f32[2,1,64]{2,1,0:T(1,128)}), f32[2,1,64]{2,1,0:T(1,128)S(1)}, u32[]{:S(2)}, u32[]{:S(2)}) async-start(f32[2,1,64]{2,1,0:T(1,128)} %broadcast_in_dim.98), calls=%async_computation.3 | async-start | bytes 2048 | tf_op jit(solution)/shard_map/all_to_all | solution.py:20
  117.7 6.2 %copy-start.11 = (f32[32]{0:T(128)}, f32[32]{0:T(128)S(1)}, u32[]{:S(2)}) copy-start(f32[32]{0:T(128)S(1)} %get-tuple-element.753) | copy-start | bytes 388
  118.4 21.0 %all-to-all-start.6 = ((f32[64,1,32]{2,1,0:T(1,128)}), f32[64,1,32]{2,1,0:T(1,128)S(1)}, u32[]{:S(2)}, u32[]{:S(2)}) async-start(f32[64,1,32]{2,1,0:T(1,128)} %broadcast_in_dim.153), calls=%async_computation.6 | async-start | bytes 65536 | tf_op jit(solution)/shard_map/all_to_all | solution.py:20
  124.0 21.9 %copy-start.4 = (bf16[2,64,32,128]{3,2,0,1:T(8,128)(2,1)S(1)}, bf16[2,64,32,128]{3,2,0,1:T(8,128)(2,1)}, u32[]{:S(2)}) copy-start(bf16[2,64,32,128]{3,2,0,1:T(8,128)(2,1)} %copy.34) | copy-start | bytes 3145732
  145.9 22.0 %copy-start.10 = (f32[128]{0:T(128)S(1)}, f32[128]{0:T(128)}, u32[]{:S(2)}) copy-start(f32[128]{0:T(128)} %copy-done.9) | copy-start | bytes 1540
  145.9 22.2 %copy-start.8 = (bf16[128,256]{1,0:T(8,128)(2,1)S(1)}, bf16[128,256]{1,0:T(8,128)(2,1)}, u32[]{:S(2)}) copy-start(bf16[128,256]{1,0:T(8,128)(2,1)} %copy-done.7) | copy-start | bytes 196612
  145.9 22.4 %copy-start.6 = (bf16[256,128]{1,0:T(8,128)(2,1)S(1)}, bf16[256,128]{1,0:T(8,128)(2,1)}, u32[]{:S(2)}) copy-start(bf16[256,128]{1,0:T(8,128)(2,1)} %param.15) | copy-start | bytes 196612
  145.9 22.4 %copy-start.14 = (f32[128,256]{1,0:T(8,128)S(1)}, f32[128,256]{1,0:T(8,128)}, u32[]{:S(2)}) copy-start(f32[128,256]{1,0:T(8,128)} %get-tuple-element.538) | copy-start | bytes 393220
  161.4 7.2 %copy-start.5 = (bf16[128,512]{1,0:T(8,128)(2,1)S(1)}, bf16[128,512]{1,0:T(8,128)(2,1)}, u32[]{:S(2)}) copy-start(bf16[128,512]{1,0:T(8,128)(2,1)} %param.12) | copy-start | bytes 393220
where the time goes:
time: 237 us; the launch traced here: 236 us
  blocking collectives  80.1 us (34%)
  waiting for transfers between devices  43.7 us (18%)
  starting transfers between devices  38.4 us (16%)
  local copies, waits for them, and re-layouts  31.4 us (13%)
  other arithmetic  18.4 us (8%)
  matrix products  17.5 us (7%)
  loops' own time  4.25 us (2%)
    all_to_all x5, blocking collectives, copy_for_each(): lax.all_to_all(jnp.broadcast_to(value[None], (length, *value.shape)), axi...  48.4 us
    all_to_all x6, waiting for transfers between devices, copy_for_each(): lax.all_to_all(jnp.broadcast_to(value[None], (length, *value.shape)), axi...  43.7 us
    all_to_all x6, starting transfers between devices, copy_for_each(): lax.all_to_all(jnp.broadcast_to(value[None], (length, *value.shape)), axi...  38.4 us
    all_to_all x1, blocking collectives, sum_by_axis(): lax.all_to_all(nearer, far, split_axis=0, concat_axis=0, tiled=True)  26.3 us
    dynamic_slice x8, local copies, waits for them, and re-layouts, on_device(): lax.scan(forward, (zero_rows, zero_rows), (col_blocks, starts))  10.4 us
    broadcast_in_dim x11, local copies, waits for them, and re-layouts, copy_for_each(): jnp.broadcast_to(value[None], (length, *value.shape))  5.9 us
    dot_general x4, matrix products, forward(): s = jnp.dot(anchors, block.T, preferred_element_type=jnp.float32) * INV_TEMP  5.81 us
    add x8, other arithmetic, column_ids(): return local // width * rows + part * width + local % width  5.45 us
  transfers between devices with their start and end apart: 6, of which 4 were waited for; matrix products, arithmetic and copies ran while one was open for 15% of the time, Pallas kernels for 0%

commit v1 on v0

v1 whole, which is shorter than its diff:
```python
import functools

import jax
import jax.numpy as jnp
from jax import lax
from jax.experimental import pallas as pl
from jax.experimental.pallas import tpu as pltpu
from jax.sharding import Mesh
from jax.sharding import PartitionSpec as P

SIZES = {"z": 8, "x": 4, "yh": 2, "c": 2}
DP = ("z", "x", "yh", "c")
FAR = ("z", "x")
QUAD = ("yh", "c")

ROWS = 128
A_DEV = 32
HALF = 16
EMB = 128
N_FAR = 32
N_QUAD = 4
ANCHORS = N_FAR * HALF
MSG = 24
PART = 88
N_NEAR = 8

INV_TEMP = 10.0
SHIFT = 10.0
EPS = 1e-06
BF16 = jnp.bfloat16
F32 = jnp.float32
I32 = jnp.int32


def call(kernel, outs, *args, smem=(), scratch=()):
    specs = [
        pl.BlockSpec(memory_space=pltpu.SMEM if i in smem else pltpu.VMEM)
        for i in range(len(args))
    ]
    return pl.pallas_call(
        kernel,
        out_shape=[jax.ShapeDtypeStruct(s, d) for s, d in outs],
        in_specs=specs,
        out_specs=[pl.BlockSpec(memory_space=pltpu.VMEM)] * len(outs),
        scratch_shapes=list(scratch),
    )(*args)


def dot(a, b, dims):
    return lax.dot_general(a, b, (dims, ((), ())), preferred_element_type=F32)


def forward(x_ref, w_in_ref, b_ref, w_out_ref, part_ref, pre_ref, hid_ref):
    pre = dot(x_ref[...], w_in_ref[...], ((1,), (0,))) + b_ref[...]
    hidden = (pre * jax.nn.sigmoid(pre)).astype(BF16)
    pre_ref[...] = pre
    hid_ref[...] = hidden
    part_ref[...] = dot(hidden, w_out_ref[...], ((1,), (0,)))


def norm_of(proj):
    return jnp.sqrt(jnp.sum(proj * proj, axis=1, keepdims=True) + EPS)


def embed(at_ref, window_ref, part_ref, other_ref, partner_ref, emb_ref, msg_ref, hold_ref):
    g, q, mp = at_ref[0], at_ref[1], at_ref[2]
    proj = part_ref[...] + other_ref[...]
    emb = (proj / norm_of(proj)).astype(BF16)
    emb_ref[...] = emb
    hold_ref[...] = emb.astype(F32)
    start = pl.multiple_of(window_ref[g * N_QUAD + q] * A_DEV + mp * HALF, HALF)
    chosen = hold_ref[pl.ds(start, HALF), :]
    to = (g % 8) * HALF
    lane = lax.broadcasted_iota(I32, (8, ROWS), 1)
    row = lax.broadcasted_iota(I32, (8, ROWS), 0)
    partner = jnp.broadcast_to(partner_ref[...], (8, ROWS))
    value = jnp.where(
        row == 0, partner // ROWS, jnp.where(row == 1, partner % ROWS, lane)
    ).astype(F32)
    value = pltpu.roll(value, (to - start + ROWS) % ROWS, axis=1)
    value = jnp.where((lane >= to) & (lane < to + HALF) & (row < 3), value, 0.0)
    message = jnp.concatenate([chosen, value], axis=0).astype(BF16)
    for i in range(N_FAR):
        msg_ref[i] = message


def block_ids(at_ref, msg_ref):
    g, q = at_ref[0], at_ref[1]
    ids = msg_ref[:, HALF:, :].astype(F32)
    ids = ids.reshape(N_FAR // 8, 8, 8, ROWS).sum(axis=1)
    ids = jnp.concatenate([ids[i] for i in range(N_FAR // 8)], axis=1)
    lane = lax.broadcasted_iota(I32, (1, ANCHORS), 1)
    partner = (ids[0:1] * float(ROWS) + ids[1:2]).astype(I32)
    own = (lane // HALF * N_QUAD + q) * ROWS + ids[2:3].astype(I32)
    return partner, own


def column_ids(at_ref, r):
    g, q = at_ref[0], at_ref[1]
    base = (g * N_QUAD + (q ^ r)) * ROWS
    return base + lax.broadcasted_iota(I32, (ROWS, 1), 0)


def anchors_of(msg_ref):
    return jnp.concatenate([msg_ref[i, :HALF, :] for i in range(N_FAR)], axis=0)


def totals(at_ref, msg_ref, e0_ref, e1_ref, e2_ref, e3_ref, out_ref):
    anchors = anchors_of(msg_ref)
    partner, own = block_ids(at_ref, msg_ref)
    total = jnp.zeros((1, ANCHORS), F32)
    hit = jnp.zeros((1, ANCHORS), F32)
    for r, e_ref in enumerate((e0_ref, e1_ref, e2_ref, e3_ref)):
        s = dot(e_ref[...], anchors, ((1,), (1,))) * INV_TEMP
        cols = column_ids(at_ref, r)
        ex = jnp.where(cols == own, 0.0, jnp.exp(s - SHIFT))
        total = total + jnp.sum(ex, axis=0, keepdims=True)
        hit = hit + jnp.sum(jnp.where(cols == partner, s, 0.0), axis=0, keepdims=True)
    lines = [total[:, i * ROWS : (i + 1) * ROWS] for i in range(4)]
    lines += [hit[:, i * ROWS : (i + 1) * ROWS] for i in range(4)]
    message = jnp.concatenate(lines, axis=0)
    for i in range(N_FAR):
        out_ref[i] = message


def weights(
    at_ref,
    msg_ref,
    sums_ref,
    e0_ref,
    e1_ref,
    e2_ref,
    e3_ref,
    row_ref,
    c0_ref,
    c1_ref,
    c2_ref,
    c3_ref,
    loss_ref,
):
    anchors = anchors_of(msg_ref)
    partner, own = block_ids(at_ref, msg_ref)
    sums = jnp.sum(sums_ref[...], axis=0)
    total, hit = sums[:4], sums[4:]
    loss_ref[...] = jnp.concatenate([jnp.log(total) + SHIFT - hit, hit], axis=0)
    total = jnp.concatenate([total[i : i + 1] for i in range(4)], axis=1)
    rows = jnp.zeros((ANCHORS, EMB), F32)
    for r, (e_ref, c_ref) in enumerate(
        ((e0_ref, c0_ref), (e1_ref, c1_ref), (e2_ref, c2_ref), (e3_ref, c3_ref))
    ):
        cols_emb = e_ref[...]
        s = dot(cols_emb, anchors, ((1,), (1,))) * INV_TEMP
        cols = column_ids(at_ref, r)
        prob = jnp.where(cols == own, 0.0, jnp.exp(s - SHIFT) / total)
        w = (prob - (cols == partner).astype(F32)).astype(BF16)
        c_ref[...] = dot(w, anchors, ((1,), (0,)))
        rows = rows + dot(w, cols_emb, ((0,), (0,)))
    for i in range(N_FAR):
        row_ref[i] = rows[i * HALF : (i + 1) * HALF]


def gather_rows(
    at_ref, window_ref, rows_ref, c0_ref, r1_ref, r2_ref, r3_ref, loss_ref, out_ref
):
    g, q, mp = at_ref[0], at_ref[1], at_ref[2]
    out_ref[0:ROWS, :] = (c0_ref[...] + r1_ref[...]) + (r2_ref[...] + r3_ref[...])
    start = pl.multiple_of(window_ref[g * N_QUAD + q] * A_DEV + mp * HALF, HALF)
    mine = jnp.sum(rows_ref[...], axis=0)
    out_ref[pl.ds(start, HALF), :] = out_ref[pl.ds(start, HALF), :] + mine
    row = lax.broadcasted_iota(I32, (8, ROWS), 0)
    line = jnp.sum(jnp.where(row == g // 8, loss_ref[...], 0.0), axis=0, keepdims=True)
    line = jnp.broadcast_to(line, (8, ROWS))
    line = pltpu.roll(line, (mp * HALF - (g % 8) * HALF + ROWS) % ROWS, axis=1)
    lane = lax.broadcasted_iota(I32, (8, ROWS), 1)
    out_ref[ROWS:, :] = jnp.where((lane >= mp * HALF) & (lane < mp * HALF + HALF), line, 0.0)


def backward(
    at_ref,
    mine_ref,
    theirs_ref,
    part_ref,
    other_ref,
    pre_ref,
    hid_ref,
    x_ref,
    w_out_ref,
    loss_ref,
    keep_ref,
    send_ref,
    all_ref,
):
    scale = INV_TEMP / (N_FAR * N_QUAD * A_DEV)
    grad_emb = (mine_ref[0:ROWS, :] + theirs_ref[0:ROWS, :]) * scale
    loss_ref[...] = mine_ref[ROWS : ROWS + 1, 0:A_DEV] + theirs_ref[ROWS : ROWS + 1, 0:A_DEV]
    proj = part_ref[...] + other_ref[...]
    norm = norm_of(proj)
    unit = proj / norm
    inner = jnp.sum(unit * grad_emb, axis=1, keepdims=True)
    grad_proj = ((grad_emb - unit * inner) / norm).astype(BF16)
    all_ref[1024:1280, :] = dot(hid_ref[...], grad_proj, ((0,), (0,)))
    grad_hidden = dot(grad_proj, w_out_ref[...], ((1,), (1,)))
    pre = pre_ref[...]
    sig = jax.nn.sigmoid(pre)
    grad_pre = (grad_hidden * sig * (1.0 + pre * (1.0 - sig))).astype(BF16)
    grad_in = dot(x_ref[...], grad_pre, ((0,), (0,)))
    all_ref[0:512, :] = grad_in[:, :128]
    all_ref[512:1024, :] = grad_in[:, 128:]
    bias = jnp.sum(grad_pre.astype(F32), axis=0, keepdims=True)
    bias = jnp.concatenate([bias[:, :128], bias[:, 128:], jnp.zeros((6, 128), F32)], axis=0)
    c = at_ref[1] % 2
    for side, out_ref in ((c, keep_ref), (1 - c, send_ref)):
        base = pl.multiple_of(side * 640, 128)
        for i in range(N_NEAR):
            out_ref[i, 0:80, :] = all_ref[pl.ds(base + i * 80, 80), :]
            out_ref[i, 80:, :] = bias if i == 0 else jnp.zeros((8, 128), F32)


def add(a_ref, b_ref, out_ref):
    out_ref[...] = a_ref[...] + b_ref[...]


def sum_spread(in_ref, out_ref):
    total = jnp.sum(in_ref[...], axis=0)
    for i in range(N_NEAR):
        out_ref[i] = total


def unpack(at_ref, mine_ref, theirs_ref, w_in_ref, b_ref, w_out_ref, all_ref):
    c = at_ref[1] % 2
    for side, in_ref in ((c, mine_ref), (1 - c, theirs_ref)):
        base = pl.multiple_of(side * 640, 128)
        for i in range(N_NEAR):
            all_ref[pl.ds(base + i * 80, 80), :] = in_ref[i, 0:80, :]
    w_in_ref[:, :128] = all_ref[0:512, :]
    w_in_ref[:, 128:] = all_ref[512:1024, :]
    w_out_ref[...] = all_ref[1024:1280, :]
    b_ref[...] = mine_ref[0, 80:82, :]


def swap(value, axes, flip):
    axes = axes if isinstance(axes, tuple) else (axes,)
    count = lax.axis_size(axes)
    return lax.ppermute(value, axes, [(i, i ^ flip) for i in range(count)])


def exchange(value, axes):
    return lax.all_to_all(value, axes, 0, 0, tiled=True)


def on_device(features, w_in, b_in, w_out, partner, window):
    at = jnp.stack([lax.axis_index(FAR), lax.axis_index(QUAD), lax.axis_index("mp")]).astype(I32)
    part, pre, hidden = call(
        forward,
        [((ROWS, EMB), F32), ((ROWS, 256), F32), ((ROWS, 256), BF16)],
        features,
        w_in,
        b_in.reshape(1, -1),
        w_out,
    )
    other = swap(part, "mp", 1)
    emb, message = call(
        embed,
        [((ROWS, EMB), BF16), ((N_FAR, MSG, EMB), BF16)],
        at,
        window,
        part,
        other,
        partner.reshape(1, -1),
        smem=(0, 1),
        scratch=[pltpu.VMEM((ROWS, EMB), F32)],
    )
    anchors = exchange(message, FAR)
    blocks = [emb] + [swap(emb, QUAD, r) for r in (1, 2, 3)]
    (sums,) = call(totals, [((N_FAR, 8, ROWS), F32)], at, anchors, *blocks, smem=(0,))
    sums = exchange(sums, FAR)
    rows, c0, c1, c2, c3, losses = call(
        weights,
        [((N_FAR, HALF, EMB), F32)] + [((ROWS, EMB), F32)] * 4 + [((8, ROWS), F32)],
        at,
        anchors,
        sums,
        *blocks,
        smem=(0,),
    )
    rows = exchange(rows, FAR)
    r1, r2, r3 = [swap(c, QUAD, r) for r, c in ((1, c1), (2, c2), (3, c3))]
    (mine,) = call(
        gather_rows,
        [((ROWS + 8, EMB), F32)],
        at,
        window,
        rows,
        c0,
        r1,
        r2,
        r3,
        losses,
        smem=(0, 1),
    )
    theirs = swap(mine, "mp", 1)
    half = (N_NEAR, PART, EMB)
    row_loss, keep, send = call(
        backward,
        [((1, A_DEV), F32), (half, F32), (half, F32)],
        at,
        mine,
        theirs,
        part,
        other,
        pre,
        hidden,
        features,
        w_out,
        smem=(0,),
        scratch=[pltpu.VMEM((1280, EMB), F32)],
    )
    got = swap(send, "c", 1)
    (both,) = call(add, [(half, F32)], keep, got)
    (both,) = call(sum_spread, [(half, F32)], exchange(both, ("x", "yh")))
    (both,) = call(sum_spread, [(half, F32)], exchange(both, "z"))
    both = exchange(both, ("x", "yh"))
    got = swap(both, "c", 1)
    grad_in, grad_b, grad_out = call(
        unpack,
        [((512, 256), F32), ((2, 128), F32), ((256, EMB), F32)],
        at,
        both,
        got,
        smem=(0,),
        scratch=[pltpu.VMEM((1280, EMB), F32)],
    )
    return (row_loss.reshape(-1), grad_in, grad_b.reshape(-1), grad_out)


def solution(mesh):
    finer = Mesh(mesh.devices.reshape(*SIZES.values(), mesh.shape["mp"]), (*SIZES, "mp"))
    placed = (P(DP, None), P(None, "mp"), P("mp"), P("mp", None), P(DP), P())
    return jax.shard_map(
        on_device,
        mesh=finer,
        in_specs=placed,
        out_specs=(P(DP), P(None, "mp"), P("mp"), P("mp", None)),
        check_vma=False,
    )
```

time: 237 us -> 142 us (0.60)
  local copies, waits for them, and re-layouts: 31.4 us -> 4.46 us
  waiting for transfers between devices: 43.7 us -> 19.4 us
  Pallas kernels: 0 us -> 20.4 us
  blocking collectives: 80.1 us -> 60.9 us
  other arithmetic: 18.4 us -> 0.58 us
  matrix products: 17.5 us -> 0 us
  loops' own time: 4.25 us -> 0 us
  starting transfers between devices: 38.4 us -> 34.2 us
    all_to_all x6 -> x2, waiting for transfers between devices: 43.7 us -> 4.52 us  [exchange(): return lax.all_to_all(value, axes, 0, 0, tiled=True)]
    all_to_all x6 -> x2, starting transfers between devices: 38.4 us -> 15.4 us  [exchange(): return lax.all_to_all(value, axes, 0, 0, tiled=True)]
    pallas_call x0 -> x10, Pallas kernels: none -> 20.4 us  [call(): pl.pallas_call(kernel, out_shape=[jax.ShapeDtypeStruct(s, d) for s, d in...]
    all_to_all x7 -> x4, blocking collectives: 80.1 us -> 60.9 us  [exchange(): return lax.all_to_all(value, axes, 0, 0, tiled=True)]
    ppermute x0 -> x10, starting transfers between devices: none -> 18.9 us  [swap(): return lax.ppermute(value, axes, [(i, i ^ flip) for i in range(count)])]
    dot_general x15 -> x0, matrix products: 17.5 us -> none  [the longest x4 5.81 us: forward(): s = jnp.dot(anchors, block.T, preferred_element_type=jnp.float32) * INV_TEMP]
    ppermute x0 -> x10, waiting for transfers between devices: none -> 14.9 us  [swap(): return lax.ppermute(value, axes, [(i, i ^ flip) for i in range(count)])]
    dynamic_slice x16 -> x0, local copies, waits for them, and re-layouts: 13.7 us -> none  [the longest x8 10.4 us: on_device(): lax.scan(forward, (zero_rows, zero_rows), (col_blocks, starts))]
  transfers between devices with their start and end apart: 6 -> 12, of which waited for: 4 -> 10; matrix products, arithmetic and copies ran while one was open for 15% -> 0% of each run, Pallas kernels for 0% -> 0%
where the time goes in v1:
time: 142 us; the launch traced here: 141 us
  blocking collectives  60.9 us (43%)
  starting transfers between devices  34.2 us (24%)
  Pallas kernels  20.4 us (14%)
  waiting for transfers between devices  19.4 us (14%)
  local copies, waits for them, and re-layouts  4.46 us (3%)
    all_to_all x4, blocking collectives, exchange(): return lax.all_to_all(value, axes, 0, 0, tiled=True)  60.9 us
    pallas_call x10, Pallas kernels, call(): pl.pallas_call(kernel, out_shape=[jax.ShapeDtypeStruct(s, d) for s, d in...  20.4 us
    ppermute x10, starting transfers between devices, swap(): return lax.ppermute(value, axes, [(i, i ^ flip) for i in range(count)])  18.9 us
    all_to_all x2, starting transfers between devices, exchange(): return lax.all_to_all(value, axes, 0, 0, tiled=True)  15.4 us
    ppermute x10, waiting for transfers between devices, swap(): return lax.ppermute(value, axes, [(i, i ^ flip) for i in range(count)])  14.9 us
    all_to_all x2, waiting for transfers between devices, exchange(): return lax.all_to_all(value, axes, 0, 0, tiled=True)  4.52 us
    unnamed x34, local copies, waits for them, and re-layouts  4.46 us
  transfers between devices with their start and end apart: 12, of which 10 were waited for; matrix products, arithmetic and copies ran while one was open for 0% of the time, Pallas kernels for 0%

profile of v1, /device:TPU:1, one launch (start us, length us, event | category | flops | bytes accessed | tf_op | source)
XLA Modules:
  0.0 140.8 jit_solution(6767755121139090870)
XLA Ops:
  0.6 2.0 %shard_map.93 = (f32[128,128]{1,0:T(8,128)}, f32[128,256]{1,0:T(8,128)}, bf16[128,256]{1,0:T(8,128)(2,1)}) custom-call(bf16[128,512]{1,0:T(8,128)(2,1)} %x_ref.3, bf16[512,256]{1,0:T(8,128)(2,1)} %w_in_ref.1, f32[1,256]{1,0:T(1,128)} %bitcast.7, bf16[256,128]{1,0:T(8,128)(2,1)} %w_out_ref.3), custom_call_target="tpu_custom_call" | custom-call | tf_op jit(solution)/shard_map/pallas_call | solution.py:40
  2.6 2.1 %collective-permute-start = (f32[128,128]{1,0:T(8,128)}, f32[128,128]{1,0:T(8,128)S(1)}, u32[]{:S(2)}, u32[]{:S(2)}) collective-permute-start(f32[128,128]{1,0:T(8,128)} %get-tuple-element.21.part_ref), channel_id=1, source_target_pairs={{0,1},{1,0},{2,3},{3,2},{4,5},{5,4},{6,7},{7,6},{8,9},{9,8},{10,11... | collective-permute-start | bytes 196616 | tf_op jit(solution)/shard_map/ppermute | solution.py:244
  8.9 11.3 %all-to-all-start = ((bf16[32,24,128]{2,1,0:T(8,128)(2,1)}), bf16[32,24,128]{2,1,0:T(8,128)(2,1)S(1)}, u32[]{:S(2)}, u32[]{:S(2)}) async-start(bf16[32,24,128]{2,1,0:T(8,128)(2,1)} %get-tuple-element.22), calls=%async_computation | async-start | bytes 393216 | tf_op jit(solution)/shard_map/all_to_all | solution.py:248
  20.3 5.0 %collective-permute-start.3 = (bf16[128,128]{1,0:T(8,128)(2,1)S(1)}, bf16[128,128]{1,0:T(8,128)(2,1)S(1)}, u32[]{:S(2)}, u32[]{:S(2)}) collective-permute-start(bf16[128,128]{1,0:T(8,128)(2,1)S(1)} %copy-done.6), channel_id=1, source_target_pairs={{0,6},{2,4},{4,2},{6,0},{1,7},{3,5},{5,3},{7,1},{8,14},{10,12},{12... | collective-permute-start | bytes 98312 | tf_op jit(solution)/shard_map/ppermute | solution.py:244
  27.0 2.8 %collective-permute-done.2.e2_ref = bf16[128,128]{1,0:T(8,128)(2,1)S(1)} collective-permute-done((bf16[128,128]{1,0:T(8,128)(2,1)S(1)}, bf16[128,128]{1,0:T(8,128)(2,1)S(1)}, u32[]{:S(2)}, u32[]{:S(2)}) %collective-permute-start.2) | collective-permute-done | bytes 32800 | tf_op jit(solution)/shard_map/ppermute | solution.py:244
  31.1 2.2 %shard_map.95 = f32[32,8,128]{2,1,0:T(8,128)} custom-call(s32[3]{0:T(128)} %pad_add_fusion.at_ref, bf16[32,24,128]{2,1,0:T(8,128)(2,1)} %copy-done, bf16[128,128]{1,0:T(8,128)(2,1)} %get-tuple-element.23.e0_ref, bf16[128,128]{1,0:T(8,128)(2,1)} %copy-done.9, bf16[128,128]{1,0:T(8,128)(2,1)} %copy-done.8, bf16[128,128]{1,0:T(8,128)(2,1)} %copy-done.7), custom_call_target="tpu_custom_call" | custom-call | tf_op jit(solution)/shard_map/pallas_call | solution.py:40
  33.3 20.0 %all_to_all.30.sums_ref = f32[32,8,128]{2,1,0:T(8,128)} all-to-all(f32[32,8,128]{2,1,0:T(8,128)} %shard_map.95), channel_id=1, replica_groups=mesh['z'=8,'x'=4,'yh'=2,'c'=2,'mp'=2] {'z','x'}, dimensions={0} | all-to-all | bytes 262144 | tf_op jit(solution)/shard_map/all_to_all | solution.py:248
  53.3 2.7 %shard_map.96 = (f32[32,16,128]{2,1,0:T(8,128)}, f32[128,128]{1,0:T(8,128)}, f32[128,128]{1,0:T(8,128)}, f32[128,128]{1,0:T(8,128)}, f32[128,128]{1,0:T(8,128)}, /*index=5*/f32[8,128]{1,0:T(8,128)}) custom-call(s32[3]{0:T(128)} %pad_add_fusion.at_ref, bf16[32,24,128]{2,1,0:T(8,128)(2,1)} %copy-done, f32[32,8,128]{2,1,0:T(8,128)} %all_to_all.30.sums_ref, ...), custom_call_target="tpu_custom_call" | custom-call | tf_op jit(solution)/shard_map/pallas_call | solution.py:40
  56.1 4.0 %all-to-all-start.2 = ((f32[32,16,128]{2,1,0:T(8,128)}), f32[32,16,128]{2,1,0:T(8,128)S(1)}, u32[]{:S(2)}, u32[]{:S(2)}) async-start(f32[32,16,128]{2,1,0:T(8,128)} %get-tuple-element.24), calls=%async_computation.2 | async-start | bytes 524288 | tf_op jit(solution)/shard_map/all_to_all | solution.py:248
  61.7 2.2 %collective-permute-start.6 = (f32[128,128]{1,0:T(8,128)S(1)}, f32[128,128]{1,0:T(8,128)S(1)}, u32[]{:S(2)}, u32[]{:S(2)}) collective-permute-start(f32[128,128]{1,0:T(8,128)S(1)} %copy-done.14), channel_id=1, source_target_pairs={{0,6},{2,4},{4,2},{6,0},{1,7},{3,5},{5,3},{7,1},{8,14},{10,12},{12... | collective-permute-start | bytes 196616 | tf_op jit(solution)/shard_map/ppermute | solution.py:244
  63.8 1.8 %collective-permute-done.5.r2_ref = f32[128,128]{1,0:T(8,128)S(1)} collective-permute-done((f32[128,128]{1,0:T(8,128)S(1)}, f32[128,128]{1,0:T(8,128)S(1)}, u32[]{:S(2)}, u32[]{:S(2)}) %collective-permute-start.5) | collective-permute-done | bytes 65568 | tf_op jit(solution)/shard_map/ppermute | solution.py:244
  65.6 2.0 %collective-permute-done.6.r3_ref = f32[128,128]{1,0:T(8,128)S(1)} collective-permute-done((f32[128,128]{1,0:T(8,128)S(1)}, f32[128,128]{1,0:T(8,128)S(1)}, u32[]{:S(2)}, u32[]{:S(2)}) %collective-permute-start.6) | collective-permute-done | bytes 65568 | tf_op jit(solution)/shard_map/ppermute | solution.py:244
  67.6 4.2 %all-to-all-done.2.rows_ref = f32[32,16,128]{2,1,0:T(8,128)S(1)} async-done(((f32[32,16,128]{2,1,0:T(8,128)}), f32[32,16,128]{2,1,0:T(8,128)S(1)}, u32[]{:S(2)}, u32[]{:S(2)}) %all-to-all-start.2) | async-done | bytes 262176 | tf_op jit(solution)/shard_map/all_to_all | solution.py:248
  72.5 1.8 %shard_map.97.mine_ref = f32[136,128]{1,0:T(8,128)} custom-call(s32[3]{0:T(128)} %pad_add_fusion.at_ref, s32[128]{0:T(128)} %window_ref.3, f32[32,16,128]{2,1,0:T(8,128)} %copy-done.2, f32[128,128]{1,0:T(8,128)} %get-tuple-element.25.c0_ref, f32[128,128]{1,0:T(8,128)} %copy-done.11, f32[128,128]{1,0:T(8,128)} %copy-done.12, f32[128,128]{1,0:T(8,128)} %copy-done.13, ...), custom_call_target="tpu_custom_call" | custom-call | tf_op jit(solution)/shard_map/pallas_call | solution.py:40
  74.7 3.0 %collective-permute-done.7.theirs_ref = f32[136,128]{1,0:T(8,128)S(1)} collective-permute-done((f32[136,128]{1,0:T(8,128)}, f32[136,128]{1,0:T(8,128)S(1)}, u32[]{:S(2)}, u32[]{:S(2)}) %collective-permute-start.7) | collective-permute-done | bytes 69664 | tf_op jit(solution)/shard_map/ppermute | solution.py:244
  78.3 2.6 %shard_map.98 = (f32[1,32]{1,0:T(1,128)}, f32[8,88,128]{2,1,0:T(8,128)}, f32[8,88,128]{2,1,0:T(8,128)}) custom-call(s32[3]{0:T(128)} %pad_add_fusion.at_ref, f32[136,128]{1,0:T(8,128)} %shard_map.97.mine_ref, f32[136,128]{1,0:T(8,128)} %copy-done.10, f32[128,128]{1,0:T(8,128)} %get-tuple-element.21.part_ref, f32[128,128]{1,0:T(8,128)} %copy-done.5, ...), custom_call_target="tpu_custom_call" | custom-call | tf_op jit(solution)/shard_map/pallas_call | solution.py:40
  80.9 3.3 %collective-permute-start.8 = (f32[8,88,128]{2,1,0:T(8,128)}, f32[8,88,128]{2,1,0:T(8,128)S(1)}, u32[]{:S(2)}, u32[]{:S(2)}) collective-permute-start(f32[8,88,128]{2,1,0:T(8,128)} %get-tuple-element.34), channel_id=1, source_target_pairs={{0,2},{2,0},{1,3},{3,1},{4,6},{6,4},{5,7},{7,5},{8,10},{10,8},{9,1... | collective-permute-start | bytes 1081352 | tf_op jit(solution)/shard_map/ppermute | solution.py:244
  86.5 1.9 %shard_map.99 = f32[8,88,128]{2,1,0:T(8,128)} custom-call(f32[8,88,128]{2,1,0:T(8,128)} %get-tuple-element.33.a_ref, f32[8,88,128]{2,1,0:T(8,128)} %copy-done.4), custom_call_target="tpu_custom_call" | custom-call | tf_op jit(solution)/shard_map/pallas_call | solution.py:40
  88.4 13.2 %all_to_all.31.in_ref = f32[8,88,128]{2,1,0:T(8,128)} all-to-all(f32[8,88,128]{2,1,0:T(8,128)} %shard_map.99), channel_id=1, replica_groups=mesh['z'=8,'x'=4,'yh'=2,'c'=2,'mp'=2] {'x','yh'}, dimensions={0} | all-to-all | bytes 720896 | tf_op jit(solution)/shard_map/all_to_all | solution.py:248
  103.4 16.3 %all_to_all.32.in_ref = f32[8,88,128]{2,1,0:T(8,128)} all-to-all(f32[8,88,128]{2,1,0:T(8,128)} %shard_map.100), channel_id=1, replica_groups=mesh['z'=8,'x'=4,'yh'=2,'c'=2,'mp'=2] {'z'}, dimensions={0} | all-to-all | bytes 720896 | tf_op jit(solution)/shard_map/all_to_all | solution.py:248
  119.7 1.7 %shard_map.101 = f32[8,88,128]{2,1,0:T(8,128)} custom-call(f32[8,88,128]{2,1,0:T(8,128)} %all_to_all.32.in_ref), custom_call_target="tpu_custom_call" | custom-call | tf_op jit(solution)/shard_map/pallas_call | solution.py:40
  121.4 11.4 %all_to_all.33.mine_ref = f32[8,88,128]{2,1,0:T(8,128)S(1)} all-to-all(f32[8,88,128]{2,1,0:T(8,128)} %shard_map.101), channel_id=1, replica_groups=mesh['z'=8,'x'=4,'yh'=2,'c'=2,'mp'=2] {'x','yh'}, dimensions={0} | all-to-all | bytes 720896 | tf_op jit(solution)/shard_map/all_to_all | solution.py:248
  132.8 3.8 %collective-permute-start.9 = (f32[8,88,128]{2,1,0:T(8,128)S(1)}, f32[8,88,128]{2,1,0:T(8,128)S(1)}, u32[]{:S(2)}, u32[]{:S(2)}) collective-permute-start(f32[8,88,128]{2,1,0:T(8,128)S(1)} %all_to_all.33.mine_ref), channel_id=1, source_target_pairs={{0,2},{2,0},{1,3},{3,1},{4,6},{6,4},{5,7},{7,5},{8,10},{10,8},{9,1... | collective-permute-start | bytes 1081352 | tf_op jit(solution)/shard_map/ppermute | solution.py:244
  138.7 2.0 %shard_map.102 = (f32[512,256]{1,0:T(8,128)}, f32[2,128]{1,0:T(2,128)}, f32[256,128]{1,0:T(8,128)}) custom-call(s32[3]{0:T(128)} %pad_add_fusion.at_ref, f32[8,88,128]{2,1,0:T(8,128)} %copy-done.1, f32[8,88,128]{2,1,0:T(8,128)} %copy-done.3), custom_call_target="tpu_custom_call" | custom-call | tf_op jit(solution)/shard_map/pallas_call | solution.py:40
  (49 shorter events, 16.6 us)
Async XLA Ops:
  2.6 4.0 %collective-permute-start = (f32[128,128]{1,0:T(8,128)}, f32[128,128]{1,0:T(8,128)S(1)}, u32[]{:S(2)}, u32[]{:S(2)}) collective-permute-start(f32[128,128]{1,0:T(8,128)} %get-tuple-element.21.part_ref), channel_id=1, source_target_pairs={{0,1},{1,0},{2,3},{3,2},{4,5},{5,4},{6,7},{7,6},{8,9},{9,8},{10,11... | collective-permute-start | bytes 196616 | tf_op jit(solution)/shard_map/ppermute | solution.py:244
  8.9 11.3 %copy-start.6 = (bf16[128,128]{1,0:T(8,128)(2,1)S(1)}, bf16[128,128]{1,0:T(8,128)(2,1)}, u32[]{:S(2)}) copy-start(bf16[128,128]{1,0:T(8,128)(2,1)} %get-tuple-element.23.e0_ref) | copy-start | bytes 98308
  8.9 21.2 %all-to-all-start = ((bf16[32,24,128]{2,1,0:T(8,128)(2,1)}), bf16[32,24,128]{2,1,0:T(8,128)(2,1)S(1)}, u32[]{:S(2)}, u32[]{:S(2)}) async-start(bf16[32,24,128]{2,1,0:T(8,128)(2,1)} %get-tuple-element.22), calls=%async_computation | async-start | bytes 393216 | tf_op jit(solution)/shard_map/all_to_all | solution.py:248
  20.3 6.8 %collective-permute-start.3 = (bf16[128,128]{1,0:T(8,128)(2,1)S(1)}, bf16[128,128]{1,0:T(8,128)(2,1)S(1)}, u32[]{:S(2)}, u32[]{:S(2)}) collective-permute-start(bf16[128,128]{1,0:T(8,128)(2,1)S(1)} %copy-done.6), channel_id=1, source_target_pairs={{0,6},{2,4},{4,2},{6,0},{1,7},{3,5},{5,3},{7,1},{8,14},{10,12},{12... | collective-permute-start | bytes 98312 | tf_op jit(solution)/shard_map/ppermute | solution.py:244
  25.3 4.6 %collective-permute-start.2 = (bf16[128,128]{1,0:T(8,128)(2,1)S(1)}, bf16[128,128]{1,0:T(8,128)(2,1)S(1)}, u32[]{:S(2)}, u32[]{:S(2)}) collective-permute-start(bf16[128,128]{1,0:T(8,128)(2,1)S(1)} %copy-done.6), channel_id=1, source_target_pairs={{0,4},{2,6},{4,0},{6,2},{1,5},{3,7},{5,1},{7,3},{8,12},{10,14},{12... | collective-permute-start | bytes 98312 | tf_op jit(solution)/shard_map/ppermute | solution.py:244
  25.3 4.5 %collective-permute-start.1 = (bf16[128,128]{1,0:T(8,128)(2,1)S(1)}, bf16[128,128]{1,0:T(8,128)(2,1)S(1)}, u32[]{:S(2)}, u32[]{:S(2)}) collective-permute-start(bf16[128,128]{1,0:T(8,128)(2,1)S(1)} %copy-done.6), channel_id=1, source_target_pairs={{0,2},{2,0},{4,6},{6,4},{1,3},{3,1},{5,7},{7,5},{8,10},{10,8},{12,... | collective-permute-start | bytes 98312 | tf_op jit(solution)/shard_map/ppermute | solution.py:244
  27.0 3.1 %copy-start.7 = (bf16[128,128]{1,0:T(8,128)(2,1)}, bf16[128,128]{1,0:T(8,128)(2,1)S(1)}, u32[]{:S(2)}) copy-start(bf16[128,128]{1,0:T(8,128)(2,1)S(1)} %collective-permute-done.3.e3_ref) | copy-start | bytes 98308
  56.0 4.1 %copy-start.16 = (f32[128,128]{1,0:T(8,128)S(1)}, f32[128,128]{1,0:T(8,128)}, u32[]{:S(2)}) copy-start(f32[128,128]{1,0:T(8,128)} %get-tuple-element.26) | copy-start | bytes 196612
  56.0 4.5 %copy-start.15 = (f32[128,128]{1,0:T(8,128)S(1)}, f32[128,128]{1,0:T(8,128)}, u32[]{:S(2)}) copy-start(f32[128,128]{1,0:T(8,128)} %get-tuple-element.27) | copy-start | bytes 196612
  56.1 5.6 %copy-start.14 = (f32[128,128]{1,0:T(8,128)S(1)}, f32[128,128]{1,0:T(8,128)}, u32[]{:S(2)}) copy-start(f32[128,128]{1,0:T(8,128)} %get-tuple-element.28) | copy-start | bytes 196612
  56.1 15.8 %all-to-all-start.2 = ((f32[32,16,128]{2,1,0:T(8,128)}), f32[32,16,128]{2,1,0:T(8,128)S(1)}, u32[]{:S(2)}, u32[]{:S(2)}) async-start(f32[32,16,128]{2,1,0:T(8,128)} %get-tuple-element.24), calls=%async_computation.2 | async-start | bytes 524288 | tf_op jit(solution)/shard_map/all_to_all | solution.py:248
  60.1 3.7 %collective-permute-start.4 = (f32[128,128]{1,0:T(8,128)S(1)}, f32[128,128]{1,0:T(8,128)S(1)}, u32[]{:S(2)}, u32[]{:S(2)}) collective-permute-start(f32[128,128]{1,0:T(8,128)S(1)} %copy-done.16), channel_id=1, source_target_pairs={{0,2},{2,0},{4,6},{6,4},{1,3},{3,1},{5,7},{7,5},{8,10},{10,8},{12,... | collective-permute-start | bytes 196616 | tf_op jit(solution)/shard_map/ppermute | solution.py:244
  60.6 5.0 %collective-permute-start.5 = (f32[128,128]{1,0:T(8,128)S(1)}, f32[128,128]{1,0:T(8,128)S(1)}, u32[]{:S(2)}, u32[]{:S(2)}) collective-permute-start(f32[128,128]{1,0:T(8,128)S(1)} %copy-done.15), channel_id=1, source_target_pairs={{0,4},{2,6},{4,0},{6,2},{1,5},{3,7},{5,1},{7,3},{8,12},{10,14},{12... | collective-permute-start | bytes 196616 | tf_op jit(solution)/shard_map/ppermute | solution.py:244
  61.7 5.9 %collective-permute-start.6 = (f32[128,128]{1,0:T(8,128)S(1)}, f32[128,128]{1,0:T(8,128)S(1)}, u32[]{:S(2)}, u32[]{:S(2)}) collective-permute-start(f32[128,128]{1,0:T(8,128)S(1)} %copy-done.14), channel_id=1, source_target_pairs={{0,6},{2,4},{4,2},{6,0},{1,7},{3,5},{5,3},{7,1},{8,14},{10,12},{12... | collective-permute-start | bytes 196616 | tf_op jit(solution)/shard_map/ppermute | solution.py:244
  63.8 8.0 %copy-start.11 = (f32[128,128]{1,0:T(8,128)}, f32[128,128]{1,0:T(8,128)S(1)}, u32[]{:S(2)}) copy-start(f32[128,128]{1,0:T(8,128)S(1)} %collective-permute-done.4.r1_ref) | copy-start | bytes 196612
  65.6 6.2 %copy-start.12 = (f32[128,128]{1,0:T(8,128)}, f32[128,128]{1,0:T(8,128)S(1)}, u32[]{:S(2)}) copy-start(f32[128,128]{1,0:T(8,128)S(1)} %collective-permute-done.5.r2_ref) | copy-start | bytes 196612
  67.6 4.2 %copy-start.13 = (f32[128,128]{1,0:T(8,128)}, f32[128,128]{1,0:T(8,128)S(1)}, u32[]{:S(2)}) copy-start(f32[128,128]{1,0:T(8,128)S(1)} %collective-permute-done.6.r3_ref) | copy-start | bytes 196612
  71.8 0.7 copy-start.2
  74.3 3.4 %collective-permute-start.7 = (f32[136,128]{1,0:T(8,128)}, f32[136,128]{1,0:T(8,128)S(1)}, u32[]{:S(2)}, u32[]{:S(2)}) collective-permute-start(f32[136,128]{1,0:T(8,128)} %shard_map.97.mine_ref), channel_id=1, source_target_pairs={{0,1},{1,0},{2,3},{3,2},{4,5},{5,4},{6,7},{7,6},{8,9},{9,8},{10,11... | collective-permute-start | bytes 208904 | tf_op jit(solution)/shard_map/ppermute | solution.py:244
  80.9 4.8 %collective-permute-start.8 = (f32[8,88,128]{2,1,0:T(8,128)}, f32[8,88,128]{2,1,0:T(8,128)S(1)}, u32[]{:S(2)}, u32[]{:S(2)}) collective-permute-start(f32[8,88,128]{2,1,0:T(8,128)} %get-tuple-element.34), channel_id=1, source_target_pairs={{0,2},{2,0},{1,3},{3,1},{4,6},{6,4},{5,7},{7,5},{8,10},{10,8},{9,1... | collective-permute-start | bytes 1081352 | tf_op jit(solution)/shard_map/ppermute | solution.py:244
  85.8 0.8 copy-start.4
  132.8 5.1 %copy-start.1 = (f32[8,88,128]{2,1,0:T(8,128)}, f32[8,88,128]{2,1,0:T(8,128)S(1)}, u32[]{:S(2)}) copy-start(f32[8,88,128]{2,1,0:T(8,128)S(1)} %all_to_all.33.mine_ref) | copy-start | bytes 1081348
  132.8 5.1 %collective-permute-start.9 = (f32[8,88,128]{2,1,0:T(8,128)S(1)}, f32[8,88,128]{2,1,0:T(8,128)S(1)}, u32[]{:S(2)}, u32[]{:S(2)}) collective-permute-start(f32[8,88,128]{2,1,0:T(8,128)S(1)} %all_to_all.33.mine_ref), channel_id=1, source_target_pairs={{0,2},{2,0},{1,3},{3,1},{4,6},{6,4},{5,7},{7,5},{8,10},{10,8},{9,1... | collective-permute-start | bytes 1081352 | tf_op jit(solution)/shard_map/ppermute | solution.py:244
  138.0 0.8 copy-start.3
  (5 other events, 3.1 us)

commit v2 on v1

--- a/solution.py
+++ b/solution.py
@@ -32,14 +32,20 @@
 I32 = jnp.int32
 
 
-def call(kernel, outs, *args, smem=(), scratch=()):
+def call(kernel, outs, *args, smem=(), scratch=(), first=False, last=False):
     specs = [
         pl.BlockSpec(memory_space=pltpu.SMEM if i in smem else pltpu.VMEM)
         for i in range(len(args))
     ]
+    if not first:
+        args = [
+            a if i in smem else pltpu.with_memory_space_constraint(a, pltpu.VMEM)
+            for i, a in enumerate(args)
+        ]
+    kind = jax.ShapeDtypeStruct if last else pltpu.VMEM
     return pl.pallas_call(
         kernel,
-        out_shape=[jax.ShapeDtypeStruct(s, d) for s, d in outs],
+        out_shape=[kind(s, d) for s, d in outs],
         in_specs=specs,
         out_specs=[pl.BlockSpec(memory_space=pltpu.VMEM)] * len(outs),
         scratch_shapes=list(scratch),
@@ -257,6 +263,7 @@
         w_in,
         b_in.reshape(1, -1),
         w_out,
+        first=True,
     )
     other = swap(part, "mp", 1)
     emb, message = call(
@@ -329,6 +336,7 @@
         got,
         smem=(0,),
         scratch=[pltpu.VMEM((1280, EMB), F32)],
+        last=True,
     )
     return (row_loss.reshape(-1), grad_in, grad_b.reshape(-1), grad_out)
 

time: 142 us -> 122 us (0.86)
  Pallas kernels: 20.4 us -> 10.3 us
  blocking collectives: 60.9 us -> 56.7 us
  local copies, waits for them, and re-layouts: 4.46 us -> 0.52 us
    pallas_call x10, Pallas kernels: 20.4 us -> 10.3 us  [call(): pl.pallas_call(kernel, out_shape=[kind(s, d) for s, d in outs], in_specs=...]
    all_to_all x4, blocking collectives: 60.9 us -> 56.7 us  [exchange(): return lax.all_to_all(value, axes, 0, 0, tiled=True)]
    unnamed x34 -> x7, local copies, waits for them, and re-layouts: 4.46 us -> 0.52 us
  transfers between devices with their start and end apart: 12 -> 12, of which waited for: 10 -> 10; matrix products, arithmetic and copies ran while one was open for 0% -> 1% of each run, Pallas kernels for 0% -> 0%
where the time goes in v2:
time: 122 us
  blocking collectives  56.7 us (46%)
  starting transfers between devices  34.4 us (28%)
  waiting for transfers between devices  18.3 us (15%)
  Pallas kernels  10.3 us (8%)
    all_to_all x4, blocking collectives, exchange(): return lax.all_to_all(value, axes, 0, 0, tiled=True)  56.7 us
    ppermute x10, starting transfers between devices, swap(): return lax.ppermute(value, axes, [(i, i ^ flip) for i in range(count)])  19.4 us
    all_to_all x2, starting transfers between devices, exchange(): return lax.all_to_all(value, axes, 0, 0, tiled=True)  15.1 us
    ppermute x10, waiting for transfers between devices, swap(): return lax.ppermute(value, axes, [(i, i ^ flip) for i in range(count)])  13.7 us
    pallas_call x10, Pallas kernels, call(): pl.pallas_call(kernel, out_shape=[kind(s, d) for s, d in outs], in_specs=...  10.3 us
    all_to_all x2, waiting for transfers between devices, exchange(): return lax.all_to_all(value, axes, 0, 0, tiled=True)  4.56 us
  transfers between devices with their start and end apart: 12, of which 10 were waited for; matrix products, arithmetic and copies ran while one was open for 1% of the time, Pallas kernels for 0%

profile of v2, /device:TPU:1, one launch (start us, length us, event | category | flops | bytes accessed | tf_op | source)
XLA Modules:
  0.0 121.6 jit_solution(17717887694866911296)
XLA Ops:
  0.6 1.3 %shard_map.93 = (f32[128,128]{1,0:T(8,128)S(1)}, f32[128,256]{1,0:T(8,128)S(1)}, bf16[128,256]{1,0:T(8,128)(2,1)S(1)}) custom-call(bf16[128,512]{1,0:T(8,128)(2,1)} %x_ref.3, bf16[512,256]{1,0:T(8,128)(2,1)} %w_in_ref.1, f32[1,256]{1,0:T(1,128)} %bitcast.9, bf16[256,128]{1,0:T(8,128)(2,1)} %w_out_ref.3), custom_call_target="tpu_custom_call" | custom-call | tf_op jit(solution)/shard_map/pallas_call | solution.py:46
  2.0 2.2 %collective-permute-start = (f32[128,128]{1,0:T(8,128)S(1)}, f32[128,128]{1,0:T(8,128)S(1)}, u32[]{:S(2)}, u32[]{:S(2)}) collective-permute-start(f32[128,128]{1,0:T(8,128)S(1)} %get-tuple-element.21.part_ref), channel_id=1, source_target_pairs={{0,1},{1,0},{2,3},{3,2},{4,5},{5,4},{6,7},{7,6},{8,9},{9,8},{10,11... | collective-permute-start | bytes 196616 | tf_op jit(solution)/shard_map/ppermute | solution.py:250
  5.8 1.5 %shard_map.94 = (bf16[128,128]{1,0:T(8,128)(2,1)S(1)}, bf16[32,24,128]{2,1,0:T(8,128)(2,1)}) custom-call(s32[3]{0:T(128)} %pad_add_fusion.at_ref, s32[128]{0:T(128)} %window_ref.3, f32[128,128]{1,0:T(8,128)S(1)} %get-tuple-element.21.part_ref, f32[128,128]{1,0:T(8,128)S(1)} %collective-permute-done.other_ref, s32[1,128]{1,0:T(1,128)S(1)} %bitcast.8), custom_call_target="tpu_custom_call" | custom-call | tf_op jit(solution)/shard_map/pallas_call | solution.py:46
  7.3 11.2 %all-to-all-start = ((bf16[32,24,128]{2,1,0:T(8,128)(2,1)}), bf16[32,24,128]{2,1,0:T(8,128)(2,1)S(1)}, u32[]{:S(2)}, u32[]{:S(2)}) async-start(bf16[32,24,128]{2,1,0:T(8,128)(2,1)} %get-tuple-element.22), calls=%async_computation | async-start | bytes 393216 | tf_op jit(solution)/shard_map/all_to_all | solution.py:254
  18.5 5.0 %collective-permute-start.3 = (bf16[128,128]{1,0:T(8,128)(2,1)S(1)}, bf16[128,128]{1,0:T(8,128)(2,1)S(1)}, u32[]{:S(2)}, u32[]{:S(2)}) collective-permute-start(bf16[128,128]{1,0:T(8,128)(2,1)S(1)} %get-tuple-element.23.e0_ref), channel_id=1, source_target_pairs={{0,6},{2,4},{4,2},{6,0},{1,7},{3,5},{5,3},{7,1},{8,14},{10,12},{12... | collective-permute-start | bytes 98312 | tf_op jit(solution)/shard_map/ppermute | solution.py:250
  24.0 1.4 %collective-permute-done.3.e3_ref = bf16[128,128]{1,0:T(8,128)(2,1)S(1)} collective-permute-done((bf16[128,128]{1,0:T(8,128)(2,1)S(1)}, bf16[128,128]{1,0:T(8,128)(2,1)S(1)}, u32[]{:S(2)}, u32[]{:S(2)}) %collective-permute-start.3) | collective-permute-done | bytes 32800 | tf_op jit(solution)/shard_map/ppermute | solution.py:250
  25.4 2.7 %collective-permute-done.2.e2_ref = bf16[128,128]{1,0:T(8,128)(2,1)S(1)} collective-permute-done((bf16[128,128]{1,0:T(8,128)(2,1)S(1)}, bf16[128,128]{1,0:T(8,128)(2,1)S(1)}, u32[]{:S(2)}, u32[]{:S(2)}) %collective-permute-start.2) | collective-permute-done | bytes 32800 | tf_op jit(solution)/shard_map/ppermute | solution.py:250
  28.4 1.2 shard_map.95
  29.6 19.4 %all_to_all.30.sums_ref = f32[32,8,128]{2,1,0:T(8,128)S(1)} all-to-all(f32[32,8,128]{2,1,0:T(8,128)S(1)} %shard_map.95), channel_id=1, replica_groups=mesh['z'=8,'x'=4,'yh'=2,'c'=2,'mp'=2] {'z','x'}, dimensions={0} | all-to-all | bytes 262144 | tf_op jit(solution)/shard_map/all_to_all | solution.py:254
  49.0 2.4 %shard_map.96 = (f32[32,16,128]{2,1,0:T(8,128)}, f32[128,128]{1,0:T(8,128)S(1)}, f32[128,128]{1,0:T(8,128)S(1)}, f32[128,128]{1,0:T(8,128)S(1)}, f32[128,128]{1,0:T(8,128)S(1)}, /*index=5*/f32[8,128]{1,0:T(8,128)S(1)}) custom-call(s32[3]{0:T(128)} %pad_add_fusion.at_ref, bf16[32,24,128]{2,1,0:T(8,128)(2,1)S(1)} %all-to-all-done.msg_ref, ...), custom_call_target="tpu_custom_call" | custom-call | tf_op jit(solution)/shard_map/pallas_call | solution.py:46
  51.4 3.9 %all-to-all-start.2 = ((f32[32,16,128]{2,1,0:T(8,128)}), f32[32,16,128]{2,1,0:T(8,128)S(1)}, u32[]{:S(2)}, u32[]{:S(2)}) async-start(f32[32,16,128]{2,1,0:T(8,128)} %get-tuple-element.24), calls=%async_computation.2 | async-start | bytes 524288 | tf_op jit(solution)/shard_map/all_to_all | solution.py:254
  56.8 2.2 %collective-permute-start.6 = (f32[128,128]{1,0:T(8,128)S(1)}, f32[128,128]{1,0:T(8,128)S(1)}, u32[]{:S(2)}, u32[]{:S(2)}) collective-permute-start(f32[128,128]{1,0:T(8,128)S(1)} %get-tuple-element.28), channel_id=1, source_target_pairs={{0,6},{2,4},{4,2},{6,0},{1,7},{3,5},{5,3},{7,1},{8,14},{10,12},{12... | collective-permute-start | bytes 196616 | tf_op jit(solution)/shard_map/ppermute | solution.py:250
  59.0 1.8 %collective-permute-done.5.r2_ref = f32[128,128]{1,0:T(8,128)S(1)} collective-permute-done((f32[128,128]{1,0:T(8,128)S(1)}, f32[128,128]{1,0:T(8,128)S(1)}, u32[]{:S(2)}, u32[]{:S(2)}) %collective-permute-start.5) | collective-permute-done | bytes 65568 | tf_op jit(solution)/shard_map/ppermute | solution.py:250
  60.8 2.0 %collective-permute-done.6.r3_ref = f32[128,128]{1,0:T(8,128)S(1)} collective-permute-done((f32[128,128]{1,0:T(8,128)S(1)}, f32[128,128]{1,0:T(8,128)S(1)}, u32[]{:S(2)}, u32[]{:S(2)}) %collective-permute-start.6) | collective-permute-done | bytes 65568 | tf_op jit(solution)/shard_map/ppermute | solution.py:250
  62.8 4.2 %all-to-all-done.2.rows_ref = f32[32,16,128]{2,1,0:T(8,128)S(1)} async-done(((f32[32,16,128]{2,1,0:T(8,128)}), f32[32,16,128]{2,1,0:T(8,128)S(1)}, u32[]{:S(2)}, u32[]{:S(2)}) %all-to-all-start.2) | async-done | bytes 262176 | tf_op jit(solution)/shard_map/all_to_all | solution.py:254
  68.4 2.8 %collective-permute-done.7.theirs_ref = f32[136,128]{1,0:T(8,128)S(1)} collective-permute-done((f32[136,128]{1,0:T(8,128)S(1)}, f32[136,128]{1,0:T(8,128)S(1)}, u32[]{:S(2)}, u32[]{:S(2)}) %collective-permute-start.7) | collective-permute-done | bytes 69664 | tf_op jit(solution)/shard_map/ppermute | solution.py:250
  71.1 1.3 %shard_map.98 = (f32[1,32]{1,0:T(1,128)S(1)}, f32[8,88,128]{2,1,0:T(8,128)S(1)}, f32[8,88,128]{2,1,0:T(8,128)S(1)}) custom-call(s32[3]{0:T(128)} %pad_add_fusion.at_ref, f32[136,128]{1,0:T(8,128)S(1)} %shard_map.97.mine_ref, f32[136,128]{1,0:T(8,128)S(1)} %collective-permute-done.7.theirs_ref, f32[128,128]{1,0:T(8,128)S(1)} %get-tuple-element.21.part_ref, ...), custom_call_target="tpu_custom_call" | custom-call | tf_op jit(solution)/shard_map/pallas_call | solution.py:46
  72.4 3.4 %collective-permute-start.8 = (f32[8,88,128]{2,1,0:T(8,128)S(1)}, f32[8,88,128]{2,1,0:T(8,128)S(1)}, u32[]{:S(2)}, u32[]{:S(2)}) collective-permute-start(f32[8,88,128]{2,1,0:T(8,128)S(1)} %get-tuple-element.34), channel_id=1, source_target_pairs={{0,2},{2,0},{1,3},{3,1},{4,6},{6,4},{5,7},{7,5},{8,10},{10,8},{9,1... | collective-permute-start | bytes 1081352 | tf_op jit(solution)/shard_map/ppermute | solution.py:250
  75.8 1.3 %collective-permute-done.8.b_ref = f32[8,88,128]{2,1,0:T(8,128)S(1)} collective-permute-done((f32[8,88,128]{2,1,0:T(8,128)S(1)}, f32[8,88,128]{2,1,0:T(8,128)S(1)}, u32[]{:S(2)}, u32[]{:S(2)}) %collective-permute-start.8) | collective-permute-done | bytes 360480 | tf_op jit(solution)/shard_map/ppermute | solution.py:250
  77.2 11.0 %all_to_all.31.in_ref = f32[8,88,128]{2,1,0:T(8,128)S(1)} all-to-all(f32[8,88,128]{2,1,0:T(8,128)S(1)} %shard_map.99), channel_id=1, replica_groups=mesh['z'=8,'x'=4,'yh'=2,'c'=2,'mp'=2] {'x','yh'}, dimensions={0} | all-to-all | bytes 720896 | tf_op jit(solution)/shard_map/all_to_all | solution.py:254
  88.3 14.4 %all_to_all.32.in_ref = f32[8,88,128]{2,1,0:T(8,128)S(1)} all-to-all(f32[8,88,128]{2,1,0:T(8,128)S(1)} %shard_map.100), channel_id=1, replica_groups=mesh['z'=8,'x'=4,'yh'=2,'c'=2,'mp'=2] {'z'}, dimensions={0} | all-to-all | bytes 720896 | tf_op jit(solution)/shard_map/all_to_all | solution.py:254
  102.7 11.9 %all_to_all.33.mine_ref = f32[8,88,128]{2,1,0:T(8,128)S(1)} all-to-all(f32[8,88,128]{2,1,0:T(8,128)S(1)} %shard_map.101), channel_id=1, replica_groups=mesh['z'=8,'x'=4,'yh'=2,'c'=2,'mp'=2] {'x','yh'}, dimensions={0} | all-to-all | bytes 720896 | tf_op jit(solution)/shard_map/all_to_all | solution.py:254
  114.6 4.1 %collective-permute-start.9 = (f32[8,88,128]{2,1,0:T(8,128)S(1)}, f32[8,88,128]{2,1,0:T(8,128)S(1)}, u32[]{:S(2)}, u32[]{:S(2)}) collective-permute-start(f32[8,88,128]{2,1,0:T(8,128)S(1)} %all_to_all.33.mine_ref), channel_id=1, source_target_pairs={{0,2},{2,0},{1,3},{3,1},{4,6},{6,4},{5,7},{7,5},{8,10},{10,8},{9,1... | collective-permute-start | bytes 1081352 | tf_op jit(solution)/shard_map/ppermute | solution.py:250
  120.0 1.6 %shard_map.102 = (f32[512,256]{1,0:T(8,128)}, f32[2,128]{1,0:T(2,128)}, f32[256,128]{1,0:T(8,128)}) custom-call(s32[3]{0:T(128)} %pad_add_fusion.at_ref, f32[8,88,128]{2,1,0:T(8,128)S(1)} %all_to_all.33.mine_ref, f32[8,88,128]{2,1,0:T(8,128)S(1)} %collective-permute-done.9.theirs_ref), custom_call_target="tpu_custom_call" | custom-call | tf_op jit(solution)/shard_map/pallas_call | solution.py:46
  (22 shorter events, 6.8 us)
Async XLA Ops:
  2.0 3.9 %collective-permute-start = (f32[128,128]{1,0:T(8,128)S(1)}, f32[128,128]{1,0:T(8,128)S(1)}, u32[]{:S(2)}, u32[]{:S(2)}) collective-permute-start(f32[128,128]{1,0:T(8,128)S(1)} %get-tuple-element.21.part_ref), channel_id=1, source_target_pairs={{0,1},{1,0},{2,3},{3,2},{4,5},{5,4},{6,7},{7,6},{8,9},{9,8},{10,11... | collective-permute-start | bytes 196616 | tf_op jit(solution)/shard_map/ppermute | solution.py:250
  4.8 1.1 copy-start.2
  7.3 21.1 %all-to-all-start = ((bf16[32,24,128]{2,1,0:T(8,128)(2,1)}), bf16[32,24,128]{2,1,0:T(8,128)(2,1)S(1)}, u32[]{:S(2)}, u32[]{:S(2)}) async-start(bf16[32,24,128]{2,1,0:T(8,128)(2,1)} %get-tuple-element.22), calls=%async_computation | async-start | bytes 393216 | tf_op jit(solution)/shard_map/all_to_all | solution.py:254
  18.5 6.9 %collective-permute-start.3 = (bf16[128,128]{1,0:T(8,128)(2,1)S(1)}, bf16[128,128]{1,0:T(8,128)(2,1)S(1)}, u32[]{:S(2)}, u32[]{:S(2)}) collective-permute-start(bf16[128,128]{1,0:T(8,128)(2,1)S(1)} %get-tuple-element.23.e0_ref), channel_id=1, source_target_pairs={{0,6},{2,4},{4,2},{6,0},{1,7},{3,5},{5,3},{7,1},{8,14},{10,12},{12... | collective-permute-start | bytes 98312 | tf_op jit(solution)/shard_map/ppermute | solution.py:250
  23.5 4.6 %collective-permute-start.2 = (bf16[128,128]{1,0:T(8,128)(2,1)S(1)}, bf16[128,128]{1,0:T(8,128)(2,1)S(1)}, u32[]{:S(2)}, u32[]{:S(2)}) collective-permute-start(bf16[128,128]{1,0:T(8,128)(2,1)S(1)} %get-tuple-element.23.e0_ref), channel_id=1, source_target_pairs={{0,4},{2,6},{4,0},{6,2},{1,5},{3,7},{5,1},{7,3},{8,12},{10,14},{12... | collective-permute-start | bytes 98312 | tf_op jit(solution)/shard_map/ppermute | solution.py:250
  23.6 4.5 %collective-permute-start.1 = (bf16[128,128]{1,0:T(8,128)(2,1)S(1)}, bf16[128,128]{1,0:T(8,128)(2,1)S(1)}, u32[]{:S(2)}, u32[]{:S(2)}) collective-permute-start(bf16[128,128]{1,0:T(8,128)(2,1)S(1)} %get-tuple-element.23.e0_ref), channel_id=1, source_target_pairs={{0,2},{2,0},{4,6},{6,4},{1,3},{3,1},{5,7},{7,5},{8,10},{10,8},{12,... | collective-permute-start | bytes 98312 | tf_op jit(solution)/shard_map/ppermute | solution.py:250
  51.4 15.6 %all-to-all-start.2 = ((f32[32,16,128]{2,1,0:T(8,128)}), f32[32,16,128]{2,1,0:T(8,128)S(1)}, u32[]{:S(2)}, u32[]{:S(2)}) async-start(f32[32,16,128]{2,1,0:T(8,128)} %get-tuple-element.24), calls=%async_computation.2 | async-start | bytes 524288 | tf_op jit(solution)/shard_map/all_to_all | solution.py:254
  55.3 3.7 %collective-permute-start.4 = (f32[128,128]{1,0:T(8,128)S(1)}, f32[128,128]{1,0:T(8,128)S(1)}, u32[]{:S(2)}, u32[]{:S(2)}) collective-permute-start(f32[128,128]{1,0:T(8,128)S(1)} %get-tuple-element.26), channel_id=1, source_target_pairs={{0,2},{2,0},{4,6},{6,4},{1,3},{3,1},{5,7},{7,5},{8,10},{10,8},{12,... | collective-permute-start | bytes 196616 | tf_op jit(solution)/shard_map/ppermute | solution.py:250
  55.7 5.0 %collective-permute-start.5 = (f32[128,128]{1,0:T(8,128)S(1)}, f32[128,128]{1,0:T(8,128)S(1)}, u32[]{:S(2)}, u32[]{:S(2)}) collective-permute-start(f32[128,128]{1,0:T(8,128)S(1)} %get-tuple-element.27), channel_id=1, source_target_pairs={{0,4},{2,6},{4,0},{6,2},{1,5},{3,7},{5,1},{7,3},{8,12},{10,14},{12... | collective-permute-start | bytes 196616 | tf_op jit(solution)/shard_map/ppermute | solution.py:250
  56.8 5.9 %collective-permute-start.6 = (f32[128,128]{1,0:T(8,128)S(1)}, f32[128,128]{1,0:T(8,128)S(1)}, u32[]{:S(2)}, u32[]{:S(2)}) collective-permute-start(f32[128,128]{1,0:T(8,128)S(1)} %get-tuple-element.28), channel_id=1, source_target_pairs={{0,6},{2,4},{4,2},{6,0},{1,7},{3,5},{5,3},{7,1},{8,14},{10,12},{12... | collective-permute-start | bytes 196616 | tf_op jit(solution)/shard_map/ppermute | solution.py:250
  67.0 4.1 %copy-start = (bf16[128,512]{1,0:T(8,128)(2,1)S(1)}, bf16[128,512]{1,0:T(8,128)(2,1)}, u32[]{:S(2)}) copy-start(bf16[128,512]{1,0:T(8,128)(2,1)} %x_ref.3) | copy-start | bytes 393220
  67.0 4.1 %copy-start.1 = (bf16[256,128]{1,0:T(8,128)(2,1)S(1)}, bf16[256,128]{1,0:T(8,128)(2,1)}, u32[]{:S(2)}) copy-start(bf16[256,128]{1,0:T(8,128)(2,1)} %w_out_ref.3) | copy-start | bytes 196612
  67.9 3.2 %collective-permute-start.7 = (f32[136,128]{1,0:T(8,128)S(1)}, f32[136,128]{1,0:T(8,128)S(1)}, u32[]{:S(2)}, u32[]{:S(2)}) collective-permute-start(f32[136,128]{1,0:T(8,128)S(1)} %shard_map.97.mine_ref), channel_id=1, source_target_pairs={{0,1},{1,0},{2,3},{3,2},{4,5},{5,4},{6,7},{7,6},{8,9},{9,8},{10,11... | collective-permute-start | bytes 208904 | tf_op jit(solution)/shard_map/ppermute | solution.py:250
  72.4 4.7 %collective-permute-start.8 = (f32[8,88,128]{2,1,0:T(8,128)S(1)}, f32[8,88,128]{2,1,0:T(8,128)S(1)}, u32[]{:S(2)}, u32[]{:S(2)}) collective-permute-start(f32[8,88,128]{2,1,0:T(8,128)S(1)} %get-tuple-element.34), channel_id=1, source_target_pairs={{0,2},{2,0},{1,3},{3,1},{4,6},{6,4},{5,7},{7,5},{8,10},{10,8},{9,1... | collective-permute-start | bytes 1081352 | tf_op jit(solution)/shard_map/ppermute | solution.py:250
  114.6 5.4 %collective-permute-start.9 = (f32[8,88,128]{2,1,0:T(8,128)S(1)}, f32[8,88,128]{2,1,0:T(8,128)S(1)}, u32[]{:S(2)}, u32[]{:S(2)}) collective-permute-start(f32[8,88,128]{2,1,0:T(8,128)S(1)} %all_to_all.33.mine_ref), channel_id=1, source_target_pairs={{0,2},{2,0},{1,3},{3,1},{4,6},{6,4},{5,7},{7,5},{8,10},{10,8},{9,1... | collective-permute-start | bytes 1081352 | tf_op jit(solution)/shard_map/ppermute | solution.py:250

commit v3 on v2

--- a/solution.py
+++ b/solution.py
@@ -1,5 +1,3 @@
-import functools
-
 import jax
 import jax.numpy as jnp
 from jax import lax
@@ -8,9 +6,10 @@
 from jax.sharding import Mesh
 from jax.sharding import PartitionSpec as P
 
-SIZES = {"z": 8, "x": 4, "yh": 2, "c": 2}
-DP = ("z", "x", "yh", "c")
-FAR = ("z", "x")
+SIZES = {"zh": 4, "zl": 2, "x": 4, "yh": 2, "c": 2}
+DP = ("zh", "zl", "x", "yh", "c")
+NEAR = ("zl", "x", "yh")
+FAR = ("zh", "zl", "x")
 QUAD = ("yh", "c")
 
 ROWS = 128
@@ -21,8 +20,8 @@
 N_QUAD = 4
 ANCHORS = N_FAR * HALF
 MSG = 24
-PART = 88
-N_NEAR = 8
+PART = 48
+N_NEAR = 16
 
 INV_TEMP = 10.0
 SHIFT = 10.0
@@ -32,23 +31,28 @@
 I32 = jnp.int32
 
 
-def call(kernel, outs, *args, smem=(), scratch=(), first=False, last=False):
+def call(kernel, outs, *args, smem=(), scratch=(), first=False, last=(), alias={}):
     specs = [
-        pl.BlockSpec(memory_space=pltpu.SMEM if i in smem else pltpu.VMEM)
+        pl.BlockSpec(memory_space=pltpu.SMEM if i in smem else pl.ANY if i in alias else pltpu.VMEM)
         for i in range(len(args))
     ]
     if not first:
         args = [
-            a if i in smem else pltpu.with_memory_space_constraint(a, pltpu.VMEM)
+            a if i in smem or i in alias else pltpu.with_memory_space_constraint(a, pltpu.VMEM)
             for i, a in enumerate(args)
         ]
-    kind = jax.ShapeDtypeStruct if last else pltpu.VMEM
+    shapes = [
+        jax.ShapeDtypeStruct(s, d) if last else pltpu.VMEM(s, d) for i, (s, d) in enumerate(outs)
+    ]
     return pl.pallas_call(
         kernel,
-        out_shape=[kind(s, d) for s, d in outs],
+        out_shape=shapes,
         in_specs=specs,
-        out_specs=[pl.BlockSpec(memory_space=pltpu.VMEM)] * len(outs),
+        out_specs=[
+            pl.BlockSpec(memory_space=pl.ANY if i in last else pltpu.VMEM) for i in range(len(outs))
+        ],
         scratch_shapes=list(scratch),
+        input_output_aliases=alias,
     )(*args)
 
 
@@ -194,7 +198,6 @@
     loss_ref,
     keep_ref,
     send_ref,
-    all_ref,
 ):
     scale = INV_TEMP / (N_FAR * N_QUAD * A_DEV)
     grad_emb = (mine_ref[0:ROWS, :] + theirs_ref[0:ROWS, :]) * scale
@@ -204,22 +207,30 @@
     unit = proj / norm
     inner = jnp.sum(unit * grad_emb, axis=1, keepdims=True)
     grad_proj = ((grad_emb - unit * inner) / norm).astype(BF16)
-    all_ref[1024:1280, :] = dot(hid_ref[...], grad_proj, ((0,), (0,)))
+    grad_out = dot(hid_ref[...], grad_proj, ((0,), (0,)))
     grad_hidden = dot(grad_proj, w_out_ref[...], ((1,), (1,)))
     pre = pre_ref[...]
     sig = jax.nn.sigmoid(pre)
     grad_pre = (grad_hidden * sig * (1.0 + pre * (1.0 - sig))).astype(BF16)
     grad_in = dot(x_ref[...], grad_pre, ((0,), (0,)))
-    all_ref[0:512, :] = grad_in[:, :128]
-    all_ref[512:1024, :] = grad_in[:, 128:]
     bias = jnp.sum(grad_pre.astype(F32), axis=0, keepdims=True)
-    bias = jnp.concatenate([bias[:, :128], bias[:, 128:], jnp.zeros((6, 128), F32)], axis=0)
+    first = lax.broadcasted_iota(I32, (8, 128), 0) == 0
     c = at_ref[1] % 2
-    for side, out_ref in ((c, keep_ref), (1 - c, send_ref)):
-        base = pl.multiple_of(side * 640, 128)
+
+    def store(half, out_ref):
+        lanes = slice(half * 128, half * 128 + 128)
         for i in range(N_NEAR):
-            out_ref[i, 0:80, :] = all_ref[pl.ds(base + i * 80, 80), :]
-            out_ref[i, 80:, :] = bias if i == 0 else jnp.zeros((8, 128), F32)
+            out_ref[i, 0:32, :] = grad_in[i * 32 : i * 32 + 32, lanes]
+            out_ref[i, 32:40, :] = grad_out[half * 128 + i * 8 : half * 128 + i * 8 + 8]
+            line = jnp.where(first, bias[:, lanes], 0.0) if i == 0 else jnp.zeros((8, 128), F32)
+            out_ref[i, 40:, :] = line
+
+    for side in (0, 1):
+
+        @pl.when(c == side)
+        def _():
+            store(side, keep_ref)
+            store(1 - side, send_ref)
 
 
 def add(a_ref, b_ref, out_ref):
@@ -228,20 +239,41 @@
 
 def sum_spread(in_ref, out_ref):
     total = jnp.sum(in_ref[...], axis=0)
-    for i in range(N_NEAR):
+    for i in range(out_ref.shape[0]):
         out_ref[i] = total
 
 
-def unpack(at_ref, mine_ref, theirs_ref, w_in_ref, b_ref, w_out_ref, all_ref):
+def place(side, in_ref, w_in_ref, w_out_ref, sems):
+    lanes = pl.ds(pl.multiple_of(side * 128, 128), 128)
+    copies = [
+        pltpu.make_async_copy(in_ref.at[:, 0:32, :], w_in_ref.at[:, :, lanes], sems.at[0]),
+        pltpu.make_async_copy(in_ref.at[:, 32:40, :], w_out_ref.at[side], sems.at[1]),
+    ]
+    for copy in copies:
+        copy.start()
+    return copies
+
+
+def place_mine(at_ref, mine_ref, loss_in_ref, w_in_ref, w_out_ref, loss_ref, sems):
+    copies = place(at_ref[1] % 2, mine_ref, w_in_ref, w_out_ref, sems)
+    copies.append(pltpu.make_async_copy(loss_in_ref, loss_ref, sems.at[2]))
+    copies[-1].start()
+    for copy in copies:
+        copy.wait()
+
+
+def place_theirs(
+    at_ref, mine_ref, theirs_ref, _, __, w_in_ref, w_out_ref, b_ref, bias_ref, sems
+):
     c = at_ref[1] % 2
-    for side, in_ref in ((c, mine_ref), (1 - c, theirs_ref)):
-        base = pl.multiple_of(side * 640, 128)
-        for i in range(N_NEAR):
-            all_ref[pl.ds(base + i * 80, 80), :] = in_ref[i, 0:80, :]
-    w_in_ref[:, :128] = all_ref[0:512, :]
-    w_in_ref[:, 128:] = all_ref[512:1024, :]
-    w_out_ref[...] = all_ref[1024:1280, :]
-    b_ref[...] = mine_ref[0, 80:82, :]
+    copies = place(1 - c, theirs_ref, w_in_ref, w_out_ref, sems)
+    own, other = mine_ref[0, 40:41, :], theirs_ref[0, 40:41, :]
+    bias_ref[0:1, :] = jnp.where(c == 0, own, other)
+    bias_ref[1:2, :] = jnp.where(c == 0, other, own)
+    copies.append(pltpu.make_async_copy(bias_ref, b_ref, sems.at[2]))
+    copies[-1].start()
+    for copy in copies:
+        copy.wait()
 
 
 def swap(value, axes, flip):
@@ -320,25 +352,43 @@
         features,
         w_out,
         smem=(0,),
-        scratch=[pltpu.VMEM((1280, EMB), F32)],
     )
     got = swap(send, "c", 1)
     (both,) = call(add, [(half, F32)], keep, got)
-    (both,) = call(sum_spread, [(half, F32)], exchange(both, ("x", "yh")))
-    (both,) = call(sum_spread, [(half, F32)], exchange(both, "z"))
-    both = exchange(both, ("x", "yh"))
+    (both,) = call(sum_spread, [((4, PART, EMB), F32)], exchange(both, NEAR))
+    (both,) = call(sum_spread, [(half, F32)], exchange(both, "zh"))
+    both = exchange(both, NEAR)
     got = swap(both, "c", 1)
-    grad_in, grad_b, grad_out = call(
-        unpack,
-        [((512, 256), F32), ((2, 128), F32), ((256, EMB), F32)],
+    whole = [((N_NEAR, 32, 256), F32), ((2, N_NEAR, 8, EMB), F32)]
+    sems = [pltpu.SemaphoreType.DMA((3,))]
+    *grads, row_loss = call(
+        place_mine,
+        whole + [((1, A_DEV), F32)],
+        at,
+        both,
+        row_loss,
+        smem=(0,),
+        scratch=sems,
+        last=(0, 1, 2),
+    )
+    grad_in, grad_out, grad_b = call(
+        place_theirs,
+        whole + [((2, 128), F32)],
         at,
         both,
         got,
+        *grads,
         smem=(0,),
-        scratch=[pltpu.VMEM((1280, EMB), F32)],
-        last=True,
-    )
-    return (row_loss.reshape(-1), grad_in, grad_b.reshape(-1), grad_out)
+        scratch=[pltpu.VMEM((2, 128), F32)] + sems,
+        last=(0, 1, 2),
+        alias={3: 0, 4: 1},
+    )
+    return (
+        row_loss.reshape(-1),
+        grad_in.reshape(512, 256),
+        grad_b.reshape(-1),
+        grad_out.reshape(256, EMB),
+    )
 
 
 def solution(mesh):

time: 122 us -> 121 us (level)
  starting transfers between devices: 34.4 us -> 38.3 us
  waiting for transfers between devices: 18.3 us -> 15 us
  blocking collectives: 56.7 us -> 54 us
    ppermute x10, starting transfers between devices: 19.4 us -> 23.2 us  [swap(): return lax.ppermute(value, axes, [(i, i ^ flip) for i in range(count)])]
    all_to_all x2, waiting for transfers between devices: 4.56 us -> 1.21 us  [exchange(): return lax.all_to_all(value, axes, 0, 0, tiled=True)]
    all_to_all x4, blocking collectives: 56.7 us -> 54 us  [exchange(): return lax.all_to_all(value, axes, 0, 0, tiled=True)]
    pallas_call x10 -> x11, Pallas kernels: 10.3 us -> 11.5 us  [call(): pl.pallas_call(kernel, out_shape=shapes, in_specs=specs, out_specs=[pl.Bl...]
  transfers between devices with their start and end apart: 12 -> 12, of which waited for: 10 -> 8; matrix products, arithmetic and copies ran while one was open for 1% -> 1% of each run, Pallas kernels for 0% -> 1%
where the time goes in v3:
time: 121 us; the launch traced here: 120 us
  blocking collectives  54 us (45%)
  starting transfers between devices  38.3 us (32%)
  waiting for transfers between devices  15 us (12%)
  Pallas kernels  11.5 us (10%)
    all_to_all x4, blocking collectives, exchange(): return lax.all_to_all(value, axes, 0, 0, tiled=True)  54 us
    ppermute x10, starting transfers between devices, swap(): return lax.ppermute(value, axes, [(i, i ^ flip) for i in range(count)])  23.2 us
    all_to_all x2, starting transfers between devices, exchange(): return lax.all_to_all(value, axes, 0, 0, tiled=True)  15.1 us
    ppermute x10, waiting for transfers between devices, swap(): return lax.ppermute(value, axes, [(i, i ^ flip) for i in range(count)])  13.8 us
    pallas_call x11, Pallas kernels, call(): pl.pallas_call(kernel, out_shape=shapes, in_specs=specs, out_specs=[pl.Bl...  11.5 us
  transfers between devices with their start and end apart: 12, of which 8 were waited for; matrix products, arithmetic and copies ran while one was open for 1% of the time, Pallas kernels for 1%

profile of v3, /device:TPU:1, one launch (start us, length us, event | category | flops | bytes accessed | tf_op | source)
XLA Modules:
  0.0 120.2 jit_solution(6524296370249248763)
XLA Ops:
  0.6 1.3 %shard_map.93 = (f32[128,128]{1,0:T(8,128)S(1)}, f32[128,256]{1,0:T(8,128)S(1)}, bf16[128,256]{1,0:T(8,128)(2,1)S(1)}) custom-call(bf16[128,512]{1,0:T(8,128)(2,1)} %x_ref.3, bf16[512,256]{1,0:T(8,128)(2,1)} %w_in_ref.1, f32[1,256]{1,0:T(1,128)} %bitcast.12, bf16[256,128]{1,0:T(8,128)(2,1)} %w_out_ref.3), custom_call_target="tpu_custom_call" | custom-call | tf_op jit(solution)/shard_map/pallas_call | solution.py:47
  2.0 2.2 %collective-permute-start = (f32[128,128]{1,0:T(8,128)S(1)}, f32[128,128]{1,0:T(8,128)S(1)}, u32[]{:S(2)}, u32[]{:S(2)}) collective-permute-start(f32[128,128]{1,0:T(8,128)S(1)} %get-tuple-element.24.part_ref), channel_id=1, source_target_pairs={{0,1},{1,0},{2,3},{3,2},{4,5},{5,4},{6,7},{7,6},{8,9},{9,8},{10,11... | collective-permute-start | bytes 196616 | tf_op jit(solution)/shard_map/ppermute | solution.py:282
  5.8 1.5 %shard_map.94 = (bf16[128,128]{1,0:T(8,128)(2,1)S(1)}, bf16[32,24,128]{2,1,0:T(8,128)(2,1)}) custom-call(s32[3]{0:T(128)} %pad_add_fusion.at_ref, s32[128]{0:T(128)} %window_ref.3, f32[128,128]{1,0:T(8,128)S(1)} %get-tuple-element.24.part_ref, f32[128,128]{1,0:T(8,128)S(1)} %collective-permute-done.other_ref, s32[1,128]{1,0:T(1,128)S(1)} %bitcast.9), custom_call_target="tpu_custom_call" | custom-call | tf_op jit(solution)/shard_map/pallas_call | solution.py:47
  7.3 11.2 %all-to-all-start = ((bf16[32,24,128]{2,1,0:T(8,128)(2,1)}), bf16[32,24,128]{2,1,0:T(8,128)(2,1)S(1)}, u32[]{:S(2)}, u32[]{:S(2)}) async-start(bf16[32,24,128]{2,1,0:T(8,128)(2,1)} %get-tuple-element.25), calls=%async_computation | async-start | bytes 393216 | tf_op jit(solution)/shard_map/all_to_all | solution.py:286
  18.5 2.2 %collective-permute-start.1 = (bf16[128,128]{1,0:T(8,128)(2,1)S(1)}, bf16[128,128]{1,0:T(8,128)(2,1)S(1)}, u32[]{:S(2)}, u32[]{:S(2)}) collective-permute-start(bf16[128,128]{1,0:T(8,128)(2,1)S(1)} %get-tuple-element.26.e0_ref), channel_id=1, source_target_pairs={{0,2},{2,0},{4,6},{6,4},{1,3},{3,1},{5,7},{7,5},{8,10},{10,8},{12,... | collective-permute-start | bytes 98312 | tf_op jit(solution)/shard_map/ppermute | solution.py:282
  20.7 2.9 %collective-permute-start.2 = (bf16[128,128]{1,0:T(8,128)(2,1)S(1)}, bf16[128,128]{1,0:T(8,128)(2,1)S(1)}, u32[]{:S(2)}, u32[]{:S(2)}) collective-permute-start(bf16[128,128]{1,0:T(8,128)(2,1)S(1)} %get-tuple-element.26.e0_ref), channel_id=1, source_target_pairs={{0,4},{2,6},{4,0},{6,2},{1,5},{3,7},{5,1},{7,3},{8,12},{10,14},{12... | collective-permute-start | bytes 98312 | tf_op jit(solution)/shard_map/ppermute | solution.py:282
  24.0 1.3 %collective-permute-done.2.e2_ref = bf16[128,128]{1,0:T(8,128)(2,1)S(1)} collective-permute-done((bf16[128,128]{1,0:T(8,128)(2,1)S(1)}, bf16[128,128]{1,0:T(8,128)(2,1)S(1)}, u32[]{:S(2)}, u32[]{:S(2)}) %collective-permute-start.2) | collective-permute-done | bytes 32800 | tf_op jit(solution)/shard_map/ppermute | solution.py:282
  25.3 3.5 %collective-permute-done.3.e3_ref = bf16[128,128]{1,0:T(8,128)(2,1)S(1)} collective-permute-done((bf16[128,128]{1,0:T(8,128)(2,1)S(1)}, bf16[128,128]{1,0:T(8,128)(2,1)S(1)}, u32[]{:S(2)}, u32[]{:S(2)}) %collective-permute-start.3) | collective-permute-done | bytes 32800 | tf_op jit(solution)/shard_map/ppermute | solution.py:282
  30.0 18.4 %all_to_all.30.sums_ref = f32[32,8,128]{2,1,0:T(8,128)S(1)} all-to-all(f32[32,8,128]{2,1,0:T(8,128)S(1)} %shard_map.95), channel_id=1, replica_groups=mesh['zh'=4,'zl'=2,'x'=4,'yh'=2,'c'=2,'mp'=2] {'zh','zl','x'}, dimensions={0} | all-to-all | bytes 262144 | tf_op jit(solution)/shard_map/all_to_all | solution.py:286
  48.4 2.4 %shard_map.96 = (f32[32,16,128]{2,1,0:T(8,128)}, f32[128,128]{1,0:T(8,128)S(1)}, f32[128,128]{1,0:T(8,128)S(1)}, f32[128,128]{1,0:T(8,128)S(1)}, f32[128,128]{1,0:T(8,128)S(1)}, /*index=5*/f32[8,128]{1,0:T(8,128)S(1)}) custom-call(s32[3]{0:T(128)} %pad_add_fusion.at_ref, bf16[32,24,128]{2,1,0:T(8,128)(2,1)S(1)} %all-to-all-done.msg_ref, ...), custom_call_target="tpu_custom_call" | custom-call | tf_op jit(solution)/shard_map/pallas_call | solution.py:47
  50.8 3.9 %all-to-all-start.2 = ((f32[32,16,128]{2,1,0:T(8,128)}), f32[32,16,128]{2,1,0:T(8,128)S(1)}, u32[]{:S(2)}, u32[]{:S(2)}) async-start(f32[32,16,128]{2,1,0:T(8,128)} %get-tuple-element.27), calls=%async_computation.2 | async-start | bytes 524288 | tf_op jit(solution)/shard_map/all_to_all | solution.py:286
  54.7 2.2 %collective-permute-start.4 = (f32[128,128]{1,0:T(8,128)S(1)}, f32[128,128]{1,0:T(8,128)S(1)}, u32[]{:S(2)}, u32[]{:S(2)}) collective-permute-start(f32[128,128]{1,0:T(8,128)S(1)} %get-tuple-element.29), channel_id=1, source_target_pairs={{0,2},{2,0},{4,6},{6,4},{1,3},{3,1},{5,7},{7,5},{8,10},{10,8},{12,... | collective-permute-start | bytes 196616 | tf_op jit(solution)/shard_map/ppermute | solution.py:282
  57.3 2.8 %collective-permute-start.6 = (f32[128,128]{1,0:T(8,128)S(1)}, f32[128,128]{1,0:T(8,128)S(1)}, u32[]{:S(2)}, u32[]{:S(2)}) collective-permute-start(f32[128,128]{1,0:T(8,128)S(1)} %get-tuple-element.31), channel_id=1, source_target_pairs={{0,6},{2,4},{4,2},{6,0},{1,7},{3,5},{5,3},{7,1},{8,14},{10,12},{12... | collective-permute-start | bytes 196616 | tf_op jit(solution)/shard_map/ppermute | solution.py:282
  60.1 1.8 %collective-permute-done.5.r2_ref = f32[128,128]{1,0:T(8,128)S(1)} collective-permute-done((f32[128,128]{1,0:T(8,128)S(1)}, f32[128,128]{1,0:T(8,128)S(1)}, u32[]{:S(2)}, u32[]{:S(2)}) %collective-permute-start.5) | collective-permute-done | bytes 65568 | tf_op jit(solution)/shard_map/ppermute | solution.py:282
  61.9 2.0 %collective-permute-done.6.r3_ref = f32[128,128]{1,0:T(8,128)S(1)} collective-permute-done((f32[128,128]{1,0:T(8,128)S(1)}, f32[128,128]{1,0:T(8,128)S(1)}, u32[]{:S(2)}, u32[]{:S(2)}) %collective-permute-start.6) | collective-permute-done | bytes 65568 | tf_op jit(solution)/shard_map/ppermute | solution.py:282
  66.4 2.8 %collective-permute-done.7.theirs_ref = f32[136,128]{1,0:T(8,128)S(1)} collective-permute-done((f32[136,128]{1,0:T(8,128)S(1)}, f32[136,128]{1,0:T(8,128)S(1)}, u32[]{:S(2)}, u32[]{:S(2)}) %collective-permute-start.7) | collective-permute-done | bytes 69664 | tf_op jit(solution)/shard_map/ppermute | solution.py:282
  70.4 5.0 %collective-permute-start.8 = (f32[16,48,128]{2,1,0:T(8,128)S(1)}, f32[16,48,128]{2,1,0:T(8,128)S(1)}, u32[]{:S(2)}, u32[]{:S(2)}) collective-permute-start(f32[16,48,128]{2,1,0:T(8,128)S(1)} %get-tuple-element.36), channel_id=1, source_target_pairs={{0,2},{2,0},{1,3},{3,1},{4,6},{6,4},{5,7},{7,5},{8,10},{10,8},{9,1... | collective-permute-start | bytes 1179656 | tf_op jit(solution)/shard_map/ppermute | solution.py:282
  75.4 1.3 %collective-permute-done.8.b_ref = f32[16,48,128]{2,1,0:T(8,128)S(1)} collective-permute-done((f32[16,48,128]{2,1,0:T(8,128)S(1)}, f32[16,48,128]{2,1,0:T(8,128)S(1)}, u32[]{:S(2)}, u32[]{:S(2)}) %collective-permute-start.8) | collective-permute-done | bytes 393248 | tf_op jit(solution)/shard_map/ppermute | solution.py:282
  76.8 11.7 %all_to_all.31.in_ref = f32[16,48,128]{2,1,0:T(8,128)S(1)} all-to-all(f32[16,48,128]{2,1,0:T(8,128)S(1)} %shard_map.99), channel_id=1, replica_groups=mesh['zh'=4,'zl'=2,'x'=4,'yh'=2,'c'=2,'mp'=2] {'zl','x','yh'}, dimensions={0} | all-to-all | bytes 786432 | tf_op jit(solution)/shard_map/all_to_all | solution.py:286
  88.6 11.4 %all_to_all.32.in_ref = f32[4,48,128]{2,1,0:T(8,128)S(1)} all-to-all(f32[4,48,128]{2,1,0:T(8,128)S(1)} %shard_map.100), channel_id=1, replica_groups=mesh['zh'=4,'zl'=2,'x'=4,'yh'=2,'c'=2,'mp'=2] {'zh'}, dimensions={0} | all-to-all | bytes 196608 | tf_op jit(solution)/shard_map/all_to_all | solution.py:286
  100.0 12.6 %all_to_all.33.mine_ref = f32[16,48,128]{2,1,0:T(8,128)S(1)} all-to-all(f32[16,48,128]{2,1,0:T(8,128)S(1)} %shard_map.101), channel_id=1, replica_groups=mesh['zh'=4,'zl'=2,'x'=4,'yh'=2,'c'=2,'mp'=2] {'zl','x','yh'}, dimensions={0} | all-to-all | bytes 786432 | tf_op jit(solution)/shard_map/all_to_all | solution.py:286
  112.6 4.8 %collective-permute-start.9 = (f32[16,48,128]{2,1,0:T(8,128)S(1)}, f32[16,48,128]{2,1,0:T(8,128)S(1)}, u32[]{:S(2)}, u32[]{:S(2)}) collective-permute-start(f32[16,48,128]{2,1,0:T(8,128)S(1)} %all_to_all.33.mine_ref), channel_id=1, source_target_pairs={{0,2},{2,0},{1,3},{3,1},{4,6},{6,4},{5,7},{7,5},{8,10},{10,8},{9,1... | collective-permute-start | bytes 1179656 | tf_op jit(solution)/shard_map/ppermute | solution.py:282
  117.3 1.4 %shard_map.102 = (f32[16,32,256]{2,1,0:T(8,128)}, f32[2,16,8,128]{3,2,1,0:T(8,128)}, f32[1,32]{1,0:T(1,128)}) custom-call(s32[3]{0:T(128)} %pad_add_fusion.at_ref, f32[16,48,128]{2,1,0:T(8,128)S(1)} %all_to_all.33.mine_ref, f32[1,32]{1,0:T(1,128)S(1)} %get-tuple-element.37.loss_in_ref), custom_call_target="tpu_custom_call" | custom-call | tf_op jit(solution)/shard_map/pallas_call | solution.py:47
  118.8 1.4 %shard_map.103 = (f32[16,32,256]{2,1,0:T(8,128)}, f32[2,16,8,128]{3,2,1,0:T(8,128)}, f32[2,128]{1,0:T(2,128)}) custom-call(s32[3]{0:T(128)} %pad_add_fusion.at_ref, f32[16,48,128]{2,1,0:T(8,128)S(1)} %all_to_all.33.mine_ref, f32[16,48,128]{2,1,0:T(8,128)S(1)} %collective-permute-done.9.theirs_ref, ...), custom_call_target="tpu_custom_call", output_to_operand_aliasing={{0}: (3, {}), {1}: (4, {})} | custom-call | tf_op jit(solution)/shard_map/pallas_call | solution.py:47
  (22 shorter events, 7.6 us)
Async XLA Ops:
  2.0 3.9 %collective-permute-start = (f32[128,128]{1,0:T(8,128)S(1)}, f32[128,128]{1,0:T(8,128)S(1)}, u32[]{:S(2)}, u32[]{:S(2)}) collective-permute-start(f32[128,128]{1,0:T(8,128)S(1)} %get-tuple-element.24.part_ref), channel_id=1, source_target_pairs={{0,1},{1,0},{2,3},{3,2},{4,5},{5,4},{6,7},{7,6},{8,9},{9,8},{10,11... | collective-permute-start | bytes 196616 | tf_op jit(solution)/shard_map/ppermute | solution.py:282
  4.8 1.0 copy-start.2
  7.3 21.5 %all-to-all-start = ((bf16[32,24,128]{2,1,0:T(8,128)(2,1)}), bf16[32,24,128]{2,1,0:T(8,128)(2,1)S(1)}, u32[]{:S(2)}, u32[]{:S(2)}) async-start(bf16[32,24,128]{2,1,0:T(8,128)(2,1)} %get-tuple-element.25), calls=%async_computation | async-start | bytes 393216 | tf_op jit(solution)/shard_map/all_to_all | solution.py:286
  18.5 5.4 %collective-permute-start.1 = (bf16[128,128]{1,0:T(8,128)(2,1)S(1)}, bf16[128,128]{1,0:T(8,128)(2,1)S(1)}, u32[]{:S(2)}, u32[]{:S(2)}) collective-permute-start(bf16[128,128]{1,0:T(8,128)(2,1)S(1)} %get-tuple-element.26.e0_ref), channel_id=1, source_target_pairs={{0,2},{2,0},{4,6},{6,4},{1,3},{3,1},{5,7},{7,5},{8,10},{10,8},{12,... | collective-permute-start | bytes 98312 | tf_op jit(solution)/shard_map/ppermute | solution.py:282
  20.7 4.6 %collective-permute-start.2 = (bf16[128,128]{1,0:T(8,128)(2,1)S(1)}, bf16[128,128]{1,0:T(8,128)(2,1)S(1)}, u32[]{:S(2)}, u32[]{:S(2)}) collective-permute-start(bf16[128,128]{1,0:T(8,128)(2,1)S(1)} %get-tuple-element.26.e0_ref), channel_id=1, source_target_pairs={{0,4},{2,6},{4,0},{6,2},{1,5},{3,7},{5,1},{7,3},{8,12},{10,14},{12... | collective-permute-start | bytes 98312 | tf_op jit(solution)/shard_map/ppermute | solution.py:282
  23.6 5.2 %collective-permute-start.3 = (bf16[128,128]{1,0:T(8,128)(2,1)S(1)}, bf16[128,128]{1,0:T(8,128)(2,1)S(1)}, u32[]{:S(2)}, u32[]{:S(2)}) collective-permute-start(bf16[128,128]{1,0:T(8,128)(2,1)S(1)} %get-tuple-element.26.e0_ref), channel_id=1, source_target_pairs={{0,6},{2,4},{4,2},{6,0},{1,7},{3,5},{5,3},{7,1},{8,14},{10,12},{12... | collective-permute-start | bytes 98312 | tf_op jit(solution)/shard_map/ppermute | solution.py:282
  50.8 14.3 %all-to-all-start.2 = ((f32[32,16,128]{2,1,0:T(8,128)}), f32[32,16,128]{2,1,0:T(8,128)S(1)}, u32[]{:S(2)}, u32[]{:S(2)}) async-start(f32[32,16,128]{2,1,0:T(8,128)} %get-tuple-element.27), calls=%async_computation.2 | async-start | bytes 524288 | tf_op jit(solution)/shard_map/all_to_all | solution.py:286
  54.7 5.4 %collective-permute-start.4 = (f32[128,128]{1,0:T(8,128)S(1)}, f32[128,128]{1,0:T(8,128)S(1)}, u32[]{:S(2)}, u32[]{:S(2)}) collective-permute-start(f32[128,128]{1,0:T(8,128)S(1)} %get-tuple-element.29), channel_id=1, source_target_pairs={{0,2},{2,0},{4,6},{6,4},{1,3},{3,1},{5,7},{7,5},{8,10},{10,8},{12,... | collective-permute-start | bytes 196616 | tf_op jit(solution)/shard_map/ppermute | solution.py:282
  56.8 5.1 %collective-permute-start.5 = (f32[128,128]{1,0:T(8,128)S(1)}, f32[128,128]{1,0:T(8,128)S(1)}, u32[]{:S(2)}, u32[]{:S(2)}) collective-permute-start(f32[128,128]{1,0:T(8,128)S(1)} %get-tuple-element.30), channel_id=1, source_target_pairs={{0,4},{2,6},{4,0},{6,2},{1,5},{3,7},{5,1},{7,3},{8,12},{10,14},{12... | collective-permute-start | bytes 196616 | tf_op jit(solution)/shard_map/ppermute | solution.py:282
  57.3 6.6 %collective-permute-start.6 = (f32[128,128]{1,0:T(8,128)S(1)}, f32[128,128]{1,0:T(8,128)S(1)}, u32[]{:S(2)}, u32[]{:S(2)}) collective-permute-start(f32[128,128]{1,0:T(8,128)S(1)} %get-tuple-element.31), channel_id=1, source_target_pairs={{0,6},{2,4},{4,2},{6,0},{1,7},{3,5},{5,3},{7,1},{8,14},{10,12},{12... | collective-permute-start | bytes 196616 | tf_op jit(solution)/shard_map/ppermute | solution.py:282
  65.1 4.1 %copy-start = (bf16[128,512]{1,0:T(8,128)(2,1)S(1)}, bf16[128,512]{1,0:T(8,128)(2,1)}, u32[]{:S(2)}) copy-start(bf16[128,512]{1,0:T(8,128)(2,1)} %x_ref.3) | copy-start | bytes 393220
  65.1 4.1 %copy-start.1 = (bf16[256,128]{1,0:T(8,128)(2,1)S(1)}, bf16[256,128]{1,0:T(8,128)(2,1)}, u32[]{:S(2)}) copy-start(bf16[256,128]{1,0:T(8,128)(2,1)} %w_out_ref.3) | copy-start | bytes 196612
  66.0 3.2 %collective-permute-start.7 = (f32[136,128]{1,0:T(8,128)S(1)}, f32[136,128]{1,0:T(8,128)S(1)}, u32[]{:S(2)}, u32[]{:S(2)}) collective-permute-start(f32[136,128]{1,0:T(8,128)S(1)} %shard_map.97.mine_ref), channel_id=1, source_target_pairs={{0,1},{1,0},{2,3},{3,2},{4,5},{5,4},{6,7},{7,6},{8,9},{9,8},{10,11... | collective-permute-start | bytes 208904 | tf_op jit(solution)/shard_map/ppermute | solution.py:282
  70.4 6.3 %collective-permute-start.8 = (f32[16,48,128]{2,1,0:T(8,128)S(1)}, f32[16,48,128]{2,1,0:T(8,128)S(1)}, u32[]{:S(2)}, u32[]{:S(2)}) collective-permute-start(f32[16,48,128]{2,1,0:T(8,128)S(1)} %get-tuple-element.36), channel_id=1, source_target_pairs={{0,2},{2,0},{1,3},{3,1},{4,6},{6,4},{5,7},{7,5},{8,10},{10,8},{9,1... | collective-permute-start | bytes 1179656 | tf_op jit(solution)/shard_map/ppermute | solution.py:282
  112.6 6.2 %collective-permute-start.9 = (f32[16,48,128]{2,1,0:T(8,128)S(1)}, f32[16,48,128]{2,1,0:T(8,128)S(1)}, u32[]{:S(2)}, u32[]{:S(2)}) collective-permute-start(f32[16,48,128]{2,1,0:T(8,128)S(1)} %all_to_all.33.mine_ref), channel_id=1, source_target_pairs={{0,2},{2,0},{1,3},{3,1},{4,6},{6,4},{5,7},{7,5},{8,10},{10,8},{9,1... | collective-permute-start | bytes 1179656 | tf_op jit(solution)/shard_map/ppermute | solution.py:282

commit v4 on v3

--- a/solution.py
+++ b/solution.py
@@ -115,74 +115,94 @@
     return jnp.concatenate([msg_ref[i, :HALF, :] for i in range(N_FAR)], axis=0)
 
 
-def totals(at_ref, msg_ref, e0_ref, e1_ref, e2_ref, e3_ref, out_ref):
+def middle_of(anchors):
+    return jnp.sum(anchors.astype(F32), axis=0, keepdims=True) * (1.0 / ANCHORS)
+
+
+def block_sums(at_ref, msg_ref, e0_ref, e1_ref, e2_ref, e3_ref, out_ref):
     anchors = anchors_of(msg_ref)
     partner, own = block_ids(at_ref, msg_ref)
     total = jnp.zeros((1, ANCHORS), F32)
-    hit = jnp.zeros((1, ANCHORS), F32)
+    rows = jnp.zeros((ANCHORS, 2 * EMB), F32)
+    pairs = jnp.zeros((ANCHORS, EMB), F32)
+    ones = jnp.ones((ROWS, EMB), BF16)
+    for r, e_ref in enumerate((e0_ref, e1_ref, e2_ref, e3_ref)):
+        cols_emb = e_ref[...]
+        s = dot(cols_emb, anchors, ((1,), (1,))) * INV_TEMP
+        cols = column_ids(at_ref, r)
+        positive = cols == partner
+        ex = jnp.where(cols == own, 0.0, jnp.exp(s - SHIFT))
+        total = total + jnp.sum(ex, axis=0, keepdims=True)
+        others = jnp.where(positive, 0.0, ex).astype(BF16)
+        rows = rows + dot(others, jnp.concatenate([cols_emb, ones], axis=1), ((0,), (0,)))
+        pairs = pairs + dot(positive.astype(F32).astype(BF16), cols_emb, ((0,), (0,)))
+    rows = (rows[:, :EMB] - rows[:, EMB:] * middle_of(anchors)).astype(BF16)
+    pairs = pairs.astype(BF16)
+    lines = jnp.concatenate([total[:, i * ROWS : (i + 1) * ROWS] for i in range(4)], axis=0)
+    high = lines.astype(BF16).astype(F32)
+    lines = jnp.concatenate([high, lines - high], axis=0).astype(BF16)
+    for i in range(N_FAR):
+        here = slice(i * HALF, (i + 1) * HALF)
+        out_ref[i, 0:16, :] = rows[here]
+        out_ref[i, 16:32, :] = pairs[here]
+        out_ref[i, 32:40, :] = lines
+
+
+def totals_of(sums_ref):
+    lines = jnp.sum(sums_ref[:, 32:40, :].astype(F32), axis=0)
+    return lines[0:4] + lines[4:8]
+
+
+def weights(
+    at_ref, msg_ref, sums_ref, e0_ref, e1_ref, e2_ref, e3_ref, keep_ref, send_ref
+):
+    anchors = anchors_of(msg_ref)
+    partner, own = block_ids(at_ref, msg_ref)
+    total = totals_of(sums_ref)
+    total = jnp.concatenate([total[i : i + 1] for i in range(4)], axis=1)
     for r, e_ref in enumerate((e0_ref, e1_ref, e2_ref, e3_ref)):
         s = dot(e_ref[...], anchors, ((1,), (1,))) * INV_TEMP
         cols = column_ids(at_ref, r)
-        ex = jnp.where(cols == own, 0.0, jnp.exp(s - SHIFT))
-        total = total + jnp.sum(ex, axis=0, keepdims=True)
-        hit = hit + jnp.sum(jnp.where(cols == partner, s, 0.0), axis=0, keepdims=True)
-    lines = [total[:, i * ROWS : (i + 1) * ROWS] for i in range(4)]
-    lines += [hit[:, i * ROWS : (i + 1) * ROWS] for i in range(4)]
-    message = jnp.concatenate(lines, axis=0)
-    for i in range(N_FAR):
-        out_ref[i] = message
-
-
-def weights(
-    at_ref,
-    msg_ref,
-    sums_ref,
-    e0_ref,
-    e1_ref,
-    e2_ref,
-    e3_ref,
-    row_ref,
-    c0_ref,
-    c1_ref,
-    c2_ref,
-    c3_ref,
-    loss_ref,
-):
-    anchors = anchors_of(msg_ref)
-    partner, own = block_ids(at_ref, msg_ref)
-    sums = jnp.sum(sums_ref[...], axis=0)
-    total, hit = sums[:4], sums[4:]
-    loss_ref[...] = jnp.concatenate([jnp.log(total) + SHIFT - hit, hit], axis=0)
-    total = jnp.concatenate([total[i : i + 1] for i in range(4)], axis=1)
-    rows = jnp.zeros((ANCHORS, EMB), F32)
-    for r, (e_ref, c_ref) in enumerate(
-        ((e0_ref, c0_ref), (e1_ref, c1_ref), (e2_ref, c2_ref), (e3_ref, c3_ref))
-    ):
-        cols_emb = e_ref[...]
-        s = dot(cols_emb, anchors, ((1,), (1,))) * INV_TEMP
-        cols = column_ids(at_ref, r)
         prob = jnp.where(cols == own, 0.0, jnp.exp(s - SHIFT) / total)
         w = (prob - (cols == partner).astype(F32)).astype(BF16)
-        c_ref[...] = dot(w, anchors, ((1,), (0,)))
-        rows = rows + dot(w, cols_emb, ((0,), (0,)))
-    for i in range(N_FAR):
-        row_ref[i] = rows[i * HALF : (i + 1) * HALF]
-
-
-def gather_rows(
-    at_ref, window_ref, rows_ref, c0_ref, r1_ref, r2_ref, r3_ref, loss_ref, out_ref
-):
+        c_ref = send_ref if r % 2 else keep_ref
+        c_ref[r // 2] = dot(w, anchors, ((1,), (0,)))
+
+
+def own_rows(at_ref, msg_ref, sums_ref, out_ref):
+    g, mp = at_ref[0], at_ref[2]
+    line = lax.broadcasted_iota(I32, (4, ROWS), 0)
+    total = jnp.sum(jnp.where(line == g // 8, totals_of(sums_ref), 0.0), axis=0, keepdims=True)
+    total = jnp.broadcast_to(total, (HALF, ROWS))
+    to = mp * HALF
+    total = pltpu.roll(total, (to - (g % 8) * HALF + ROWS) % ROWS, axis=1)
+    lane = lax.broadcasted_iota(I32, (HALF, ROWS), 1)
+    here = lane == to + lax.broadcasted_iota(I32, (HALF, ROWS), 0)
+    pair = jnp.sum(sums_ref[:, 16:32, :].astype(F32), axis=0)
+    emb = msg_ref[g, 0:HALF, :].astype(F32)
+    hit_of = jnp.sum(emb * pair, axis=1, keepdims=True) * INV_TEMP
+    hit = jnp.sum(jnp.where(here, hit_of, 0.0), axis=0, keepdims=True)
+    loss = jnp.where((lane >= to) & (lane < to + HALF), jnp.log(total) + SHIFT - hit, 0.0)
+    out_ref[HALF:, :] = loss[0:8]
+    total_of = jnp.sum(jnp.where(here, total, 0.0), axis=1, keepdims=True)
+    ex_pair = jnp.exp(hit_of - SHIFT)
+    weight = (ex_pair / total_of - 1.0).astype(BF16).astype(F32)
+    rows = jnp.sum(sums_ref[:, 0:16, :].astype(F32), axis=0)
+    rows = rows + (total_of - ex_pair) * middle_of(anchors_of(msg_ref))
+    out_ref[0:HALF, :] = rows / total_of + weight * pair
+
+
+def add_pair(a_ref, b_ref, mine_ref, next_ref):
+    mine_ref[...] = a_ref[0] + b_ref[0]
+    next_ref[...] = a_ref[1] + b_ref[1]
+
+
+def gather_rows(at_ref, window_ref, rows_ref, c0_ref, c2_ref, out_ref):
     g, q, mp = at_ref[0], at_ref[1], at_ref[2]
-    out_ref[0:ROWS, :] = (c0_ref[...] + r1_ref[...]) + (r2_ref[...] + r3_ref[...])
+    out_ref[0:ROWS, :] = c0_ref[...] + c2_ref[...]
     start = pl.multiple_of(window_ref[g * N_QUAD + q] * A_DEV + mp * HALF, HALF)
-    mine = jnp.sum(rows_ref[...], axis=0)
-    out_ref[pl.ds(start, HALF), :] = out_ref[pl.ds(start, HALF), :] + mine
-    row = lax.broadcasted_iota(I32, (8, ROWS), 0)
-    line = jnp.sum(jnp.where(row == g // 8, loss_ref[...], 0.0), axis=0, keepdims=True)
-    line = jnp.broadcast_to(line, (8, ROWS))
-    line = pltpu.roll(line, (mp * HALF - (g % 8) * HALF + ROWS) % ROWS, axis=1)
-    lane = lax.broadcasted_iota(I32, (8, ROWS), 1)
-    out_ref[ROWS:, :] = jnp.where((lane >= mp * HALF) & (lane < mp * HALF + HALF), line, 0.0)
+    out_ref[pl.ds(start, HALF), :] = out_ref[pl.ds(start, HALF), :] + rows_ref[0:HALF, :]
+    out_ref[ROWS:, :] = rows_ref[HALF:, :]
 
 
 def backward(
@@ -311,31 +331,18 @@
     )
     anchors = exchange(message, FAR)
     blocks = [emb] + [swap(emb, QUAD, r) for r in (1, 2, 3)]
-    (sums,) = call(totals, [((N_FAR, 8, ROWS), F32)], at, anchors, *blocks, smem=(0,))
+    (sums,) = call(block_sums, [((N_FAR, 40, EMB), BF16)], at, anchors, *blocks, smem=(0,))
     sums = exchange(sums, FAR)
-    rows, c0, c1, c2, c3, losses = call(
-        weights,
-        [((N_FAR, HALF, EMB), F32)] + [((ROWS, EMB), F32)] * 4 + [((8, ROWS), F32)],
-        at,
-        anchors,
-        sums,
-        *blocks,
-        smem=(0,),
-    )
-    rows = exchange(rows, FAR)
-    r1, r2, r3 = [swap(c, QUAD, r) for r, c in ((1, c1), (2, c2), (3, c3))]
+    pair = (2, ROWS, EMB)
+    keep, send = call(
+        weights, [(pair, F32), (pair, F32)], at, anchors, sums, *blocks, smem=(0,)
+    )
+    got = swap(send, "c", 1)
+    (rows,) = call(own_rows, [((HALF + 8, EMB), F32)], at, anchors, sums, smem=(0,))
+    c0, c2 = call(add_pair, [((ROWS, EMB), F32)] * 2, keep, got)
+    c2 = swap(c2, "yh", 1)
     (mine,) = call(
-        gather_rows,
-        [((ROWS + 8, EMB), F32)],
-        at,
-        window,
-        rows,
-        c0,
-        r1,
-        r2,
-        r3,
-        losses,
-        smem=(0, 1),
+        gather_rows, [((ROWS + 8, EMB), F32)], at, window, rows, c0, c2, smem=(0, 1)
     )
     theirs = swap(mine, "mp", 1)
     half = (N_NEAR, PART, EMB)

time: 121 us -> 114 us (0.942)
  starting transfers between devices: 38.3 us -> 29.7 us
  blocking collectives: 54 us -> 56 us
    ppermute x10 -> x9, starting transfers between devices: 23.2 us -> 18.5 us  [swap(): return lax.ppermute(value, axes, [(i, i ^ flip) for i in range(count)])]
    all_to_all x2 -> x1, starting transfers between devices: 15.1 us -> 11.2 us  [exchange(): return lax.all_to_all(value, axes, 0, 0, tiled=True)]
    all_to_all x4, blocking collectives: 54 us -> 56 us  [exchange(): return lax.all_to_all(value, axes, 0, 0, tiled=True)]
    pallas_call x11 -> x13, Pallas kernels: 11.5 us -> 12.1 us  [call(): pl.pallas_call(kernel, out_shape=shapes, in_specs=specs, out_specs=[pl.Bl...]
    ppermute x10 -> x9, waiting for transfers between devices: 13.8 us -> 14.4 us  [swap(): return lax.ppermute(value, axes, [(i, i ^ flip) for i in range(count)])]
  transfers between devices with their start and end apart: 12 -> 10, of which waited for: 8 -> 7; matrix products, arithmetic and copies ran while one was open for 1% -> 1% of each run, Pallas kernels for 1% -> 2%
where the time goes in v4:
time: 114 us
  blocking collectives  56 us (49%)
  starting transfers between devices  29.7 us (26%)
  waiting for transfers between devices  14.4 us (13%)
  Pallas kernels  12.1 us (11%)
    all_to_all x4, blocking collectives, exchange(): return lax.all_to_all(value, axes, 0, 0, tiled=True)  56 us
    ppermute x9, starting transfers between devices, swap(): return lax.ppermute(value, axes, [(i, i ^ flip) for i in range(count)])  18.5 us
    ppermute x9, waiting for transfers between devices, swap(): return lax.ppermute(value, axes, [(i, i ^ flip) for i in range(count)])  14.4 us
    pallas_call x13, Pallas kernels, call(): pl.pallas_call(kernel, out_shape=shapes, in_specs=specs, out_specs=[pl.Bl...  12.1 us
    all_to_all x1, starting transfers between devices, exchange(): return lax.all_to_all(value, axes, 0, 0, tiled=True)  11.2 us
  transfers between devices with their start and end apart: 10, of which 7 were waited for; matrix products, arithmetic and copies ran while one was open for 1% of the time, Pallas kernels for 2%

profile of v4, /device:TPU:1, one launch (start us, length us, event | category | flops | bytes accessed | tf_op | source)
XLA Modules:
  0.0 113.5 jit_solution(16150562174055874904)
XLA Ops:
  0.6 1.3 %shard_map.93 = (f32[128,128]{1,0:T(8,128)S(1)}, f32[128,256]{1,0:T(8,128)S(1)}, bf16[128,256]{1,0:T(8,128)(2,1)S(1)}) custom-call(bf16[128,512]{1,0:T(8,128)(2,1)} %x_ref.3, bf16[512,256]{1,0:T(8,128)(2,1)} %w_in_ref.1, f32[1,256]{1,0:T(1,128)} %bitcast.12, bf16[256,128]{1,0:T(8,128)(2,1)} %w_out_ref.3), custom_call_target="tpu_custom_call" | custom-call | tf_op jit(solution)/shard_map/pallas_call | solution.py:47
  2.0 2.2 %collective-permute-start = (f32[128,128]{1,0:T(8,128)S(1)}, f32[128,128]{1,0:T(8,128)S(1)}, u32[]{:S(2)}, u32[]{:S(2)}) collective-permute-start(f32[128,128]{1,0:T(8,128)S(1)} %get-tuple-element.22.part_ref), channel_id=1, source_target_pairs={{0,1},{1,0},{2,3},{3,2},{4,5},{5,4},{6,7},{7,6},{8,9},{9,8},{10,11... | collective-permute-start | bytes 196616 | tf_op jit(solution)/shard_map/ppermute | solution.py:302
  4.8 1.1 collective-permute-done.other_ref
  5.8 1.5 %shard_map.94 = (bf16[128,128]{1,0:T(8,128)(2,1)S(1)}, bf16[32,24,128]{2,1,0:T(8,128)(2,1)}) custom-call(s32[3]{0:T(128)} %pad_add_fusion.at_ref, s32[128]{0:T(128)} %window_ref.3, f32[128,128]{1,0:T(8,128)S(1)} %get-tuple-element.22.part_ref, f32[128,128]{1,0:T(8,128)S(1)} %collective-permute-done.other_ref, s32[1,128]{1,0:T(1,128)S(1)} %bitcast.9), custom_call_target="tpu_custom_call" | custom-call | tf_op jit(solution)/shard_map/pallas_call | solution.py:47
  7.3 11.2 %all-to-all-start = ((bf16[32,24,128]{2,1,0:T(8,128)(2,1)}), bf16[32,24,128]{2,1,0:T(8,128)(2,1)S(1)}, u32[]{:S(2)}, u32[]{:S(2)}) async-start(bf16[32,24,128]{2,1,0:T(8,128)(2,1)} %get-tuple-element.23), calls=%async_computation | async-start | bytes 393216 | tf_op jit(solution)/shard_map/all_to_all | solution.py:306
  18.5 2.2 %collective-permute-start.1 = (bf16[128,128]{1,0:T(8,128)(2,1)S(1)}, bf16[128,128]{1,0:T(8,128)(2,1)S(1)}, u32[]{:S(2)}, u32[]{:S(2)}) collective-permute-start(bf16[128,128]{1,0:T(8,128)(2,1)S(1)} %get-tuple-element.24.e0_ref), channel_id=1, source_target_pairs={{0,2},{2,0},{4,6},{6,4},{1,3},{3,1},{5,7},{7,5},{8,10},{10,8},{12,... | collective-permute-start | bytes 98312 | tf_op jit(solution)/shard_map/ppermute | solution.py:302
  20.7 2.9 %collective-permute-start.2 = (bf16[128,128]{1,0:T(8,128)(2,1)S(1)}, bf16[128,128]{1,0:T(8,128)(2,1)S(1)}, u32[]{:S(2)}, u32[]{:S(2)}) collective-permute-start(bf16[128,128]{1,0:T(8,128)(2,1)S(1)} %get-tuple-element.24.e0_ref), channel_id=1, source_target_pairs={{0,4},{2,6},{4,0},{6,2},{1,5},{3,7},{5,1},{7,3},{8,12},{10,14},{12... | collective-permute-start | bytes 98312 | tf_op jit(solution)/shard_map/ppermute | solution.py:302
  24.0 1.3 %collective-permute-done.2.e2_ref = bf16[128,128]{1,0:T(8,128)(2,1)S(1)} collective-permute-done((bf16[128,128]{1,0:T(8,128)(2,1)S(1)}, bf16[128,128]{1,0:T(8,128)(2,1)S(1)}, u32[]{:S(2)}, u32[]{:S(2)}) %collective-permute-start.2) | collective-permute-done | bytes 32800 | tf_op jit(solution)/shard_map/ppermute | solution.py:302
  25.3 3.5 %collective-permute-done.3.e3_ref = bf16[128,128]{1,0:T(8,128)(2,1)S(1)} collective-permute-done((bf16[128,128]{1,0:T(8,128)(2,1)S(1)}, bf16[128,128]{1,0:T(8,128)(2,1)S(1)}, u32[]{:S(2)}, u32[]{:S(2)}) %collective-permute-start.3) | collective-permute-done | bytes 32800 | tf_op jit(solution)/shard_map/ppermute | solution.py:302
  28.8 1.8 %shard_map.95 = bf16[32,40,128]{2,1,0:T(8,128)(2,1)S(1)} custom-call(s32[3]{0:T(128)} %pad_add_fusion.at_ref, bf16[32,24,128]{2,1,0:T(8,128)(2,1)S(1)} %all-to-all-done.msg_ref, bf16[128,128]{1,0:T(8,128)(2,1)S(1)} %get-tuple-element.24.e0_ref, bf16[128,128]{1,0:T(8,128)(2,1)S(1)} %collective-permute-done.1.e1_ref, ...), custom_call_target="tpu_custom_call" | custom-call | tf_op jit(solution)/shard_map/pallas_call | solution.py:47
  30.6 21.8 %all_to_all.25.sums_ref = bf16[32,40,128]{2,1,0:T(8,128)(2,1)S(1)} all-to-all(bf16[32,40,128]{2,1,0:T(8,128)(2,1)S(1)} %shard_map.95), channel_id=1, replica_groups=mesh['zh'=4,'zl'=2,'x'=4,'yh'=2,'c'=2,'mp'=2] {'zh','zl','x'}, dimensions={0} | all-to-all | bytes 655360 | tf_op jit(solution)/shard_map/all_to_all | solution.py:306
  52.4 1.6 %shard_map.97 = (f32[2,128,128]{2,1,0:T(8,128)S(1)}, f32[2,128,128]{2,1,0:T(8,128)S(1)}) custom-call(s32[3]{0:T(128)} %pad_add_fusion.at_ref, bf16[32,24,128]{2,1,0:T(8,128)(2,1)S(1)} %all-to-all-done.msg_ref, bf16[32,40,128]{2,1,0:T(8,128)(2,1)S(1)} %all_to_all.25.sums_ref, bf16[128,128]{1,0:T(8,128)(2,1)S(1)} %get-tuple-element.24.e0_ref, ...), custom_call_target="tpu_custom_call" | custom-call | tf_op jit(solution)/shard_map/pallas_call | solution.py:47
  54.0 2.5 %collective-permute-start.4 = (f32[2,128,128]{2,1,0:T(8,128)S(1)}, f32[2,128,128]{2,1,0:T(8,128)S(1)}, u32[]{:S(2)}, u32[]{:S(2)}) collective-permute-start(f32[2,128,128]{2,1,0:T(8,128)S(1)} %get-tuple-element.26), channel_id=1, source_target_pairs={{0,2},{2,0},{1,3},{3,1},{4,6},{6,4},{5,7},{7,5},{8,10},{10,8},{9,1... | collective-permute-start | bytes 393224 | tf_op jit(solution)/shard_map/ppermute | solution.py:302
  58.9 3.3 %collective-permute-done.5.c2_ref = f32[128,128]{1,0:T(8,128)S(1)} collective-permute-done((f32[128,128]{1,0:T(8,128)S(1)}, f32[128,128]{1,0:T(8,128)S(1)}, u32[]{:S(2)}, u32[]{:S(2)}) %collective-permute-start.5) | collective-permute-done | bytes 65568 | tf_op jit(solution)/shard_map/ppermute | solution.py:302
  63.5 2.8 %collective-permute-done.6.theirs_ref = f32[136,128]{1,0:T(8,128)S(1)} collective-permute-done((f32[136,128]{1,0:T(8,128)S(1)}, f32[136,128]{1,0:T(8,128)S(1)}, u32[]{:S(2)}, u32[]{:S(2)}) %collective-permute-start.6) | collective-permute-done | bytes 69664 | tf_op jit(solution)/shard_map/ppermute | solution.py:302
  66.3 1.3 %shard_map.100 = (f32[1,32]{1,0:T(1,128)S(1)}, f32[16,48,128]{2,1,0:T(8,128)S(1)}, f32[16,48,128]{2,1,0:T(8,128)S(1)}) custom-call(s32[3]{0:T(128)} %pad_add_fusion.at_ref, f32[136,128]{1,0:T(8,128)S(1)} %shard_map.99.mine_ref, f32[136,128]{1,0:T(8,128)S(1)} %collective-permute-done.6.theirs_ref, f32[128,128]{1,0:T(8,128)S(1)} %get-tuple-element.22.part_ref, ...), custom_call_target="tpu_custom_call" | custom-call | tf_op jit(solution)/shard_map/pallas_call | solution.py:47
  67.5 2.7 %collective-permute-start.7 = (f32[16,48,128]{2,1,0:T(8,128)S(1)}, f32[16,48,128]{2,1,0:T(8,128)S(1)}, u32[]{:S(2)}, u32[]{:S(2)}) collective-permute-start(f32[16,48,128]{2,1,0:T(8,128)S(1)} %get-tuple-element.32), channel_id=1, source_target_pairs={{0,2},{2,0},{1,3},{3,1},{4,6},{6,4},{5,7},{7,5},{8,10},{10,8},{9,1... | collective-permute-start | bytes 1179656 | tf_op jit(solution)/shard_map/ppermute | solution.py:302
  70.3 1.3 %collective-permute-done.7.b_ref = f32[16,48,128]{2,1,0:T(8,128)S(1)} collective-permute-done((f32[16,48,128]{2,1,0:T(8,128)S(1)}, f32[16,48,128]{2,1,0:T(8,128)S(1)}, u32[]{:S(2)}, u32[]{:S(2)}) %collective-permute-start.7) | collective-permute-done | bytes 393248 | tf_op jit(solution)/shard_map/ppermute | solution.py:302
  71.7 11.7 %all_to_all.26.in_ref = f32[16,48,128]{2,1,0:T(8,128)S(1)} all-to-all(f32[16,48,128]{2,1,0:T(8,128)S(1)} %shard_map.101), channel_id=1, replica_groups=mesh['zh'=4,'zl'=2,'x'=4,'yh'=2,'c'=2,'mp'=2] {'zl','x','yh'}, dimensions={0} | all-to-all | bytes 786432 | tf_op jit(solution)/shard_map/all_to_all | solution.py:306
  83.5 9.7 %all_to_all.27.in_ref = f32[4,48,128]{2,1,0:T(8,128)S(1)} all-to-all(f32[4,48,128]{2,1,0:T(8,128)S(1)} %shard_map.102), channel_id=1, replica_groups=mesh['zh'=4,'zl'=2,'x'=4,'yh'=2,'c'=2,'mp'=2] {'zh'}, dimensions={0} | all-to-all | bytes 196608 | tf_op jit(solution)/shard_map/all_to_all | solution.py:306
  93.2 12.8 %all_to_all.28.mine_ref = f32[16,48,128]{2,1,0:T(8,128)S(1)} all-to-all(f32[16,48,128]{2,1,0:T(8,128)S(1)} %shard_map.103), channel_id=1, replica_groups=mesh['zh'=4,'zl'=2,'x'=4,'yh'=2,'c'=2,'mp'=2] {'zl','x','yh'}, dimensions={0} | all-to-all | bytes 786432 | tf_op jit(solution)/shard_map/all_to_all | solution.py:306
  106.0 4.7 %collective-permute-start.8 = (f32[16,48,128]{2,1,0:T(8,128)S(1)}, f32[16,48,128]{2,1,0:T(8,128)S(1)}, u32[]{:S(2)}, u32[]{:S(2)}) collective-permute-start(f32[16,48,128]{2,1,0:T(8,128)S(1)} %all_to_all.28.mine_ref), channel_id=1, source_target_pairs={{0,2},{2,0},{1,3},{3,1},{4,6},{6,4},{5,7},{7,5},{8,10},{10,8},{9,1... | collective-permute-start | bytes 1179656 | tf_op jit(solution)/shard_map/ppermute | solution.py:302
  110.7 1.4 %shard_map.104 = (f32[16,32,256]{2,1,0:T(8,128)}, f32[2,16,8,128]{3,2,1,0:T(8,128)}, f32[1,32]{1,0:T(1,128)}) custom-call(s32[3]{0:T(128)} %pad_add_fusion.at_ref, f32[16,48,128]{2,1,0:T(8,128)S(1)} %all_to_all.28.mine_ref, f32[1,32]{1,0:T(1,128)S(1)} %get-tuple-element.33.loss_in_ref), custom_call_target="tpu_custom_call" | custom-call | tf_op jit(solution)/shard_map/pallas_call | solution.py:47
  112.1 1.4 %shard_map.105 = (f32[16,32,256]{2,1,0:T(8,128)}, f32[2,16,8,128]{3,2,1,0:T(8,128)}, f32[2,128]{1,0:T(2,128)}) custom-call(s32[3]{0:T(128)} %pad_add_fusion.at_ref, f32[16,48,128]{2,1,0:T(8,128)S(1)} %all_to_all.28.mine_ref, f32[16,48,128]{2,1,0:T(8,128)S(1)} %collective-permute-done.8.theirs_ref, ...), custom_call_target="tpu_custom_call", output_to_operand_aliasing={{0}: (3, {}), {1}: (4, {})} | custom-call | tf_op jit(solution)/shard_map/pallas_call | solution.py:47
  (20 shorter events, 4.7 us)
Async XLA Ops:
  2.0 3.9 %collective-permute-start = (f32[128,128]{1,0:T(8,128)S(1)}, f32[128,128]{1,0:T(8,128)S(1)}, u32[]{:S(2)}, u32[]{:S(2)}) collective-permute-start(f32[128,128]{1,0:T(8,128)S(1)} %get-tuple-element.22.part_ref), channel_id=1, source_target_pairs={{0,1},{1,0},{2,3},{3,2},{4,5},{5,4},{6,7},{7,6},{8,9},{9,8},{10,11... | collective-permute-start | bytes 196616 | tf_op jit(solution)/shard_map/ppermute | solution.py:302
  4.8 1.1 copy-start.2
  7.3 21.5 %all-to-all-start = ((bf16[32,24,128]{2,1,0:T(8,128)(2,1)}), bf16[32,24,128]{2,1,0:T(8,128)(2,1)S(1)}, u32[]{:S(2)}, u32[]{:S(2)}) async-start(bf16[32,24,128]{2,1,0:T(8,128)(2,1)} %get-tuple-element.23), calls=%async_computation | async-start | bytes 393216 | tf_op jit(solution)/shard_map/all_to_all | solution.py:306
  18.5 5.4 %collective-permute-start.1 = (bf16[128,128]{1,0:T(8,128)(2,1)S(1)}, bf16[128,128]{1,0:T(8,128)(2,1)S(1)}, u32[]{:S(2)}, u32[]{:S(2)}) collective-permute-start(bf16[128,128]{1,0:T(8,128)(2,1)S(1)} %get-tuple-element.24.e0_ref), channel_id=1, source_target_pairs={{0,2},{2,0},{4,6},{6,4},{1,3},{3,1},{5,7},{7,5},{8,10},{10,8},{12,... | collective-permute-start | bytes 98312 | tf_op jit(solution)/shard_map/ppermute | solution.py:302
  20.7 4.6 %collective-permute-start.2 = (bf16[128,128]{1,0:T(8,128)(2,1)S(1)}, bf16[128,128]{1,0:T(8,128)(2,1)S(1)}, u32[]{:S(2)}, u32[]{:S(2)}) collective-permute-start(bf16[128,128]{1,0:T(8,128)(2,1)S(1)} %get-tuple-element.24.e0_ref), channel_id=1, source_target_pairs={{0,4},{2,6},{4,0},{6,2},{1,5},{3,7},{5,1},{7,3},{8,12},{10,14},{12... | collective-permute-start | bytes 98312 | tf_op jit(solution)/shard_map/ppermute | solution.py:302
  23.6 5.2 %collective-permute-start.3 = (bf16[128,128]{1,0:T(8,128)(2,1)S(1)}, bf16[128,128]{1,0:T(8,128)(2,1)S(1)}, u32[]{:S(2)}, u32[]{:S(2)}) collective-permute-start(bf16[128,128]{1,0:T(8,128)(2,1)S(1)} %get-tuple-element.24.e0_ref), channel_id=1, source_target_pairs={{0,6},{2,4},{4,2},{6,0},{1,7},{3,5},{5,3},{7,1},{8,14},{10,12},{12... | collective-permute-start | bytes 98312 | tf_op jit(solution)/shard_map/ppermute | solution.py:302
  54.0 3.5 %collective-permute-start.4 = (f32[2,128,128]{2,1,0:T(8,128)S(1)}, f32[2,128,128]{2,1,0:T(8,128)S(1)}, u32[]{:S(2)}, u32[]{:S(2)}) collective-permute-start(f32[2,128,128]{2,1,0:T(8,128)S(1)} %get-tuple-element.26), channel_id=1, source_target_pairs={{0,2},{2,0},{1,3},{3,1},{4,6},{6,4},{5,7},{7,5},{8,10},{10,8},{9,1... | collective-permute-start | bytes 393224 | tf_op jit(solution)/shard_map/ppermute | solution.py:302
  57.5 4.7 %collective-permute-start.5 = (f32[128,128]{1,0:T(8,128)S(1)}, f32[128,128]{1,0:T(8,128)S(1)}, u32[]{:S(2)}, u32[]{:S(2)}) collective-permute-start(f32[128,128]{1,0:T(8,128)S(1)} %get-tuple-element.28), channel_id=1, source_target_pairs={{0,4},{4,0},{1,5},{5,1},{2,6},{6,2},{3,7},{7,3},{8,12},{12,8},{9,1... | collective-permute-start | bytes 196616 | tf_op jit(solution)/shard_map/ppermute | solution.py:302
  58.9 7.4 %copy-start = (bf16[128,512]{1,0:T(8,128)(2,1)S(1)}, bf16[128,512]{1,0:T(8,128)(2,1)}, u32[]{:S(2)}) copy-start(bf16[128,512]{1,0:T(8,128)(2,1)} %x_ref.3) | copy-start | bytes 393220
  62.2 4.1 %copy-start.1 = (bf16[256,128]{1,0:T(8,128)(2,1)S(1)}, bf16[256,128]{1,0:T(8,128)(2,1)}, u32[]{:S(2)}) copy-start(bf16[256,128]{1,0:T(8,128)(2,1)} %w_out_ref.3) | copy-start | bytes 196612
  63.0 3.2 %collective-permute-start.6 = (f32[136,128]{1,0:T(8,128)S(1)}, f32[136,128]{1,0:T(8,128)S(1)}, u32[]{:S(2)}, u32[]{:S(2)}) collective-permute-start(f32[136,128]{1,0:T(8,128)S(1)} %shard_map.99.mine_ref), channel_id=1, source_target_pairs={{0,1},{1,0},{2,3},{3,2},{4,5},{5,4},{6,7},{7,6},{8,9},{9,8},{10,11... | collective-permute-start | bytes 208904 | tf_op jit(solution)/shard_map/ppermute | solution.py:302
  67.5 4.1 %collective-permute-start.7 = (f32[16,48,128]{2,1,0:T(8,128)S(1)}, f32[16,48,128]{2,1,0:T(8,128)S(1)}, u32[]{:S(2)}, u32[]{:S(2)}) collective-permute-start(f32[16,48,128]{2,1,0:T(8,128)S(1)} %get-tuple-element.32), channel_id=1, source_target_pairs={{0,2},{2,0},{1,3},{3,1},{4,6},{6,4},{5,7},{7,5},{8,10},{10,8},{9,1... | collective-permute-start | bytes 1179656 | tf_op jit(solution)/shard_map/ppermute | solution.py:302
  106.0 6.1 %collective-permute-start.8 = (f32[16,48,128]{2,1,0:T(8,128)S(1)}, f32[16,48,128]{2,1,0:T(8,128)S(1)}, u32[]{:S(2)}, u32[]{:S(2)}) collective-permute-start(f32[16,48,128]{2,1,0:T(8,128)S(1)} %all_to_all.28.mine_ref), channel_id=1, source_target_pairs={{0,2},{2,0},{1,3},{3,1},{4,6},{6,4},{5,7},{7,5},{8,10},{10,8},{9,1... | collective-permute-start | bytes 1179656 | tf_op jit(solution)/shard_map/ppermute | solution.py:302

commit v5 on v4

--- a/solution.py
+++ b/solution.py
@@ -26,6 +26,7 @@
 INV_TEMP = 10.0
 SHIFT = 10.0
 EPS = 1e-06
+LOG2E = 1.4426950408889634
 BF16 = jnp.bfloat16
 F32 = jnp.float32
 I32 = jnp.int32
@@ -128,10 +129,10 @@
     ones = jnp.ones((ROWS, EMB), BF16)
     for r, e_ref in enumerate((e0_ref, e1_ref, e2_ref, e3_ref)):
         cols_emb = e_ref[...]
-        s = dot(cols_emb, anchors, ((1,), (1,))) * INV_TEMP
+        s = dot(cols_emb, anchors, ((1,), (1,)))
         cols = column_ids(at_ref, r)
         positive = cols == partner
-        ex = jnp.where(cols == own, 0.0, jnp.exp(s - SHIFT))
+        ex = jnp.where(cols == own, 0.0, jnp.exp2(s * (INV_TEMP * LOG2E) - SHIFT * LOG2E))
         total = total + jnp.sum(ex, axis=0, keepdims=True)
         others = jnp.where(positive, 0.0, ex).astype(BF16)
         rows = rows + dot(others, jnp.concatenate([cols_emb, ones], axis=1), ((0,), (0,)))
@@ -160,11 +161,12 @@
     partner, own = block_ids(at_ref, msg_ref)
     total = totals_of(sums_ref)
     total = jnp.concatenate([total[i : i + 1] for i in range(4)], axis=1)
+    offset = SHIFT * LOG2E + jnp.log2(total)
     for r, e_ref in enumerate((e0_ref, e1_ref, e2_ref, e3_ref)):
-        s = dot(e_ref[...], anchors, ((1,), (1,))) * INV_TEMP
+        s = dot(e_ref[...], anchors, ((1,), (1,)))
         cols = column_ids(at_ref, r)
-        prob = jnp.where(cols == own, 0.0, jnp.exp(s - SHIFT) / total)
-        w = (prob - (cols == partner).astype(F32)).astype(BF16)
+        prob = jnp.where(cols == own, 0.0, jnp.exp2(s * (INV_TEMP * LOG2E) - offset))
+        w = jnp.where(cols == partner, prob - 1.0, prob).astype(BF16)
         c_ref = send_ref if r % 2 else keep_ref
         c_ref[r // 2] = dot(w, anchors, ((1,), (0,)))
 
@@ -192,23 +194,21 @@
     out_ref[0:HALF, :] = rows / total_of + weight * pair
 
 
-def add_pair(a_ref, b_ref, mine_ref, next_ref):
-    mine_ref[...] = a_ref[0] + b_ref[0]
+def add_pair(at_ref, window_ref, a_ref, b_ref, rows_ref, mine_ref, next_ref):
+    g, q, mp = at_ref[0], at_ref[1], at_ref[2]
+    mine_ref[0:ROWS, :] = a_ref[0] + b_ref[0]
     next_ref[...] = a_ref[1] + b_ref[1]
-
-
-def gather_rows(at_ref, window_ref, rows_ref, c0_ref, c2_ref, out_ref):
-    g, q, mp = at_ref[0], at_ref[1], at_ref[2]
-    out_ref[0:ROWS, :] = c0_ref[...] + c2_ref[...]
     start = pl.multiple_of(window_ref[g * N_QUAD + q] * A_DEV + mp * HALF, HALF)
-    out_ref[pl.ds(start, HALF), :] = out_ref[pl.ds(start, HALF), :] + rows_ref[0:HALF, :]
-    out_ref[ROWS:, :] = rows_ref[HALF:, :]
+    mine_ref[pl.ds(start, HALF), :] = mine_ref[pl.ds(start, HALF), :] + rows_ref[0:HALF, :]
+    mine_ref[ROWS:, :] = rows_ref[HALF:, :]
 
 
 def backward(
     at_ref,
     mine_ref,
     theirs_ref,
+    third_ref,
+    fourth_ref,
     part_ref,
     other_ref,
     pre_ref,
@@ -220,7 +220,8 @@
     send_ref,
 ):
     scale = INV_TEMP / (N_FAR * N_QUAD * A_DEV)
-    grad_emb = (mine_ref[0:ROWS, :] + theirs_ref[0:ROWS, :]) * scale
+    grad_emb = mine_ref[0:ROWS, :] + theirs_ref[0:ROWS, :]
+    grad_emb = (grad_emb + (third_ref[...] + fourth_ref[...])) * scale
     loss_ref[...] = mine_ref[ROWS : ROWS + 1, 0:A_DEV] + theirs_ref[ROWS : ROWS + 1, 0:A_DEV]
     proj = part_ref[...] + other_ref[...]
     norm = norm_of(proj)
@@ -339,11 +340,18 @@
     )
     got = swap(send, "c", 1)
     (rows,) = call(own_rows, [((HALF + 8, EMB), F32)], at, anchors, sums, smem=(0,))
-    c0, c2 = call(add_pair, [((ROWS, EMB), F32)] * 2, keep, got)
-    c2 = swap(c2, "yh", 1)
-    (mine,) = call(
-        gather_rows, [((ROWS + 8, EMB), F32)], at, window, rows, c0, c2, smem=(0, 1)
-    )
+    mine, away = call(
+        add_pair,
+        [((ROWS + 8, EMB), F32), ((ROWS, EMB), F32)],
+        at,
+        window,
+        keep,
+        got,
+        rows,
+        smem=(0, 1),
+    )
+    third = swap(away, "yh", 1)
+    fourth = swap(away, ("yh", "mp"), 3)
     theirs = swap(mine, "mp", 1)
     half = (N_NEAR, PART, EMB)
     row_loss, keep, send = call(
@@ -352,6 +360,8 @@
         at,
         mine,
         theirs,
+        third,
+        fourth,
         part,
         other,
         pre,

time: 114 us -> 112 us (0.982)
  waiting for transfers between devices: 14.4 us -> 10.4 us
  starting transfers between devices: 29.7 us -> 31.6 us
    ppermute x9 -> x10, waiting for transfers between devices: 14.4 us -> 10.4 us  [swap(): return lax.ppermute(value, axes, [(i, i ^ flip) for i in range(count)])]
    ppermute x9 -> x10, starting transfers between devices: 18.5 us -> 20.4 us  [swap(): return lax.ppermute(value, axes, [(i, i ^ flip) for i in range(count)])]
    pallas_call x13 -> x12, Pallas kernels: 12.1 us -> 12.1 us  [call(): pl.pallas_call(kernel, out_shape=shapes, in_specs=specs, out_specs=[pl.Bl...]
  transfers between devices with their start and end apart: 10 -> 11, of which waited for: 7 -> 7; matrix products, arithmetic and copies ran while one was open for 1% -> 1% of each run, Pallas kernels for 2% -> 2%
where the time goes in v5:
time: 112 us
  blocking collectives  56.3 us (50%)
  starting transfers between devices  31.6 us (28%)
  Pallas kernels  12.1 us (11%)
  waiting for transfers between devices  10.4 us (9%)
    all_to_all x4, blocking collectives, exchange(): return lax.all_to_all(value, axes, 0, 0, tiled=True)  56.3 us
    ppermute x10, starting transfers between devices, swap(): return lax.ppermute(value, axes, [(i, i ^ flip) for i in range(count)])  20.4 us
    pallas_call x12, Pallas kernels, call(): pl.pallas_call(kernel, out_shape=shapes, in_specs=specs, out_specs=[pl.Bl...  12.1 us
    all_to_all x1, starting transfers between devices, exchange(): return lax.all_to_all(value, axes, 0, 0, tiled=True)  11.2 us
    ppermute x10, waiting for transfers between devices, swap(): return lax.ppermute(value, axes, [(i, i ^ flip) for i in range(count)])  10.4 us
  transfers between devices with their start and end apart: 11, of which 7 were waited for; matrix products, arithmetic and copies ran while one was open for 1% of the time, Pallas kernels for 2%

profile of v5, /device:TPU:1, one launch (start us, length us, event | category | flops | bytes accessed | tf_op | source)
XLA Modules:
  0.0 111.7 jit_solution(6295643356507646180)
XLA Ops:
  0.6 1.3 %shard_map.93 = (f32[128,128]{1,0:T(8,128)S(1)}, f32[128,256]{1,0:T(8,128)S(1)}, bf16[128,256]{1,0:T(8,128)(2,1)S(1)}) custom-call(bf16[128,512]{1,0:T(8,128)(2,1)} %x_ref.3, bf16[512,256]{1,0:T(8,128)(2,1)} %w_in_ref.1, f32[1,256]{1,0:T(1,128)} %bitcast.12, bf16[256,128]{1,0:T(8,128)(2,1)} %w_out_ref.3), custom_call_target="tpu_custom_call" | custom-call | tf_op jit(solution)/shard_map/pallas_call | solution.py:48
  2.0 2.2 %collective-permute-start = (f32[128,128]{1,0:T(8,128)S(1)}, f32[128,128]{1,0:T(8,128)S(1)}, u32[]{:S(2)}, u32[]{:S(2)}) collective-permute-start(f32[128,128]{1,0:T(8,128)S(1)} %get-tuple-element.22.part_ref), channel_id=1, source_target_pairs={{0,1},{1,0},{2,3},{3,2},{4,5},{5,4},{6,7},{7,6},{8,9},{9,8},{10,11... | collective-permute-start | bytes 196616 | tf_op jit(solution)/shard_map/ppermute | solution.py:303
  5.8 1.5 %shard_map.94 = (bf16[128,128]{1,0:T(8,128)(2,1)S(1)}, bf16[32,24,128]{2,1,0:T(8,128)(2,1)}) custom-call(s32[3]{0:T(128)} %pad_add_fusion.at_ref, s32[128]{0:T(128)} %window_ref.3, f32[128,128]{1,0:T(8,128)S(1)} %get-tuple-element.22.part_ref, f32[128,128]{1,0:T(8,128)S(1)} %collective-permute-done.other_ref, s32[1,128]{1,0:T(1,128)S(1)} %bitcast.9), custom_call_target="tpu_custom_call" | custom-call | tf_op jit(solution)/shard_map/pallas_call | solution.py:48
  7.3 11.2 %all-to-all-start = ((bf16[32,24,128]{2,1,0:T(8,128)(2,1)}), bf16[32,24,128]{2,1,0:T(8,128)(2,1)S(1)}, u32[]{:S(2)}, u32[]{:S(2)}) async-start(bf16[32,24,128]{2,1,0:T(8,128)(2,1)} %get-tuple-element.23), calls=%async_computation | async-start | bytes 393216 | tf_op jit(solution)/shard_map/all_to_all | solution.py:307
  18.5 2.2 %collective-permute-start.1 = (bf16[128,128]{1,0:T(8,128)(2,1)S(1)}, bf16[128,128]{1,0:T(8,128)(2,1)S(1)}, u32[]{:S(2)}, u32[]{:S(2)}) collective-permute-start(bf16[128,128]{1,0:T(8,128)(2,1)S(1)} %get-tuple-element.24.e0_ref), channel_id=1, source_target_pairs={{0,2},{2,0},{4,6},{6,4},{1,3},{3,1},{5,7},{7,5},{8,10},{10,8},{12,... | collective-permute-start | bytes 98312 | tf_op jit(solution)/shard_map/ppermute | solution.py:303
  20.7 2.9 %collective-permute-start.2 = (bf16[128,128]{1,0:T(8,128)(2,1)S(1)}, bf16[128,128]{1,0:T(8,128)(2,1)S(1)}, u32[]{:S(2)}, u32[]{:S(2)}) collective-permute-start(bf16[128,128]{1,0:T(8,128)(2,1)S(1)} %get-tuple-element.24.e0_ref), channel_id=1, source_target_pairs={{0,4},{2,6},{4,0},{6,2},{1,5},{3,7},{5,1},{7,3},{8,12},{10,14},{12... | collective-permute-start | bytes 98312 | tf_op jit(solution)/shard_map/ppermute | solution.py:303
  24.0 1.3 %collective-permute-done.2.e2_ref = bf16[128,128]{1,0:T(8,128)(2,1)S(1)} collective-permute-done((bf16[128,128]{1,0:T(8,128)(2,1)S(1)}, bf16[128,128]{1,0:T(8,128)(2,1)S(1)}, u32[]{:S(2)}, u32[]{:S(2)}) %collective-permute-start.2) | collective-permute-done | bytes 32800 | tf_op jit(solution)/shard_map/ppermute | solution.py:303
  25.3 3.5 %collective-permute-done.3.e3_ref = bf16[128,128]{1,0:T(8,128)(2,1)S(1)} collective-permute-done((bf16[128,128]{1,0:T(8,128)(2,1)S(1)}, bf16[128,128]{1,0:T(8,128)(2,1)S(1)}, u32[]{:S(2)}, u32[]{:S(2)}) %collective-permute-start.3) | collective-permute-done | bytes 32800 | tf_op jit(solution)/shard_map/ppermute | solution.py:303
  28.8 1.8 %shard_map.95 = bf16[32,40,128]{2,1,0:T(8,128)(2,1)S(1)} custom-call(s32[3]{0:T(128)} %pad_add_fusion.at_ref, bf16[32,24,128]{2,1,0:T(8,128)(2,1)S(1)} %all-to-all-done.msg_ref, bf16[128,128]{1,0:T(8,128)(2,1)S(1)} %get-tuple-element.24.e0_ref, bf16[128,128]{1,0:T(8,128)(2,1)S(1)} %collective-permute-done.1.e1_ref, ...), custom_call_target="tpu_custom_call" | custom-call | tf_op jit(solution)/shard_map/pallas_call | solution.py:48
  30.6 21.8 %all_to_all.25.sums_ref = bf16[32,40,128]{2,1,0:T(8,128)(2,1)S(1)} all-to-all(bf16[32,40,128]{2,1,0:T(8,128)(2,1)S(1)} %shard_map.95), channel_id=1, replica_groups=mesh['zh'=4,'zl'=2,'x'=4,'yh'=2,'c'=2,'mp'=2] {'zh','zl','x'}, dimensions={0} | all-to-all | bytes 655360 | tf_op jit(solution)/shard_map/all_to_all | solution.py:307
  52.4 1.6 %shard_map.96 = (f32[2,128,128]{2,1,0:T(8,128)S(1)}, f32[2,128,128]{2,1,0:T(8,128)S(1)}) custom-call(s32[3]{0:T(128)} %pad_add_fusion.at_ref, bf16[32,24,128]{2,1,0:T(8,128)(2,1)S(1)} %all-to-all-done.msg_ref, bf16[32,40,128]{2,1,0:T(8,128)(2,1)S(1)} %all_to_all.25.sums_ref, bf16[128,128]{1,0:T(8,128)(2,1)S(1)} %get-tuple-element.24.e0_ref, ...), custom_call_target="tpu_custom_call" | custom-call | tf_op jit(solution)/shard_map/pallas_call | solution.py:48
  54.0 2.5 %collective-permute-start.4 = (f32[2,128,128]{2,1,0:T(8,128)S(1)}, f32[2,128,128]{2,1,0:T(8,128)S(1)}, u32[]{:S(2)}, u32[]{:S(2)}) collective-permute-start(f32[2,128,128]{2,1,0:T(8,128)S(1)} %get-tuple-element.26), channel_id=1, source_target_pairs={{0,2},{2,0},{1,3},{3,1},{4,6},{6,4},{5,7},{7,5},{8,10},{10,8},{9,1... | collective-permute-start | bytes 393224 | tf_op jit(solution)/shard_map/ppermute | solution.py:303
  58.8 1.6 %collective-permute-start.6 = (f32[128,128]{1,0:T(8,128)S(1)}, f32[128,128]{1,0:T(8,128)S(1)}, u32[]{:S(2)}, u32[]{:S(2)}) collective-permute-start(f32[128,128]{1,0:T(8,128)S(1)} %get-tuple-element.28), channel_id=1, source_target_pairs={{0,4},{4,0},{1,5},{5,1},{2,6},{6,2},{3,7},{7,3},{8,12},{12,8},{9,1... | collective-permute-start | bytes 196616 | tf_op jit(solution)/shard_map/ppermute | solution.py:303
  60.3 1.9 %collective-permute-start.7 = (f32[128,128]{1,0:T(8,128)S(1)}, f32[128,128]{1,0:T(8,128)S(1)}, u32[]{:S(2)}, u32[]{:S(2)}) collective-permute-start(f32[128,128]{1,0:T(8,128)S(1)} %get-tuple-element.28), channel_id=1, source_target_pairs={{0,5},{1,4},{4,1},{5,0},{2,7},{3,6},{6,3},{7,2},{8,13},{9,12},{12,... | collective-permute-start | bytes 196616 | tf_op jit(solution)/shard_map/ppermute | solution.py:303
  62.2 1.3 %collective-permute-done.6.third_ref = f32[128,128]{1,0:T(8,128)S(1)} collective-permute-done((f32[128,128]{1,0:T(8,128)S(1)}, f32[128,128]{1,0:T(8,128)S(1)}, u32[]{:S(2)}, u32[]{:S(2)}) %collective-permute-start.6) | collective-permute-done | bytes 65568 | tf_op jit(solution)/shard_map/ppermute | solution.py:303
  63.5 1.6 %collective-permute-done.7.fourth_ref = f32[128,128]{1,0:T(8,128)S(1)} collective-permute-done((f32[128,128]{1,0:T(8,128)S(1)}, f32[128,128]{1,0:T(8,128)S(1)}, u32[]{:S(2)}, u32[]{:S(2)}) %collective-permute-start.7) | collective-permute-done | bytes 65568 | tf_op jit(solution)/shard_map/ppermute | solution.py:303
  66.5 1.6 %collective-permute-start.8 = (f32[16,48,128]{2,1,0:T(8,128)S(1)}, f32[16,48,128]{2,1,0:T(8,128)S(1)}, u32[]{:S(2)}, u32[]{:S(2)}) collective-permute-start(f32[16,48,128]{2,1,0:T(8,128)S(1)} %get-tuple-element.32), channel_id=1, source_target_pairs={{0,2},{2,0},{1,3},{3,1},{4,6},{6,4},{5,7},{7,5},{8,10},{10,8},{9,1... | collective-permute-start | bytes 1179656 | tf_op jit(solution)/shard_map/ppermute | solution.py:303
  68.1 1.3 %collective-permute-done.8.b_ref = f32[16,48,128]{2,1,0:T(8,128)S(1)} collective-permute-done((f32[16,48,128]{2,1,0:T(8,128)S(1)}, f32[16,48,128]{2,1,0:T(8,128)S(1)}, u32[]{:S(2)}, u32[]{:S(2)}) %collective-permute-start.8) | collective-permute-done | bytes 393248 | tf_op jit(solution)/shard_map/ppermute | solution.py:303
  69.5 12.2 %all_to_all.26.in_ref = f32[16,48,128]{2,1,0:T(8,128)S(1)} all-to-all(f32[16,48,128]{2,1,0:T(8,128)S(1)} %shard_map.100), channel_id=1, replica_groups=mesh['zh'=4,'zl'=2,'x'=4,'yh'=2,'c'=2,'mp'=2] {'zl','x','yh'}, dimensions={0} | all-to-all | bytes 786432 | tf_op jit(solution)/shard_map/all_to_all | solution.py:307
  81.7 9.7 %all_to_all.27.in_ref = f32[4,48,128]{2,1,0:T(8,128)S(1)} all-to-all(f32[4,48,128]{2,1,0:T(8,128)S(1)} %shard_map.101), channel_id=1, replica_groups=mesh['zh'=4,'zl'=2,'x'=4,'yh'=2,'c'=2,'mp'=2] {'zh'}, dimensions={0} | all-to-all | bytes 196608 | tf_op jit(solution)/shard_map/all_to_all | solution.py:307
  91.5 12.6 %all_to_all.28.mine_ref = f32[16,48,128]{2,1,0:T(8,128)S(1)} all-to-all(f32[16,48,128]{2,1,0:T(8,128)S(1)} %shard_map.102), channel_id=1, replica_groups=mesh['zh'=4,'zl'=2,'x'=4,'yh'=2,'c'=2,'mp'=2] {'zl','x','yh'}, dimensions={0} | all-to-all | bytes 786432 | tf_op jit(solution)/shard_map/all_to_all | solution.py:307
  104.1 4.8 %collective-permute-start.9 = (f32[16,48,128]{2,1,0:T(8,128)S(1)}, f32[16,48,128]{2,1,0:T(8,128)S(1)}, u32[]{:S(2)}, u32[]{:S(2)}) collective-permute-start(f32[16,48,128]{2,1,0:T(8,128)S(1)} %all_to_all.28.mine_ref), channel_id=1, source_target_pairs={{0,2},{2,0},{1,3},{3,1},{4,6},{6,4},{5,7},{7,5},{8,10},{10,8},{9,1... | collective-permute-start | bytes 1179656 | tf_op jit(solution)/shard_map/ppermute | solution.py:303
  108.8 1.4 %shard_map.103 = (f32[16,32,256]{2,1,0:T(8,128)}, f32[2,16,8,128]{3,2,1,0:T(8,128)}, f32[1,32]{1,0:T(1,128)}) custom-call(s32[3]{0:T(128)} %pad_add_fusion.at_ref, f32[16,48,128]{2,1,0:T(8,128)S(1)} %all_to_all.28.mine_ref, f32[1,32]{1,0:T(1,128)S(1)} %get-tuple-element.33.loss_in_ref), custom_call_target="tpu_custom_call" | custom-call | tf_op jit(solution)/shard_map/pallas_call | solution.py:48
  110.3 1.4 %shard_map.104 = (f32[16,32,256]{2,1,0:T(8,128)}, f32[2,16,8,128]{3,2,1,0:T(8,128)}, f32[2,128]{1,0:T(2,128)}) custom-call(s32[3]{0:T(128)} %pad_add_fusion.at_ref, f32[16,48,128]{2,1,0:T(8,128)S(1)} %all_to_all.28.mine_ref, f32[16,48,128]{2,1,0:T(8,128)S(1)} %collective-permute-done.9.theirs_ref, ...), custom_call_target="tpu_custom_call", output_to_operand_aliasing={{0}: (3, {}), {1}: (4, {})} | custom-call | tf_op jit(solution)/shard_map/pallas_call | solution.py:48
  (21 shorter events, 5.7 us)
Async XLA Ops:
  2.0 3.9 %collective-permute-start = (f32[128,128]{1,0:T(8,128)S(1)}, f32[128,128]{1,0:T(8,128)S(1)}, u32[]{:S(2)}, u32[]{:S(2)}) collective-permute-start(f32[128,128]{1,0:T(8,128)S(1)} %get-tuple-element.22.part_ref), channel_id=1, source_target_pairs={{0,1},{1,0},{2,3},{3,2},{4,5},{5,4},{6,7},{7,6},{8,9},{9,8},{10,11... | collective-permute-start | bytes 196616 | tf_op jit(solution)/shard_map/ppermute | solution.py:303
  4.8 1.1 copy-start.2
  7.3 21.5 %all-to-all-start = ((bf16[32,24,128]{2,1,0:T(8,128)(2,1)}), bf16[32,24,128]{2,1,0:T(8,128)(2,1)S(1)}, u32[]{:S(2)}, u32[]{:S(2)}) async-start(bf16[32,24,128]{2,1,0:T(8,128)(2,1)} %get-tuple-element.23), calls=%async_computation | async-start | bytes 393216 | tf_op jit(solution)/shard_map/all_to_all | solution.py:307
  18.5 5.4 %collective-permute-start.1 = (bf16[128,128]{1,0:T(8,128)(2,1)S(1)}, bf16[128,128]{1,0:T(8,128)(2,1)S(1)}, u32[]{:S(2)}, u32[]{:S(2)}) collective-permute-start(bf16[128,128]{1,0:T(8,128)(2,1)S(1)} %get-tuple-element.24.e0_ref), channel_id=1, source_target_pairs={{0,2},{2,0},{4,6},{6,4},{1,3},{3,1},{5,7},{7,5},{8,10},{10,8},{12,... | collective-permute-start | bytes 98312 | tf_op jit(solution)/shard_map/ppermute | solution.py:303
  20.7 4.6 %collective-permute-start.2 = (bf16[128,128]{1,0:T(8,128)(2,1)S(1)}, bf16[128,128]{1,0:T(8,128)(2,1)S(1)}, u32[]{:S(2)}, u32[]{:S(2)}) collective-permute-start(bf16[128,128]{1,0:T(8,128)(2,1)S(1)} %get-tuple-element.24.e0_ref), channel_id=1, source_target_pairs={{0,4},{2,6},{4,0},{6,2},{1,5},{3,7},{5,1},{7,3},{8,12},{10,14},{12... | collective-permute-start | bytes 98312 | tf_op jit(solution)/shard_map/ppermute | solution.py:303
  23.6 5.2 %collective-permute-start.3 = (bf16[128,128]{1,0:T(8,128)(2,1)S(1)}, bf16[128,128]{1,0:T(8,128)(2,1)S(1)}, u32[]{:S(2)}, u32[]{:S(2)}) collective-permute-start(bf16[128,128]{1,0:T(8,128)(2,1)S(1)} %get-tuple-element.24.e0_ref), channel_id=1, source_target_pairs={{0,6},{2,4},{4,2},{6,0},{1,7},{3,5},{5,3},{7,1},{8,14},{10,12},{12... | collective-permute-start | bytes 98312 | tf_op jit(solution)/shard_map/ppermute | solution.py:303
  54.0 3.5 %collective-permute-start.4 = (f32[2,128,128]{2,1,0:T(8,128)S(1)}, f32[2,128,128]{2,1,0:T(8,128)S(1)}, u32[]{:S(2)}, u32[]{:S(2)}) collective-permute-start(f32[2,128,128]{2,1,0:T(8,128)S(1)} %get-tuple-element.26), channel_id=1, source_target_pairs={{0,2},{2,0},{1,3},{3,1},{4,6},{6,4},{5,7},{7,5},{8,10},{10,8},{9,1... | collective-permute-start | bytes 393224 | tf_op jit(solution)/shard_map/ppermute | solution.py:303
  57.4 7.7 %copy-start = (bf16[128,512]{1,0:T(8,128)(2,1)S(1)}, bf16[128,512]{1,0:T(8,128)(2,1)}, u32[]{:S(2)}) copy-start(bf16[128,512]{1,0:T(8,128)(2,1)} %x_ref.3) | copy-start | bytes 393220
  57.4 7.7 %copy-start.1 = (bf16[256,128]{1,0:T(8,128)(2,1)S(1)}, bf16[256,128]{1,0:T(8,128)(2,1)}, u32[]{:S(2)}) copy-start(bf16[256,128]{1,0:T(8,128)(2,1)} %w_out_ref.3) | copy-start | bytes 196612
  58.3 6.9 %collective-permute-start.5 = (f32[136,128]{1,0:T(8,128)S(1)}, f32[136,128]{1,0:T(8,128)S(1)}, u32[]{:S(2)}, u32[]{:S(2)}) collective-permute-start(f32[136,128]{1,0:T(8,128)S(1)} %get-tuple-element.27.mine_ref), channel_id=1, source_target_pairs={{0,1},{1,0},{2,3},{3,2},{4,5},{5,4},{6,7},{7,6},{8,9},{9,8},{10,11... | collective-permute-start | bytes 208904 | tf_op jit(solution)/shard_map/ppermute | solution.py:303
  58.8 4.8 %collective-permute-start.6 = (f32[128,128]{1,0:T(8,128)S(1)}, f32[128,128]{1,0:T(8,128)S(1)}, u32[]{:S(2)}, u32[]{:S(2)}) collective-permute-start(f32[128,128]{1,0:T(8,128)S(1)} %get-tuple-element.28), channel_id=1, source_target_pairs={{0,4},{4,0},{1,5},{5,1},{2,6},{6,2},{3,7},{7,3},{8,12},{12,8},{9,1... | collective-permute-start | bytes 196616 | tf_op jit(solution)/shard_map/ppermute | solution.py:303
  60.3 4.9 %collective-permute-start.7 = (f32[128,128]{1,0:T(8,128)S(1)}, f32[128,128]{1,0:T(8,128)S(1)}, u32[]{:S(2)}, u32[]{:S(2)}) collective-permute-start(f32[128,128]{1,0:T(8,128)S(1)} %get-tuple-element.28), channel_id=1, source_target_pairs={{0,5},{1,4},{4,1},{5,0},{2,7},{3,6},{6,3},{7,2},{8,13},{9,12},{12,... | collective-permute-start | bytes 196616 | tf_op jit(solution)/shard_map/ppermute | solution.py:303
  66.5 3.0 %collective-permute-start.8 = (f32[16,48,128]{2,1,0:T(8,128)S(1)}, f32[16,48,128]{2,1,0:T(8,128)S(1)}, u32[]{:S(2)}, u32[]{:S(2)}) collective-permute-start(f32[16,48,128]{2,1,0:T(8,128)S(1)} %get-tuple-element.32), channel_id=1, source_target_pairs={{0,2},{2,0},{1,3},{3,1},{4,6},{6,4},{5,7},{7,5},{8,10},{10,8},{9,1... | collective-permute-start | bytes 1179656 | tf_op jit(solution)/shard_map/ppermute | solution.py:303
  104.1 6.2 %collective-permute-start.9 = (f32[16,48,128]{2,1,0:T(8,128)S(1)}, f32[16,48,128]{2,1,0:T(8,128)S(1)}, u32[]{:S(2)}, u32[]{:S(2)}) collective-permute-start(f32[16,48,128]{2,1,0:T(8,128)S(1)} %all_to_all.28.mine_ref), channel_id=1, source_target_pairs={{0,2},{2,0},{1,3},{3,1},{4,6},{6,4},{5,7},{7,5},{8,10},{10,8},{9,1... | collective-permute-start | bytes 1179656 | tf_op jit(solution)/shard_map/ppermute | solution.py:303

commit v6 on v5

--- a/solution.py
+++ b/solution.py
@@ -32,14 +32,13 @@
 I32 = jnp.int32
 
 
-def call(kernel, outs, *args, smem=(), scratch=(), first=False, last=(), alias={}):
+def call(kernel, outs, *args, scratch=(), first=False, last=(), alias={}):
     specs = [
-        pl.BlockSpec(memory_space=pltpu.SMEM if i in smem else pl.ANY if i in alias else pltpu.VMEM)
-        for i in range(len(args))
+        pl.BlockSpec(memory_space=pl.ANY if i in alias else pltpu.VMEM) for i in range(len(args))
     ]
     if not first:
         args = [
-            a if i in smem or i in alias else pltpu.with_memory_space_constraint(a, pltpu.VMEM)
+            a if i in alias else pltpu.with_memory_space_constraint(a, pltpu.VMEM)
             for i, a in enumerate(args)
         ]
     shapes = [
@@ -57,11 +56,27 @@
     )(*args)
 
 
+def place_of():
+    return lax.axis_index(FAR), lax.axis_index(QUAD), lax.axis_index("mp")
+
+
+def start_of(window_ref):
+    g, q, mp = place_of()
+    lane = lax.broadcasted_iota(I32, (1, ROWS), 1)
+    block = jnp.where(lane == g * N_QUAD + q, window_ref[...], 0)
+    return jnp.sum(block, axis=1, keepdims=True) * A_DEV + mp * HALF
+
+
 def dot(a, b, dims):
     return lax.dot_general(a, b, (dims, ((), ())), preferred_element_type=F32)
 
 
-def forward(x_ref, w_in_ref, b_ref, w_out_ref, part_ref, pre_ref, hid_ref):
+def forward(
+    x_ref, w_in_ref, b_ref, w_out_ref, *refs
+):
+    partner_ref, window_ref, part_ref, pre_ref, hid_ref, partner_out_ref, window_out_ref = refs
+    partner_out_ref[...] = partner_ref[...]
+    window_out_ref[...] = window_ref[...]
     pre = dot(x_ref[...], w_in_ref[...], ((1,), (0,))) + b_ref[...]
     hidden = (pre * jax.nn.sigmoid(pre)).astype(BF16)
     pre_ref[...] = pre
@@ -73,30 +88,34 @@
     return jnp.sqrt(jnp.sum(proj * proj, axis=1, keepdims=True) + EPS)
 
 
-def embed(at_ref, window_ref, part_ref, other_ref, partner_ref, emb_ref, msg_ref, hold_ref):
-    g, q, mp = at_ref[0], at_ref[1], at_ref[2]
+def embed(window_ref, part_ref, other_ref, partner_ref, emb_ref, msg_ref):
+    g, q, mp = place_of()
     proj = part_ref[...] + other_ref[...]
-    emb = (proj / norm_of(proj)).astype(BF16)
-    emb_ref[...] = emb
-    hold_ref[...] = emb.astype(F32)
-    start = pl.multiple_of(window_ref[g * N_QUAD + q] * A_DEV + mp * HALF, HALF)
-    chosen = hold_ref[pl.ds(start, HALF), :]
+    rounded = (proj / norm_of(proj)).astype(BF16)
+    emb_ref[...] = rounded
+    emb = rounded.astype(F32)
+    start = start_of(window_ref)
     to = (g % 8) * HALF
     lane = lax.broadcasted_iota(I32, (8, ROWS), 1)
     row = lax.broadcasted_iota(I32, (8, ROWS), 0)
     partner = jnp.broadcast_to(partner_ref[...], (8, ROWS))
-    value = jnp.where(
+    ids = jnp.where(
         row == 0, partner // ROWS, jnp.where(row == 1, partner % ROWS, lane)
     ).astype(F32)
-    value = pltpu.roll(value, (to - start + ROWS) % ROWS, axis=1)
-    value = jnp.where((lane >= to) & (lane < to + HALF) & (row < 3), value, 0.0)
+    chosen = jnp.zeros((HALF, EMB), F32)
+    value = jnp.zeros((8, ROWS), F32)
+    for at in range(0, ROWS, HALF):
+        chosen = chosen + jnp.where(start == at, emb[at : at + HALF], 0.0)
+        value = value + jnp.where(start == at, pltpu.roll(ids, (ROWS - at) % ROWS, axis=1), 0.0)
+    value = jnp.where((lane < HALF) & (row < 3), value, 0.0)
+    value = pltpu.roll(value, to, axis=1)
     message = jnp.concatenate([chosen, value], axis=0).astype(BF16)
     for i in range(N_FAR):
         msg_ref[i] = message
 
 
-def block_ids(at_ref, msg_ref):
-    g, q = at_ref[0], at_ref[1]
+def block_ids(msg_ref):
+    _, q, _ = place_of()
     ids = msg_ref[:, HALF:, :].astype(F32)
     ids = ids.reshape(N_FAR // 8, 8, 8, ROWS).sum(axis=1)
     ids = jnp.concatenate([ids[i] for i in range(N_FAR // 8)], axis=1)
@@ -106,8 +125,8 @@
     return partner, own
 
 
-def column_ids(at_ref, r):
-    g, q = at_ref[0], at_ref[1]
+def column_ids(r):
+    g, q, _ = place_of()
     base = (g * N_QUAD + (q ^ r)) * ROWS
     return base + lax.broadcasted_iota(I32, (ROWS, 1), 0)
 
@@ -120,9 +139,9 @@
     return jnp.sum(anchors.astype(F32), axis=0, keepdims=True) * (1.0 / ANCHORS)
 
 
-def block_sums(at_ref, msg_ref, e0_ref, e1_ref, e2_ref, e3_ref, out_ref):
+def block_sums(msg_ref, e0_ref, e1_ref, e2_ref, e3_ref, out_ref):
     anchors = anchors_of(msg_ref)
-    partner, own = block_ids(at_ref, msg_ref)
+    partner, own = block_ids(msg_ref)
     total = jnp.zeros((1, ANCHORS), F32)
     rows = jnp.zeros((ANCHORS, 2 * EMB), F32)
     pairs = jnp.zeros((ANCHORS, EMB), F32)
@@ -130,7 +149,7 @@
     for r, e_ref in enumerate((e0_ref, e1_ref, e2_ref, e3_ref)):
         cols_emb = e_ref[...]
         s = dot(cols_emb, anchors, ((1,), (1,)))
-        cols = column_ids(at_ref, r)
+        cols = column_ids(r)
         positive = cols == partner
         ex = jnp.where(cols == own, 0.0, jnp.exp2(s * (INV_TEMP * LOG2E) - SHIFT * LOG2E))
         total = total + jnp.sum(ex, axis=0, keepdims=True)
@@ -155,24 +174,24 @@
 
 
 def weights(
-    at_ref, msg_ref, sums_ref, e0_ref, e1_ref, e2_ref, e3_ref, keep_ref, send_ref
+    msg_ref, sums_ref, e0_ref, e1_ref, e2_ref, e3_ref, keep_ref, send_ref
 ):
     anchors = anchors_of(msg_ref)
-    partner, own = block_ids(at_ref, msg_ref)
+    partner, own = block_ids(msg_ref)
     total = totals_of(sums_ref)
     total = jnp.concatenate([total[i : i + 1] for i in range(4)], axis=1)
     offset = SHIFT * LOG2E + jnp.log2(total)
     for r, e_ref in enumerate((e0_ref, e1_ref, e2_ref, e3_ref)):
         s = dot(e_ref[...], anchors, ((1,), (1,)))
-        cols = column_ids(at_ref, r)
+        cols = column_ids(r)
         prob = jnp.where(cols == own, 0.0, jnp.exp2(s * (INV_TEMP * LOG2E) - offset))
         w = jnp.where(cols == partner, prob - 1.0, prob).astype(BF16)
         c_ref = send_ref if r % 2 else keep_ref
         c_ref[r // 2] = dot(w, anchors, ((1,), (0,)))
 
 
-def own_rows(at_ref, msg_ref, sums_ref, out_ref):
-    g, mp = at_ref[0], at_ref[2]
+def own_rows(msg_ref, sums_ref, out_ref):
+    g, _, mp = place_of()
     line = lax.broadcasted_iota(I32, (4, ROWS), 0)
     total = jnp.sum(jnp.where(line == g // 8, totals_of(sums_ref), 0.0), axis=0, keepdims=True)
     total = jnp.broadcast_to(total, (HALF, ROWS))
@@ -194,17 +213,17 @@
     out_ref[0:HALF, :] = rows / total_of + weight * pair
 
 
-def add_pair(at_ref, window_ref, a_ref, b_ref, rows_ref, mine_ref, next_ref):
-    g, q, mp = at_ref[0], at_ref[1], at_ref[2]
-    mine_ref[0:ROWS, :] = a_ref[0] + b_ref[0]
+def add_pair(window_ref, a_ref, b_ref, rows_ref, mine_ref, next_ref):
     next_ref[...] = a_ref[1] + b_ref[1]
-    start = pl.multiple_of(window_ref[g * N_QUAD + q] * A_DEV + mp * HALF, HALF)
-    mine_ref[pl.ds(start, HALF), :] = mine_ref[pl.ds(start, HALF), :] + rows_ref[0:HALF, :]
+    start = start_of(window_ref)
+    rows = rows_ref[0:HALF, :]
+    for at in range(0, ROWS, HALF):
+        here = slice(at, at + HALF)
+        mine_ref[here, :] = a_ref[0, here] + b_ref[0, here] + jnp.where(start == at, rows, 0.0)
     mine_ref[ROWS:, :] = rows_ref[HALF:, :]
 
 
 def backward(
-    at_ref,
     mine_ref,
     theirs_ref,
     third_ref,
@@ -236,7 +255,7 @@
     grad_in = dot(x_ref[...], grad_pre, ((0,), (0,)))
     bias = jnp.sum(grad_pre.astype(F32), axis=0, keepdims=True)
     first = lax.broadcasted_iota(I32, (8, 128), 0) == 0
-    c = at_ref[1] % 2
+    c = lax.axis_index("c")
 
     def store(half, out_ref):
         lanes = slice(half * 128, half * 128 + 128)
@@ -275,8 +294,8 @@
     return copies
 
 
-def place_mine(at_ref, mine_ref, loss_in_ref, w_in_ref, w_out_ref, loss_ref, sems):
-    copies = place(at_ref[1] % 2, mine_ref, w_in_ref, w_out_ref, sems)
+def place_mine(mine_ref, loss_in_ref, w_in_ref, w_out_ref, loss_ref, sems):
+    copies = place(lax.axis_index("c"), mine_ref, w_in_ref, w_out_ref, sems)
     copies.append(pltpu.make_async_copy(loss_in_ref, loss_ref, sems.at[2]))
     copies[-1].start()
     for copy in copies:
@@ -284,9 +303,9 @@
 
 
 def place_theirs(
-    at_ref, mine_ref, theirs_ref, _, __, w_in_ref, w_out_ref, b_ref, bias_ref, sems
+    mine_ref, theirs_ref, _, __, w_in_ref, w_out_ref, b_ref, bias_ref, sems
 ):
-    c = at_ref[1] % 2
+    c = lax.axis_index("c")
     copies = place(1 - c, theirs_ref, w_in_ref, w_out_ref, sems)
     own, other = mine_ref[0, 40:41, :], theirs_ref[0, 40:41, :]
     bias_ref[0:1, :] = jnp.where(c == 0, own, other)
@@ -308,47 +327,42 @@
 
 
 def on_device(features, w_in, b_in, w_out, partner, window):
-    at = jnp.stack([lax.axis_index(FAR), lax.axis_index(QUAD), lax.axis_index("mp")]).astype(I32)
-    part, pre, hidden = call(
+    line = (1, ROWS)
+    part, pre, hidden, partner, window = call(
         forward,
-        [((ROWS, EMB), F32), ((ROWS, 256), F32), ((ROWS, 256), BF16)],
+        [((ROWS, EMB), F32), ((ROWS, 256), F32), ((ROWS, 256), BF16), (line, I32), (line, I32)],
         features,
         w_in,
         b_in.reshape(1, -1),
         w_out,
+        partner.reshape(line),
+        window.reshape(line),
         first=True,
     )
     other = swap(part, "mp", 1)
     emb, message = call(
         embed,
         [((ROWS, EMB), BF16), ((N_FAR, MSG, EMB), BF16)],
-        at,
         window,
         part,
         other,
-        partner.reshape(1, -1),
-        smem=(0, 1),
-        scratch=[pltpu.VMEM((ROWS, EMB), F32)],
+        partner,
     )
     anchors = exchange(message, FAR)
     blocks = [emb] + [swap(emb, QUAD, r) for r in (1, 2, 3)]
-    (sums,) = call(block_sums, [((N_FAR, 40, EMB), BF16)], at, anchors, *blocks, smem=(0,))
+    (sums,) = call(block_sums, [((N_FAR, 40, EMB), BF16)], anchors, *blocks)
     sums = exchange(sums, FAR)
     pair = (2, ROWS, EMB)
-    keep, send = call(
-        weights, [(pair, F32), (pair, F32)], at, anchors, sums, *blocks, smem=(0,)
-    )
+    keep, send = call(weights, [(pair, F32), (pair, F32)], anchors, sums, *blocks)
     got = swap(send, "c", 1)
-    (rows,) = call(own_rows, [((HALF + 8, EMB), F32)], at, anchors, sums, smem=(0,))
+    (rows,) = call(own_rows, [((HALF + 8, EMB), F32)], anchors, sums)
     mine, away = call(
         add_pair,
         [((ROWS + 8, EMB), F32), ((ROWS, EMB), F32)],
-        at,
         window,
         keep,
         got,
         rows,
-        smem=(0, 1),
     )
     third = swap(away, "yh", 1)
     fourth = swap(away, ("yh", "mp"), 3)
@@ -357,7 +371,6 @@
     row_loss, keep, send = call(
         backward,
         [((1, A_DEV), F32), (half, F32), (half, F32)],
-        at,
         mine,
         theirs,
         third,
@@ -368,7 +381,6 @@
         hidden,
         features,
         w_out,
-        smem=(0,),
     )
     got = swap(send, "c", 1)
     (both,) = call(add, [(half, F32)], keep, got)
@@ -381,24 +393,20 @@
     *grads, row_loss = call(
         place_mine,
         whole + [((1, A_DEV), F32)],
-        at,
         both,
         row_loss,
-        smem=(0,),
         scratch=sems,
         last=(0, 1, 2),
     )
     grad_in, grad_out, grad_b = call(
         place_theirs,
         whole + [((2, 128), F32)],
-        at,
         both,
         got,
         *grads,
-        smem=(0,),
         scratch=[pltpu.VMEM((2, 128), F32)] + sems,
         last=(0, 1, 2),
-        alias={3: 0, 4: 1},
+        alias={2: 0, 3: 1},
     )
     return (
         row_loss.reshape(-1),

time: 112 us -> 108 us (0.964)
  Pallas kernels: 12.1 us -> 6.81 us
  waiting for transfers between devices: 10.4 us -> 12.2 us
    pallas_call x12, Pallas kernels: 12.1 us -> 6.81 us  [call(): pl.pallas_call(kernel, out_shape=shapes, in_specs=specs, out_specs=[pl.Bl...]
    ppermute x10, waiting for transfers between devices: 10.4 us -> 12.2 us  [swap(): return lax.ppermute(value, axes, [(i, i ^ flip) for i in range(count)])]
  transfers between devices with their start and end apart: 11 -> 11, of which waited for: 7 -> 8; matrix products, arithmetic and copies ran while one was open for 1% -> 0% of each run, Pallas kernels for 2% -> 1%
where the time goes in v6:
time: 108 us
  blocking collectives  56.3 us (52%)
  starting transfers between devices  31.6 us (29%)
  waiting for transfers between devices  12.2 us (11%)
  Pallas kernels  6.81 us (6%)
    all_to_all x4, blocking collectives, exchange(): return lax.all_to_all(value, axes, 0, 0, tiled=True)  56.3 us
    ppermute x10, starting transfers between devices, swap(): return lax.ppermute(value, axes, [(i, i ^ flip) for i in range(count)])  20.4 us
    ppermute x10, waiting for transfers between devices, swap(): return lax.ppermute(value, axes, [(i, i ^ flip) for i in range(count)])  12.2 us
    all_to_all x1, starting transfers between devices, exchange(): return lax.all_to_all(value, axes, 0, 0, tiled=True)  11.2 us
    pallas_call x12, Pallas kernels, call(): pl.pallas_call(kernel, out_shape=shapes, in_specs=specs, out_specs=[pl.Bl...  6.81 us
  transfers between devices with their start and end apart: 11, of which 8 were waited for; matrix products, arithmetic and copies ran while one was open for 0% of the time, Pallas kernels for 1%

profile of v6, /device:TPU:1, one launch (start us, length us, event | category | flops | bytes accessed | tf_op | source)
XLA Modules:
  0.0 107.6 jit_solution(14927170302387177394)
XLA Ops:
  0.6 1.4 %shard_map.93 = (f32[128,128]{1,0:T(8,128)S(1)}, f32[128,256]{1,0:T(8,128)S(1)}, bf16[128,256]{1,0:T(8,128)(2,1)S(1)}, s32[1,128]{1,0:T(1,128)S(1)}, s32[1,128]{1,0:T(1,128)S(1)}) custom-call(bf16[128,512]{1,0:T(8,128)(2,1)} %x_ref.3, bf16[512,256]{1,0:T(8,128)(2,1)} %w_in_ref.1, f32[1,256]{1,0:T(1,128)} %bitcast.9, bf16[256,128]{1,0:T(8,128)(2,1)} %w_out_ref.3, ...), custom_call_target="tpu_custom_call" | custom-call | tf_op jit(solution)/shard_map/pallas_call | solution.py:47
  2.0 2.2 %collective-permute-start = (f32[128,128]{1,0:T(8,128)S(1)}, f32[128,128]{1,0:T(8,128)S(1)}, u32[]{:S(2)}, u32[]{:S(2)}) collective-permute-start(f32[128,128]{1,0:T(8,128)S(1)} %get-tuple-element.25.part_ref), channel_id=1, source_target_pairs={{0,1},{1,0},{2,3},{3,2},{4,5},{5,4},{6,7},{7,6},{8,9},{9,8},{10,11... | collective-permute-start | bytes 196616 | tf_op jit(solution)/shard_map/ppermute | solution.py:322
  4.2 1.7 %collective-permute-done.other_ref = f32[128,128]{1,0:T(8,128)S(1)} collective-permute-done((f32[128,128]{1,0:T(8,128)S(1)}, f32[128,128]{1,0:T(8,128)S(1)}, u32[]{:S(2)}, u32[]{:S(2)}) %collective-permute-start) | collective-permute-done | bytes 65568 | tf_op jit(solution)/shard_map/ppermute | solution.py:322
  5.9 0.9 shard_map.94
  6.7 11.2 %all-to-all-start = ((bf16[32,24,128]{2,1,0:T(8,128)(2,1)}), bf16[32,24,128]{2,1,0:T(8,128)(2,1)S(1)}, u32[]{:S(2)}, u32[]{:S(2)}) async-start(bf16[32,24,128]{2,1,0:T(8,128)(2,1)} %get-tuple-element.27), calls=%async_computation | async-start | bytes 393216 | tf_op jit(solution)/shard_map/all_to_all | solution.py:326
  17.9 2.2 %collective-permute-start.1 = (bf16[128,128]{1,0:T(8,128)(2,1)S(1)}, bf16[128,128]{1,0:T(8,128)(2,1)S(1)}, u32[]{:S(2)}, u32[]{:S(2)}) collective-permute-start(bf16[128,128]{1,0:T(8,128)(2,1)S(1)} %get-tuple-element.28.e0_ref), channel_id=1, source_target_pairs={{0,2},{2,0},{4,6},{6,4},{1,3},{3,1},{5,7},{7,5},{8,10},{10,8},{12,... | collective-permute-start | bytes 98312 | tf_op jit(solution)/shard_map/ppermute | solution.py:322
  20.1 2.9 %collective-permute-start.2 = (bf16[128,128]{1,0:T(8,128)(2,1)S(1)}, bf16[128,128]{1,0:T(8,128)(2,1)S(1)}, u32[]{:S(2)}, u32[]{:S(2)}) collective-permute-start(bf16[128,128]{1,0:T(8,128)(2,1)S(1)} %get-tuple-element.28.e0_ref), channel_id=1, source_target_pairs={{0,4},{2,6},{4,0},{6,2},{1,5},{3,7},{5,1},{7,3},{8,12},{10,14},{12... | collective-permute-start | bytes 98312 | tf_op jit(solution)/shard_map/ppermute | solution.py:322
  23.4 1.3 %collective-permute-done.2.e2_ref = bf16[128,128]{1,0:T(8,128)(2,1)S(1)} collective-permute-done((bf16[128,128]{1,0:T(8,128)(2,1)S(1)}, bf16[128,128]{1,0:T(8,128)(2,1)S(1)}, u32[]{:S(2)}, u32[]{:S(2)}) %collective-permute-start.2) | collective-permute-done | bytes 32800 | tf_op jit(solution)/shard_map/ppermute | solution.py:322
  24.7 3.5 %collective-permute-done.3.e3_ref = bf16[128,128]{1,0:T(8,128)(2,1)S(1)} collective-permute-done((bf16[128,128]{1,0:T(8,128)(2,1)S(1)}, bf16[128,128]{1,0:T(8,128)(2,1)S(1)}, u32[]{:S(2)}, u32[]{:S(2)}) %collective-permute-start.3) | collective-permute-done | bytes 32800 | tf_op jit(solution)/shard_map/ppermute | solution.py:322
  28.2 1.1 %shard_map.95 = bf16[32,40,128]{2,1,0:T(8,128)(2,1)S(1)} custom-call(bf16[32,24,128]{2,1,0:T(8,128)(2,1)S(1)} %all-to-all-done.msg_ref, bf16[128,128]{1,0:T(8,128)(2,1)S(1)} %get-tuple-element.28.e0_ref, bf16[128,128]{1,0:T(8,128)(2,1)S(1)} %collective-permute-done.1.e1_ref, bf16[128,128]{1,0:T(8,128)(2,1)S(1)} %collective-permute-done.2.e2_ref, ...), custom_call_target="tpu_custom_call" | custom-call | tf_op jit(solution)/shard_map/pallas_call | solution.py:47
  29.4 21.8 %all_to_all.25.sums_ref = bf16[32,40,128]{2,1,0:T(8,128)(2,1)S(1)} all-to-all(bf16[32,40,128]{2,1,0:T(8,128)(2,1)S(1)} %shard_map.95), channel_id=1, replica_groups=mesh['zh'=4,'zl'=2,'x'=4,'yh'=2,'c'=2,'mp'=2] {'zh','zl','x'}, dimensions={0} | all-to-all | bytes 655360 | tf_op jit(solution)/shard_map/all_to_all | solution.py:326
  51.1 0.9 shard_map.96
  52.1 2.5 %collective-permute-start.4 = (f32[2,128,128]{2,1,0:T(8,128)S(1)}, f32[2,128,128]{2,1,0:T(8,128)S(1)}, u32[]{:S(2)}, u32[]{:S(2)}) collective-permute-start(f32[2,128,128]{2,1,0:T(8,128)S(1)} %get-tuple-element.30), channel_id=1, source_target_pairs={{0,2},{2,0},{1,3},{3,1},{4,6},{6,4},{5,7},{7,5},{8,10},{10,8},{9,1... | collective-permute-start | bytes 393224 | tf_op jit(solution)/shard_map/ppermute | solution.py:322
  54.7 0.8 collective-permute-done.4.b_ref
  56.1 1.6 %collective-permute-start.6 = (f32[128,128]{1,0:T(8,128)S(1)}, f32[128,128]{1,0:T(8,128)S(1)}, u32[]{:S(2)}, u32[]{:S(2)}) collective-permute-start(f32[128,128]{1,0:T(8,128)S(1)} %get-tuple-element.32), channel_id=1, source_target_pairs={{0,4},{4,0},{1,5},{5,1},{2,6},{6,2},{3,7},{7,3},{8,12},{12,8},{9,1... | collective-permute-start | bytes 196616 | tf_op jit(solution)/shard_map/ppermute | solution.py:322
  57.7 1.9 %collective-permute-start.7 = (f32[128,128]{1,0:T(8,128)S(1)}, f32[128,128]{1,0:T(8,128)S(1)}, u32[]{:S(2)}, u32[]{:S(2)}) collective-permute-start(f32[128,128]{1,0:T(8,128)S(1)} %get-tuple-element.32), channel_id=1, source_target_pairs={{0,5},{1,4},{4,1},{5,0},{2,7},{3,6},{6,3},{7,2},{8,13},{9,12},{12,... | collective-permute-start | bytes 196616 | tf_op jit(solution)/shard_map/ppermute | solution.py:322
  59.6 1.3 %collective-permute-done.6.third_ref = f32[128,128]{1,0:T(8,128)S(1)} collective-permute-done((f32[128,128]{1,0:T(8,128)S(1)}, f32[128,128]{1,0:T(8,128)S(1)}, u32[]{:S(2)}, u32[]{:S(2)}) %collective-permute-start.6) | collective-permute-done | bytes 65568 | tf_op jit(solution)/shard_map/ppermute | solution.py:322
  60.9 1.6 %collective-permute-done.7.fourth_ref = f32[128,128]{1,0:T(8,128)S(1)} collective-permute-done((f32[128,128]{1,0:T(8,128)S(1)}, f32[128,128]{1,0:T(8,128)S(1)}, u32[]{:S(2)}, u32[]{:S(2)}) %collective-permute-start.7) | collective-permute-done | bytes 65568 | tf_op jit(solution)/shard_map/ppermute | solution.py:322
  63.2 1.6 %collective-permute-start.8 = (f32[16,48,128]{2,1,0:T(8,128)S(1)}, f32[16,48,128]{2,1,0:T(8,128)S(1)}, u32[]{:S(2)}, u32[]{:S(2)}) collective-permute-start(f32[16,48,128]{2,1,0:T(8,128)S(1)} %get-tuple-element.36), channel_id=1, source_target_pairs={{0,2},{2,0},{1,3},{3,1},{4,6},{6,4},{5,7},{7,5},{8,10},{10,8},{9,1... | collective-permute-start | bytes 1179656 | tf_op jit(solution)/shard_map/ppermute | solution.py:322
  64.8 1.3 %collective-permute-done.8.b_ref = f32[16,48,128]{2,1,0:T(8,128)S(1)} collective-permute-done((f32[16,48,128]{2,1,0:T(8,128)S(1)}, f32[16,48,128]{2,1,0:T(8,128)S(1)}, u32[]{:S(2)}, u32[]{:S(2)}) %collective-permute-start.8) | collective-permute-done | bytes 393248 | tf_op jit(solution)/shard_map/ppermute | solution.py:322
  66.2 12.2 %all_to_all.26.in_ref = f32[16,48,128]{2,1,0:T(8,128)S(1)} all-to-all(f32[16,48,128]{2,1,0:T(8,128)S(1)} %shard_map.100), channel_id=1, replica_groups=mesh['zh'=4,'zl'=2,'x'=4,'yh'=2,'c'=2,'mp'=2] {'zl','x','yh'}, dimensions={0} | all-to-all | bytes 786432 | tf_op jit(solution)/shard_map/all_to_all | solution.py:326
  78.5 9.7 %all_to_all.27.in_ref = f32[4,48,128]{2,1,0:T(8,128)S(1)} all-to-all(f32[4,48,128]{2,1,0:T(8,128)S(1)} %shard_map.101), channel_id=1, replica_groups=mesh['zh'=4,'zl'=2,'x'=4,'yh'=2,'c'=2,'mp'=2] {'zh'}, dimensions={0} | all-to-all | bytes 196608 | tf_op jit(solution)/shard_map/all_to_all | solution.py:326
  88.2 12.6 %all_to_all.28.mine_ref = f32[16,48,128]{2,1,0:T(8,128)S(1)} all-to-all(f32[16,48,128]{2,1,0:T(8,128)S(1)} %shard_map.102), channel_id=1, replica_groups=mesh['zh'=4,'zl'=2,'x'=4,'yh'=2,'c'=2,'mp'=2] {'zl','x','yh'}, dimensions={0} | all-to-all | bytes 786432 | tf_op jit(solution)/shard_map/all_to_all | solution.py:326
  100.8 4.8 %collective-permute-start.9 = (f32[16,48,128]{2,1,0:T(8,128)S(1)}, f32[16,48,128]{2,1,0:T(8,128)S(1)}, u32[]{:S(2)}, u32[]{:S(2)}) collective-permute-start(f32[16,48,128]{2,1,0:T(8,128)S(1)} %all_to_all.28.mine_ref), channel_id=1, source_target_pairs={{0,2},{2,0},{1,3},{3,1},{4,6},{6,4},{5,7},{7,5},{8,10},{10,8},{9,1... | collective-permute-start | bytes 1179656 | tf_op jit(solution)/shard_map/ppermute | solution.py:322
  (18 shorter events, 3.9 us)
Async XLA Ops:
  2.0 3.9 %collective-permute-start = (f32[128,128]{1,0:T(8,128)S(1)}, f32[128,128]{1,0:T(8,128)S(1)}, u32[]{:S(2)}, u32[]{:S(2)}) collective-permute-start(f32[128,128]{1,0:T(8,128)S(1)} %get-tuple-element.25.part_ref), channel_id=1, source_target_pairs={{0,1},{1,0},{2,3},{3,2},{4,5},{5,4},{6,7},{7,6},{8,9},{9,8},{10,11... | collective-permute-start | bytes 196616 | tf_op jit(solution)/shard_map/ppermute | solution.py:322
  6.7 21.5 %all-to-all-start = ((bf16[32,24,128]{2,1,0:T(8,128)(2,1)}), bf16[32,24,128]{2,1,0:T(8,128)(2,1)S(1)}, u32[]{:S(2)}, u32[]{:S(2)}) async-start(bf16[32,24,128]{2,1,0:T(8,128)(2,1)} %get-tuple-element.27), calls=%async_computation | async-start | bytes 393216 | tf_op jit(solution)/shard_map/all_to_all | solution.py:326
  17.9 5.4 %collective-permute-start.1 = (bf16[128,128]{1,0:T(8,128)(2,1)S(1)}, bf16[128,128]{1,0:T(8,128)(2,1)S(1)}, u32[]{:S(2)}, u32[]{:S(2)}) collective-permute-start(bf16[128,128]{1,0:T(8,128)(2,1)S(1)} %get-tuple-element.28.e0_ref), channel_id=1, source_target_pairs={{0,2},{2,0},{4,6},{6,4},{1,3},{3,1},{5,7},{7,5},{8,10},{10,8},{12,... | collective-permute-start | bytes 98312 | tf_op jit(solution)/shard_map/ppermute | solution.py:322
  20.1 4.6 %collective-permute-start.2 = (bf16[128,128]{1,0:T(8,128)(2,1)S(1)}, bf16[128,128]{1,0:T(8,128)(2,1)S(1)}, u32[]{:S(2)}, u32[]{:S(2)}) collective-permute-start(bf16[128,128]{1,0:T(8,128)(2,1)S(1)} %get-tuple-element.28.e0_ref), channel_id=1, source_target_pairs={{0,4},{2,6},{4,0},{6,2},{1,5},{3,7},{5,1},{7,3},{8,12},{10,14},{12... | collective-permute-start | bytes 98312 | tf_op jit(solution)/shard_map/ppermute | solution.py:322
  23.1 5.2 %collective-permute-start.3 = (bf16[128,128]{1,0:T(8,128)(2,1)S(1)}, bf16[128,128]{1,0:T(8,128)(2,1)S(1)}, u32[]{:S(2)}, u32[]{:S(2)}) collective-permute-start(bf16[128,128]{1,0:T(8,128)(2,1)S(1)} %get-tuple-element.28.e0_ref), channel_id=1, source_target_pairs={{0,6},{2,4},{4,2},{6,0},{1,7},{3,5},{5,3},{7,1},{8,14},{10,12},{12... | collective-permute-start | bytes 98312 | tf_op jit(solution)/shard_map/ppermute | solution.py:322
  52.1 3.5 %collective-permute-start.4 = (f32[2,128,128]{2,1,0:T(8,128)S(1)}, f32[2,128,128]{2,1,0:T(8,128)S(1)}, u32[]{:S(2)}, u32[]{:S(2)}) collective-permute-start(f32[2,128,128]{2,1,0:T(8,128)S(1)} %get-tuple-element.30), channel_id=1, source_target_pairs={{0,2},{2,0},{1,3},{3,1},{4,6},{6,4},{5,7},{7,5},{8,10},{10,8},{9,1... | collective-permute-start | bytes 393224 | tf_op jit(solution)/shard_map/ppermute | solution.py:322
  55.5 7.0 %copy-start = (bf16[128,512]{1,0:T(8,128)(2,1)S(1)}, bf16[128,512]{1,0:T(8,128)(2,1)}, u32[]{:S(2)}) copy-start(bf16[128,512]{1,0:T(8,128)(2,1)} %x_ref.3) | copy-start | bytes 393220
  55.5 7.0 %copy-start.1 = (bf16[256,128]{1,0:T(8,128)(2,1)S(1)}, bf16[256,128]{1,0:T(8,128)(2,1)}, u32[]{:S(2)}) copy-start(bf16[256,128]{1,0:T(8,128)(2,1)} %w_out_ref.3) | copy-start | bytes 196612
  55.7 6.9 %collective-permute-start.5 = (f32[136,128]{1,0:T(8,128)S(1)}, f32[136,128]{1,0:T(8,128)S(1)}, u32[]{:S(2)}, u32[]{:S(2)}) collective-permute-start(f32[136,128]{1,0:T(8,128)S(1)} %get-tuple-element.31.mine_ref), channel_id=1, source_target_pairs={{0,1},{1,0},{2,3},{3,2},{4,5},{5,4},{6,7},{7,6},{8,9},{9,8},{10,11... | collective-permute-start | bytes 208904 | tf_op jit(solution)/shard_map/ppermute | solution.py:322
  56.1 4.8 %collective-permute-start.6 = (f32[128,128]{1,0:T(8,128)S(1)}, f32[128,128]{1,0:T(8,128)S(1)}, u32[]{:S(2)}, u32[]{:S(2)}) collective-permute-start(f32[128,128]{1,0:T(8,128)S(1)} %get-tuple-element.32), channel_id=1, source_target_pairs={{0,4},{4,0},{1,5},{5,1},{2,6},{6,2},{3,7},{7,3},{8,12},{12,8},{9,1... | collective-permute-start | bytes 196616 | tf_op jit(solution)/shard_map/ppermute | solution.py:322
  57.7 4.9 %collective-permute-start.7 = (f32[128,128]{1,0:T(8,128)S(1)}, f32[128,128]{1,0:T(8,128)S(1)}, u32[]{:S(2)}, u32[]{:S(2)}) collective-permute-start(f32[128,128]{1,0:T(8,128)S(1)} %get-tuple-element.32), channel_id=1, source_target_pairs={{0,5},{1,4},{4,1},{5,0},{2,7},{3,6},{6,3},{7,2},{8,13},{9,12},{12,... | collective-permute-start | bytes 196616 | tf_op jit(solution)/shard_map/ppermute | solution.py:322
  63.2 3.0 %collective-permute-start.8 = (f32[16,48,128]{2,1,0:T(8,128)S(1)}, f32[16,48,128]{2,1,0:T(8,128)S(1)}, u32[]{:S(2)}, u32[]{:S(2)}) collective-permute-start(f32[16,48,128]{2,1,0:T(8,128)S(1)} %get-tuple-element.36), channel_id=1, source_target_pairs={{0,2},{2,0},{1,3},{3,1},{4,6},{6,4},{5,7},{7,5},{8,10},{10,8},{9,1... | collective-permute-start | bytes 1179656 | tf_op jit(solution)/shard_map/ppermute | solution.py:322
  100.8 6.1 %collective-permute-start.9 = (f32[16,48,128]{2,1,0:T(8,128)S(1)}, f32[16,48,128]{2,1,0:T(8,128)S(1)}, u32[]{:S(2)}, u32[]{:S(2)}) collective-permute-start(f32[16,48,128]{2,1,0:T(8,128)S(1)} %all_to_all.28.mine_ref), channel_id=1, source_target_pairs={{0,2},{2,0},{1,3},{3,1},{4,6},{6,4},{5,7},{7,5},{8,10},{10,8},{9,1... | collective-permute-start | bytes 1179656 | tf_op jit(solution)/shard_map/ppermute | solution.py:322

commit v7 on v6

--- a/solution.py
+++ b/solution.py
@@ -6,9 +6,10 @@
 from jax.sharding import Mesh
 from jax.sharding import PartitionSpec as P
 
+
 SIZES = {"zh": 4, "zl": 2, "x": 4, "yh": 2, "c": 2}
 DP = ("zh", "zl", "x", "yh", "c")
-NEAR = ("zl", "x", "yh")
+NEAR = ("yh", "x", "zl")
 FAR = ("zh", "zl", "x")
 QUAD = ("yh", "c")
 
@@ -41,9 +42,7 @@
             a if i in alias else pltpu.with_memory_space_constraint(a, pltpu.VMEM)
             for i, a in enumerate(args)
         ]
-    shapes = [
-        jax.ShapeDtypeStruct(s, d) if last else pltpu.VMEM(s, d) for i, (s, d) in enumerate(outs)
-    ]
+    shapes = [jax.ShapeDtypeStruct(s, d) if last else pltpu.VMEM(s, d) for s, d in outs]
     return pl.pallas_call(
         kernel,
         out_shape=shapes,
@@ -89,7 +88,7 @@
 
 
 def embed(window_ref, part_ref, other_ref, partner_ref, emb_ref, msg_ref):
-    g, q, mp = place_of()
+    g, _, _ = place_of()
     proj = part_ref[...] + other_ref[...]
     rounded = (proj / norm_of(proj)).astype(BF16)
     emb_ref[...] = rounded
@@ -364,8 +363,8 @@
         got,
         rows,
     )
+    fourth = swap(away, ("yh", "mp"), 3)
     third = swap(away, "yh", 1)
-    fourth = swap(away, ("yh", "mp"), 3)
     theirs = swap(mine, "mp", 1)
     half = (N_NEAR, PART, EMB)
     row_loss, keep, send = call(

time: 108 us -> 107 us (level)
  no operation moved by 1% of the time
where the time goes in v7:
time: 107 us
  blocking collectives  55.5 us (52%)
  starting transfers between devices  31.6 us (30%)
  waiting for transfers between devices  12.2 us (11%)
  Pallas kernels  6.81 us (6%)
    all_to_all x4, blocking collectives, exchange(): return lax.all_to_all(value, axes, 0, 0, tiled=True)  55.5 us
    ppermute x10, starting transfers between devices, swap(): return lax.ppermute(value, axes, [(i, i ^ flip) for i in range(count)])  20.4 us
    ppermute x10, waiting for transfers between devices, swap(): return lax.ppermute(value, axes, [(i, i ^ flip) for i in range(count)])  12.2 us
    all_to_all x1, starting transfers between devices, exchange(): return lax.all_to_all(value, axes, 0, 0, tiled=True)  11.2 us
    pallas_call x12, Pallas kernels, call(): pl.pallas_call(kernel, out_shape=shapes, in_specs=specs, out_specs=[pl.Bl...  6.81 us
  transfers between devices with their start and end apart: 11, of which 8 were waited for; matrix products, arithmetic and copies ran while one was open for 0% of the time, Pallas kernels for 1%

profile of v7, /device:TPU:1, one launch (start us, length us, event | category | flops | bytes accessed | tf_op | source)
XLA Modules:
  0.0 106.9 jit_solution(7918876888887115479)
XLA Ops:
  0.6 1.4 %shard_map.93 = (f32[128,128]{1,0:T(8,128)S(1)}, f32[128,256]{1,0:T(8,128)S(1)}, bf16[128,256]{1,0:T(8,128)(2,1)S(1)}, s32[1,128]{1,0:T(1,128)S(1)}, s32[1,128]{1,0:T(1,128)S(1)}) custom-call(bf16[128,512]{1,0:T(8,128)(2,1)} %x_ref.3, bf16[512,256]{1,0:T(8,128)(2,1)} %w_in_ref.1, f32[1,256]{1,0:T(1,128)} %bitcast.9, bf16[256,128]{1,0:T(8,128)(2,1)} %w_out_ref.3, ...), custom_call_target="tpu_custom_call" | custom-call | tf_op jit(solution)/shard_map/pallas_call | solution.py:46
  2.0 2.2 %collective-permute-start = (f32[128,128]{1,0:T(8,128)S(1)}, f32[128,128]{1,0:T(8,128)S(1)}, u32[]{:S(2)}, u32[]{:S(2)}) collective-permute-start(f32[128,128]{1,0:T(8,128)S(1)} %get-tuple-element.25.part_ref), channel_id=1, source_target_pairs={{0,1},{1,0},{2,3},{3,2},{4,5},{5,4},{6,7},{7,6},{8,9},{9,8},{10,11... | collective-permute-start | bytes 196616 | tf_op jit(solution)/shard_map/ppermute | solution.py:321
  4.2 1.7 %collective-permute-done.other_ref = f32[128,128]{1,0:T(8,128)S(1)} collective-permute-done((f32[128,128]{1,0:T(8,128)S(1)}, f32[128,128]{1,0:T(8,128)S(1)}, u32[]{:S(2)}, u32[]{:S(2)}) %collective-permute-start) | collective-permute-done | bytes 65568 | tf_op jit(solution)/shard_map/ppermute | solution.py:321
  5.9 0.9 shard_map.94
  6.7 11.2 %all-to-all-start = ((bf16[32,24,128]{2,1,0:T(8,128)(2,1)}), bf16[32,24,128]{2,1,0:T(8,128)(2,1)S(1)}, u32[]{:S(2)}, u32[]{:S(2)}) async-start(bf16[32,24,128]{2,1,0:T(8,128)(2,1)} %get-tuple-element.27), calls=%async_computation | async-start | bytes 393216 | tf_op jit(solution)/shard_map/all_to_all | solution.py:325
  17.9 2.2 %collective-permute-start.1 = (bf16[128,128]{1,0:T(8,128)(2,1)S(1)}, bf16[128,128]{1,0:T(8,128)(2,1)S(1)}, u32[]{:S(2)}, u32[]{:S(2)}) collective-permute-start(bf16[128,128]{1,0:T(8,128)(2,1)S(1)} %get-tuple-element.28.e0_ref), channel_id=1, source_target_pairs={{0,2},{2,0},{4,6},{6,4},{1,3},{3,1},{5,7},{7,5},{8,10},{10,8},{12,... | collective-permute-start | bytes 98312 | tf_op jit(solution)/shard_map/ppermute | solution.py:321
  20.1 2.9 %collective-permute-start.2 = (bf16[128,128]{1,0:T(8,128)(2,1)S(1)}, bf16[128,128]{1,0:T(8,128)(2,1)S(1)}, u32[]{:S(2)}, u32[]{:S(2)}) collective-permute-start(bf16[128,128]{1,0:T(8,128)(2,1)S(1)} %get-tuple-element.28.e0_ref), channel_id=1, source_target_pairs={{0,4},{2,6},{4,0},{6,2},{1,5},{3,7},{5,1},{7,3},{8,12},{10,14},{12... | collective-permute-start | bytes 98312 | tf_op jit(solution)/shard_map/ppermute | solution.py:321
  23.4 1.3 %collective-permute-done.2.e2_ref = bf16[128,128]{1,0:T(8,128)(2,1)S(1)} collective-permute-done((bf16[128,128]{1,0:T(8,128)(2,1)S(1)}, bf16[128,128]{1,0:T(8,128)(2,1)S(1)}, u32[]{:S(2)}, u32[]{:S(2)}) %collective-permute-start.2) | collective-permute-done | bytes 32800 | tf_op jit(solution)/shard_map/ppermute | solution.py:321
  24.7 3.5 %collective-permute-done.3.e3_ref = bf16[128,128]{1,0:T(8,128)(2,1)S(1)} collective-permute-done((bf16[128,128]{1,0:T(8,128)(2,1)S(1)}, bf16[128,128]{1,0:T(8,128)(2,1)S(1)}, u32[]{:S(2)}, u32[]{:S(2)}) %collective-permute-start.3) | collective-permute-done | bytes 32800 | tf_op jit(solution)/shard_map/ppermute | solution.py:321
  28.2 1.1 %shard_map.95 = bf16[32,40,128]{2,1,0:T(8,128)(2,1)S(1)} custom-call(bf16[32,24,128]{2,1,0:T(8,128)(2,1)S(1)} %all-to-all-done.msg_ref, bf16[128,128]{1,0:T(8,128)(2,1)S(1)} %get-tuple-element.28.e0_ref, bf16[128,128]{1,0:T(8,128)(2,1)S(1)} %collective-permute-done.1.e1_ref, bf16[128,128]{1,0:T(8,128)(2,1)S(1)} %collective-permute-done.2.e2_ref, ...), custom_call_target="tpu_custom_call" | custom-call | tf_op jit(solution)/shard_map/pallas_call | solution.py:46
  29.4 21.8 %all_to_all.25.sums_ref = bf16[32,40,128]{2,1,0:T(8,128)(2,1)S(1)} all-to-all(bf16[32,40,128]{2,1,0:T(8,128)(2,1)S(1)} %shard_map.95), channel_id=1, replica_groups=mesh['zh'=4,'zl'=2,'x'=4,'yh'=2,'c'=2,'mp'=2] {'zh','zl','x'}, dimensions={0} | all-to-all | bytes 655360 | tf_op jit(solution)/shard_map/all_to_all | solution.py:325
  51.1 0.9 shard_map.96
  52.1 2.5 %collective-permute-start.4 = (f32[2,128,128]{2,1,0:T(8,128)S(1)}, f32[2,128,128]{2,1,0:T(8,128)S(1)}, u32[]{:S(2)}, u32[]{:S(2)}) collective-permute-start(f32[2,128,128]{2,1,0:T(8,128)S(1)} %get-tuple-element.30), channel_id=1, source_target_pairs={{0,2},{2,0},{1,3},{3,1},{4,6},{6,4},{5,7},{7,5},{8,10},{10,8},{9,1... | collective-permute-start | bytes 393224 | tf_op jit(solution)/shard_map/ppermute | solution.py:321
  54.7 0.8 collective-permute-done.4.b_ref
  56.1 1.6 %collective-permute-start.6 = (f32[128,128]{1,0:T(8,128)S(1)}, f32[128,128]{1,0:T(8,128)S(1)}, u32[]{:S(2)}, u32[]{:S(2)}) collective-permute-start(f32[128,128]{1,0:T(8,128)S(1)} %get-tuple-element.32), channel_id=1, source_target_pairs={{0,4},{4,0},{1,5},{5,1},{2,6},{6,2},{3,7},{7,3},{8,12},{12,8},{9,1... | collective-permute-start | bytes 196616 | tf_op jit(solution)/shard_map/ppermute | solution.py:321
  57.7 1.9 %collective-permute-start.7 = (f32[128,128]{1,0:T(8,128)S(1)}, f32[128,128]{1,0:T(8,128)S(1)}, u32[]{:S(2)}, u32[]{:S(2)}) collective-permute-start(f32[128,128]{1,0:T(8,128)S(1)} %get-tuple-element.32), channel_id=1, source_target_pairs={{0,5},{1,4},{4,1},{5,0},{2,7},{3,6},{6,3},{7,2},{8,13},{9,12},{12,... | collective-permute-start | bytes 196616 | tf_op jit(solution)/shard_map/ppermute | solution.py:321
  59.6 1.3 %collective-permute-done.6.third_ref = f32[128,128]{1,0:T(8,128)S(1)} collective-permute-done((f32[128,128]{1,0:T(8,128)S(1)}, f32[128,128]{1,0:T(8,128)S(1)}, u32[]{:S(2)}, u32[]{:S(2)}) %collective-permute-start.6) | collective-permute-done | bytes 65568 | tf_op jit(solution)/shard_map/ppermute | solution.py:321
  60.9 1.6 %collective-permute-done.7.fourth_ref = f32[128,128]{1,0:T(8,128)S(1)} collective-permute-done((f32[128,128]{1,0:T(8,128)S(1)}, f32[128,128]{1,0:T(8,128)S(1)}, u32[]{:S(2)}, u32[]{:S(2)}) %collective-permute-start.7) | collective-permute-done | bytes 65568 | tf_op jit(solution)/shard_map/ppermute | solution.py:321
  63.2 1.6 %collective-permute-start.8 = (f32[16,48,128]{2,1,0:T(8,128)S(1)}, f32[16,48,128]{2,1,0:T(8,128)S(1)}, u32[]{:S(2)}, u32[]{:S(2)}) collective-permute-start(f32[16,48,128]{2,1,0:T(8,128)S(1)} %get-tuple-element.36), channel_id=1, source_target_pairs={{0,2},{2,0},{1,3},{3,1},{4,6},{6,4},{5,7},{7,5},{8,10},{10,8},{9,1... | collective-permute-start | bytes 1179656 | tf_op jit(solution)/shard_map/ppermute | solution.py:321
  64.8 1.3 %collective-permute-done.8.b_ref = f32[16,48,128]{2,1,0:T(8,128)S(1)} collective-permute-done((f32[16,48,128]{2,1,0:T(8,128)S(1)}, f32[16,48,128]{2,1,0:T(8,128)S(1)}, u32[]{:S(2)}, u32[]{:S(2)}) %collective-permute-start.8) | collective-permute-done | bytes 393248 | tf_op jit(solution)/shard_map/ppermute | solution.py:321
  66.2 11.4 %all_to_all.26.in_ref = f32[16,48,128]{2,1,0:T(8,128)S(1)} all-to-all(f32[16,48,128]{2,1,0:T(8,128)S(1)} %shard_map.100), channel_id=1, replica_groups=mesh['zh'=4,'zl'=2,'x'=4,'yh'=2,'c'=2,'mp'=2] {'yh','x','zl'}, dimensions={0} | all-to-all | bytes 786432 | tf_op jit(solution)/shard_map/all_to_all | solution.py:325
  77.6 9.7 %all_to_all.27.in_ref = f32[4,48,128]{2,1,0:T(8,128)S(1)} all-to-all(f32[4,48,128]{2,1,0:T(8,128)S(1)} %shard_map.101), channel_id=1, replica_groups=mesh['zh'=4,'zl'=2,'x'=4,'yh'=2,'c'=2,'mp'=2] {'zh'}, dimensions={0} | all-to-all | bytes 196608 | tf_op jit(solution)/shard_map/all_to_all | solution.py:325
  87.3 12.6 %all_to_all.28.mine_ref = f32[16,48,128]{2,1,0:T(8,128)S(1)} all-to-all(f32[16,48,128]{2,1,0:T(8,128)S(1)} %shard_map.102), channel_id=1, replica_groups=mesh['zh'=4,'zl'=2,'x'=4,'yh'=2,'c'=2,'mp'=2] {'yh','x','zl'}, dimensions={0} | all-to-all | bytes 786432 | tf_op jit(solution)/shard_map/all_to_all | solution.py:325
  100.0 4.8 %collective-permute-start.9 = (f32[16,48,128]{2,1,0:T(8,128)S(1)}, f32[16,48,128]{2,1,0:T(8,128)S(1)}, u32[]{:S(2)}, u32[]{:S(2)}) collective-permute-start(f32[16,48,128]{2,1,0:T(8,128)S(1)} %all_to_all.28.mine_ref), channel_id=1, source_target_pairs={{0,2},{2,0},{1,3},{3,1},{4,6},{6,4},{5,7},{7,5},{8,10},{10,8},{9,1... | collective-permute-start | bytes 1179656 | tf_op jit(solution)/shard_map/ppermute | solution.py:321
  (18 shorter events, 3.9 us)
Async XLA Ops:
  2.0 3.9 %collective-permute-start = (f32[128,128]{1,0:T(8,128)S(1)}, f32[128,128]{1,0:T(8,128)S(1)}, u32[]{:S(2)}, u32[]{:S(2)}) collective-permute-start(f32[128,128]{1,0:T(8,128)S(1)} %get-tuple-element.25.part_ref), channel_id=1, source_target_pairs={{0,1},{1,0},{2,3},{3,2},{4,5},{5,4},{6,7},{7,6},{8,9},{9,8},{10,11... | collective-permute-start | bytes 196616 | tf_op jit(solution)/shard_map/ppermute | solution.py:321
  6.7 21.5 %all-to-all-start = ((bf16[32,24,128]{2,1,0:T(8,128)(2,1)}), bf16[32,24,128]{2,1,0:T(8,128)(2,1)S(1)}, u32[]{:S(2)}, u32[]{:S(2)}) async-start(bf16[32,24,128]{2,1,0:T(8,128)(2,1)} %get-tuple-element.27), calls=%async_computation | async-start | bytes 393216 | tf_op jit(solution)/shard_map/all_to_all | solution.py:325
  17.9 5.4 %collective-permute-start.1 = (bf16[128,128]{1,0:T(8,128)(2,1)S(1)}, bf16[128,128]{1,0:T(8,128)(2,1)S(1)}, u32[]{:S(2)}, u32[]{:S(2)}) collective-permute-start(bf16[128,128]{1,0:T(8,128)(2,1)S(1)} %get-tuple-element.28.e0_ref), channel_id=1, source_target_pairs={{0,2},{2,0},{4,6},{6,4},{1,3},{3,1},{5,7},{7,5},{8,10},{10,8},{12,... | collective-permute-start | bytes 98312 | tf_op jit(solution)/shard_map/ppermute | solution.py:321
  20.1 4.6 %collective-permute-start.2 = (bf16[128,128]{1,0:T(8,128)(2,1)S(1)}, bf16[128,128]{1,0:T(8,128)(2,1)S(1)}, u32[]{:S(2)}, u32[]{:S(2)}) collective-permute-start(bf16[128,128]{1,0:T(8,128)(2,1)S(1)} %get-tuple-element.28.e0_ref), channel_id=1, source_target_pairs={{0,4},{2,6},{4,0},{6,2},{1,5},{3,7},{5,1},{7,3},{8,12},{10,14},{12... | collective-permute-start | bytes 98312 | tf_op jit(solution)/shard_map/ppermute | solution.py:321
  23.1 5.2 %collective-permute-start.3 = (bf16[128,128]{1,0:T(8,128)(2,1)S(1)}, bf16[128,128]{1,0:T(8,128)(2,1)S(1)}, u32[]{:S(2)}, u32[]{:S(2)}) collective-permute-start(bf16[128,128]{1,0:T(8,128)(2,1)S(1)} %get-tuple-element.28.e0_ref), channel_id=1, source_target_pairs={{0,6},{2,4},{4,2},{6,0},{1,7},{3,5},{5,3},{7,1},{8,14},{10,12},{12... | collective-permute-start | bytes 98312 | tf_op jit(solution)/shard_map/ppermute | solution.py:321
  52.1 3.5 %collective-permute-start.4 = (f32[2,128,128]{2,1,0:T(8,128)S(1)}, f32[2,128,128]{2,1,0:T(8,128)S(1)}, u32[]{:S(2)}, u32[]{:S(2)}) collective-permute-start(f32[2,128,128]{2,1,0:T(8,128)S(1)} %get-tuple-element.30), channel_id=1, source_target_pairs={{0,2},{2,0},{1,3},{3,1},{4,6},{6,4},{5,7},{7,5},{8,10},{10,8},{9,1... | collective-permute-start | bytes 393224 | tf_op jit(solution)/shard_map/ppermute | solution.py:321
  55.5 7.0 %copy-start = (bf16[128,512]{1,0:T(8,128)(2,1)S(1)}, bf16[128,512]{1,0:T(8,128)(2,1)}, u32[]{:S(2)}) copy-start(bf16[128,512]{1,0:T(8,128)(2,1)} %x_ref.3) | copy-start | bytes 393220
  55.5 7.0 %copy-start.1 = (bf16[256,128]{1,0:T(8,128)(2,1)S(1)}, bf16[256,128]{1,0:T(8,128)(2,1)}, u32[]{:S(2)}) copy-start(bf16[256,128]{1,0:T(8,128)(2,1)} %w_out_ref.3) | copy-start | bytes 196612
  55.7 6.9 %collective-permute-start.5 = (f32[136,128]{1,0:T(8,128)S(1)}, f32[136,128]{1,0:T(8,128)S(1)}, u32[]{:S(2)}, u32[]{:S(2)}) collective-permute-start(f32[136,128]{1,0:T(8,128)S(1)} %get-tuple-element.31.mine_ref), channel_id=1, source_target_pairs={{0,1},{1,0},{2,3},{3,2},{4,5},{5,4},{6,7},{7,6},{8,9},{9,8},{10,11... | collective-permute-start | bytes 208904 | tf_op jit(solution)/shard_map/ppermute | solution.py:321
  56.1 4.8 %collective-permute-start.6 = (f32[128,128]{1,0:T(8,128)S(1)}, f32[128,128]{1,0:T(8,128)S(1)}, u32[]{:S(2)}, u32[]{:S(2)}) collective-permute-start(f32[128,128]{1,0:T(8,128)S(1)} %get-tuple-element.32), channel_id=1, source_target_pairs={{0,4},{4,0},{1,5},{5,1},{2,6},{6,2},{3,7},{7,3},{8,12},{12,8},{9,1... | collective-permute-start | bytes 196616 | tf_op jit(solution)/shard_map/ppermute | solution.py:321
  57.7 4.9 %collective-permute-start.7 = (f32[128,128]{1,0:T(8,128)S(1)}, f32[128,128]{1,0:T(8,128)S(1)}, u32[]{:S(2)}, u32[]{:S(2)}) collective-permute-start(f32[128,128]{1,0:T(8,128)S(1)} %get-tuple-element.32), channel_id=1, source_target_pairs={{0,5},{1,4},{4,1},{5,0},{2,7},{3,6},{6,3},{7,2},{8,13},{9,12},{12,... | collective-permute-start | bytes 196616 | tf_op jit(solution)/shard_map/ppermute | solution.py:321
  63.2 3.0 %collective-permute-start.8 = (f32[16,48,128]{2,1,0:T(8,128)S(1)}, f32[16,48,128]{2,1,0:T(8,128)S(1)}, u32[]{:S(2)}, u32[]{:S(2)}) collective-permute-start(f32[16,48,128]{2,1,0:T(8,128)S(1)} %get-tuple-element.36), channel_id=1, source_target_pairs={{0,2},{2,0},{1,3},{3,1},{4,6},{6,4},{5,7},{7,5},{8,10},{10,8},{9,1... | collective-permute-start | bytes 1179656 | tf_op jit(solution)/shard_map/ppermute | solution.py:321
  100.0 6.1 %collective-permute-start.9 = (f32[16,48,128]{2,1,0:T(8,128)S(1)}, f32[16,48,128]{2,1,0:T(8,128)S(1)}, u32[]{:S(2)}, u32[]{:S(2)}) collective-permute-start(f32[16,48,128]{2,1,0:T(8,128)S(1)} %all_to_all.28.mine_ref), channel_id=1, source_target_pairs={{0,2},{2,0},{1,3},{3,1},{4,6},{6,4},{5,7},{7,5},{8,10},{10,8},{9,1... | collective-permute-start | bytes 1179656 | tf_op jit(solution)/shard_map/ppermute | solution.py:321

commit v8 on v7

--- a/solution.py
+++ b/solution.py
@@ -10,7 +10,7 @@
 SIZES = {"zh": 4, "zl": 2, "x": 4, "yh": 2, "c": 2}
 DP = ("zh", "zl", "x", "yh", "c")
 NEAR = ("yh", "x", "zl")
-FAR = ("zh", "zl", "x")
+FAR = ("x", "zh", "zl")
 QUAD = ("yh", "c")
 
 ROWS = 128
@@ -59,10 +59,14 @@
     return lax.axis_index(FAR), lax.axis_index(QUAD), lax.axis_index("mp")
 
 
+def quad_of(far):
+    return far % 8 * 4 + far // 8
+
+
 def start_of(window_ref):
     g, q, mp = place_of()
     lane = lax.broadcasted_iota(I32, (1, ROWS), 1)
-    block = jnp.where(lane == g * N_QUAD + q, window_ref[...], 0)
+    block = jnp.where(lane == quad_of(g) * N_QUAD + q, window_ref[...], 0)
     return jnp.sum(block, axis=1, keepdims=True) * A_DEV + mp * HALF
 
 
@@ -120,13 +124,13 @@
     ids = jnp.concatenate([ids[i] for i in range(N_FAR // 8)], axis=1)
     lane = lax.broadcasted_iota(I32, (1, ANCHORS), 1)
     partner = (ids[0:1] * float(ROWS) + ids[1:2]).astype(I32)
-    own = (lane // HALF * N_QUAD + q) * ROWS + ids[2:3].astype(I32)
+    own = (quad_of(lane // HALF) * N_QUAD + q) * ROWS + ids[2:3].astype(I32)
     return partner, own
 
 
 def column_ids(r):
     g, q, _ = place_of()
-    base = (g * N_QUAD + (q ^ r)) * ROWS
+    base = (quad_of(g) * N_QUAD + (q ^ r)) * ROWS
     return base + lax.broadcasted_iota(I32, (ROWS, 1), 0)
 
 

time: 107 us -> 107 us (level)
  blocking collectives: 55.5 us -> 54.1 us
  starting transfers between devices: 31.6 us -> 32.7 us
    all_to_all x4, blocking collectives: 55.5 us -> 54.1 us  [exchange(): return lax.all_to_all(value, axes, 0, 0, tiled=True)]
    ppermute x10, starting transfers between devices: 20.4 us -> 21.5 us  [swap(): return lax.ppermute(value, axes, [(i, i ^ flip) for i in range(count)])]
where the time goes in v8:
time: 107 us
  blocking collectives  54.1 us (51%)
  starting transfers between devices  32.7 us (31%)
  waiting for transfers between devices  12.2 us (11%)
  Pallas kernels  6.82 us (6%)
    all_to_all x4, blocking collectives, exchange(): return lax.all_to_all(value, axes, 0, 0, tiled=True)  54.1 us
    ppermute x10, starting transfers between devices, swap(): return lax.ppermute(value, axes, [(i, i ^ flip) for i in range(count)])  21.5 us
    ppermute x10, waiting for transfers between devices, swap(): return lax.ppermute(value, axes, [(i, i ^ flip) for i in range(count)])  12.2 us
    all_to_all x1, starting transfers between devices, exchange(): return lax.all_to_all(value, axes, 0, 0, tiled=True)  11.2 us
    pallas_call x12, Pallas kernels, call(): pl.pallas_call(kernel, out_shape=shapes, in_specs=specs, out_specs=[pl.Bl...  6.82 us
  transfers between devices with their start and end apart: 11, of which 8 were waited for; matrix products, arithmetic and copies ran while one was open for 0% of the time, Pallas kernels for 1%

profile of v8, /device:TPU:1, one launch (start us, length us, event | category | flops | bytes accessed | tf_op | source)
XLA Modules:
  0.0 106.5 jit_solution(16493293732998365994)
XLA Ops:
  0.6 1.4 %shard_map.93 = (f32[128,128]{1,0:T(8,128)S(1)}, f32[128,256]{1,0:T(8,128)S(1)}, bf16[128,256]{1,0:T(8,128)(2,1)S(1)}, s32[1,128]{1,0:T(1,128)S(1)}, s32[1,128]{1,0:T(1,128)S(1)}) custom-call(bf16[128,512]{1,0:T(8,128)(2,1)} %x_ref.3, bf16[512,256]{1,0:T(8,128)(2,1)} %w_in_ref.1, f32[1,256]{1,0:T(1,128)} %bitcast.9, bf16[256,128]{1,0:T(8,128)(2,1)} %w_out_ref.3, ...), custom_call_target="tpu_custom_call" | custom-call | tf_op jit(solution)/shard_map/pallas_call | solution.py:46
  2.0 2.2 %collective-permute-start = (f32[128,128]{1,0:T(8,128)S(1)}, f32[128,128]{1,0:T(8,128)S(1)}, u32[]{:S(2)}, u32[]{:S(2)}) collective-permute-start(f32[128,128]{1,0:T(8,128)S(1)} %get-tuple-element.25.part_ref), channel_id=1, source_target_pairs={{0,1},{1,0},{2,3},{3,2},{4,5},{5,4},{6,7},{7,6},{8,9},{9,8},{10,11... | collective-permute-start | bytes 196616 | tf_op jit(solution)/shard_map/ppermute | solution.py:325
  4.2 1.7 %collective-permute-done.other_ref = f32[128,128]{1,0:T(8,128)S(1)} collective-permute-done((f32[128,128]{1,0:T(8,128)S(1)}, f32[128,128]{1,0:T(8,128)S(1)}, u32[]{:S(2)}, u32[]{:S(2)}) %collective-permute-start) | collective-permute-done | bytes 65568 | tf_op jit(solution)/shard_map/ppermute | solution.py:325
  5.9 0.9 shard_map.94
  6.7 11.2 %all-to-all-start = ((bf16[32,24,128]{2,1,0:T(8,128)(2,1)}), bf16[32,24,128]{2,1,0:T(8,128)(2,1)S(1)}, u32[]{:S(2)}, u32[]{:S(2)}) async-start(bf16[32,24,128]{2,1,0:T(8,128)(2,1)} %get-tuple-element.27), calls=%async_computation | async-start | bytes 393216 | tf_op jit(solution)/shard_map/all_to_all | solution.py:329
  18.0 2.2 %collective-permute-start.1 = (bf16[128,128]{1,0:T(8,128)(2,1)S(1)}, bf16[128,128]{1,0:T(8,128)(2,1)S(1)}, u32[]{:S(2)}, u32[]{:S(2)}) collective-permute-start(bf16[128,128]{1,0:T(8,128)(2,1)S(1)} %get-tuple-element.28.e0_ref), channel_id=1, source_target_pairs={{0,2},{2,0},{4,6},{6,4},{1,3},{3,1},{5,7},{7,5},{8,10},{10,8},{12,... | collective-permute-start | bytes 98312 | tf_op jit(solution)/shard_map/ppermute | solution.py:325
  20.1 2.9 %collective-permute-start.2 = (bf16[128,128]{1,0:T(8,128)(2,1)S(1)}, bf16[128,128]{1,0:T(8,128)(2,1)S(1)}, u32[]{:S(2)}, u32[]{:S(2)}) collective-permute-start(bf16[128,128]{1,0:T(8,128)(2,1)S(1)} %get-tuple-element.28.e0_ref), channel_id=1, source_target_pairs={{0,4},{2,6},{4,0},{6,2},{1,5},{3,7},{5,1},{7,3},{8,12},{10,14},{12... | collective-permute-start | bytes 98312 | tf_op jit(solution)/shard_map/ppermute | solution.py:325
  23.4 1.0 collective-permute-done.2.e2_ref
  24.4 3.8 %collective-permute-done.3.e3_ref = bf16[128,128]{1,0:T(8,128)(2,1)S(1)} collective-permute-done((bf16[128,128]{1,0:T(8,128)(2,1)S(1)}, bf16[128,128]{1,0:T(8,128)(2,1)S(1)}, u32[]{:S(2)}, u32[]{:S(2)}) %collective-permute-start.3) | collective-permute-done | bytes 32800 | tf_op jit(solution)/shard_map/ppermute | solution.py:325
  28.2 1.1 %shard_map.95 = bf16[32,40,128]{2,1,0:T(8,128)(2,1)S(1)} custom-call(bf16[32,24,128]{2,1,0:T(8,128)(2,1)S(1)} %all-to-all-done.msg_ref, bf16[128,128]{1,0:T(8,128)(2,1)S(1)} %get-tuple-element.28.e0_ref, bf16[128,128]{1,0:T(8,128)(2,1)S(1)} %collective-permute-done.1.e1_ref, bf16[128,128]{1,0:T(8,128)(2,1)S(1)} %collective-permute-done.2.e2_ref, ...), custom_call_target="tpu_custom_call" | custom-call | tf_op jit(solution)/shard_map/pallas_call | solution.py:46
  29.4 19.5 %all_to_all.25.sums_ref = bf16[32,40,128]{2,1,0:T(8,128)(2,1)S(1)} all-to-all(bf16[32,40,128]{2,1,0:T(8,128)(2,1)S(1)} %shard_map.95), channel_id=1, replica_groups=mesh['zh'=4,'zl'=2,'x'=4,'yh'=2,'c'=2,'mp'=2] {'x','zh','zl'}, dimensions={0} | all-to-all | bytes 655360 | tf_op jit(solution)/shard_map/all_to_all | solution.py:329
  48.9 0.9 shard_map.96
  49.8 3.9 %collective-permute-start.4 = (f32[2,128,128]{2,1,0:T(8,128)S(1)}, f32[2,128,128]{2,1,0:T(8,128)S(1)}, u32[]{:S(2)}, u32[]{:S(2)}) collective-permute-start(f32[2,128,128]{2,1,0:T(8,128)S(1)} %get-tuple-element.30), channel_id=1, source_target_pairs={{0,2},{2,0},{1,3},{3,1},{4,6},{6,4},{5,7},{7,5},{8,10},{10,8},{9,1... | collective-permute-start | bytes 393224 | tf_op jit(solution)/shard_map/ppermute | solution.py:325
  53.9 0.8 collective-permute-done.4.b_ref
  55.3 1.6 %collective-permute-start.6 = (f32[128,128]{1,0:T(8,128)S(1)}, f32[128,128]{1,0:T(8,128)S(1)}, u32[]{:S(2)}, u32[]{:S(2)}) collective-permute-start(f32[128,128]{1,0:T(8,128)S(1)} %get-tuple-element.32), channel_id=1, source_target_pairs={{0,4},{4,0},{1,5},{5,1},{2,6},{6,2},{3,7},{7,3},{8,12},{12,8},{9,1... | collective-permute-start | bytes 196616 | tf_op jit(solution)/shard_map/ppermute | solution.py:325
  56.8 1.9 %collective-permute-start.7 = (f32[128,128]{1,0:T(8,128)S(1)}, f32[128,128]{1,0:T(8,128)S(1)}, u32[]{:S(2)}, u32[]{:S(2)}) collective-permute-start(f32[128,128]{1,0:T(8,128)S(1)} %get-tuple-element.32), channel_id=1, source_target_pairs={{0,5},{1,4},{4,1},{5,0},{2,7},{3,6},{6,3},{7,2},{8,13},{9,12},{12,... | collective-permute-start | bytes 196616 | tf_op jit(solution)/shard_map/ppermute | solution.py:325
  58.7 1.3 %collective-permute-done.6.third_ref = f32[128,128]{1,0:T(8,128)S(1)} collective-permute-done((f32[128,128]{1,0:T(8,128)S(1)}, f32[128,128]{1,0:T(8,128)S(1)}, u32[]{:S(2)}, u32[]{:S(2)}) %collective-permute-start.6) | collective-permute-done | bytes 65568 | tf_op jit(solution)/shard_map/ppermute | solution.py:325
  60.0 1.6 %collective-permute-done.7.fourth_ref = f32[128,128]{1,0:T(8,128)S(1)} collective-permute-done((f32[128,128]{1,0:T(8,128)S(1)}, f32[128,128]{1,0:T(8,128)S(1)}, u32[]{:S(2)}, u32[]{:S(2)}) %collective-permute-start.7) | collective-permute-done | bytes 65568 | tf_op jit(solution)/shard_map/ppermute | solution.py:325
  62.3 1.6 %collective-permute-start.8 = (f32[16,48,128]{2,1,0:T(8,128)S(1)}, f32[16,48,128]{2,1,0:T(8,128)S(1)}, u32[]{:S(2)}, u32[]{:S(2)}) collective-permute-start(f32[16,48,128]{2,1,0:T(8,128)S(1)} %get-tuple-element.36), channel_id=1, source_target_pairs={{0,2},{2,0},{1,3},{3,1},{4,6},{6,4},{5,7},{7,5},{8,10},{10,8},{9,1... | collective-permute-start | bytes 1179656 | tf_op jit(solution)/shard_map/ppermute | solution.py:325
  63.9 1.3 %collective-permute-done.8.b_ref = f32[16,48,128]{2,1,0:T(8,128)S(1)} collective-permute-done((f32[16,48,128]{2,1,0:T(8,128)S(1)}, f32[16,48,128]{2,1,0:T(8,128)S(1)}, u32[]{:S(2)}, u32[]{:S(2)}) %collective-permute-start.8) | collective-permute-done | bytes 393248 | tf_op jit(solution)/shard_map/ppermute | solution.py:325
  65.3 12.5 %all_to_all.26.in_ref = f32[16,48,128]{2,1,0:T(8,128)S(1)} all-to-all(f32[16,48,128]{2,1,0:T(8,128)S(1)} %shard_map.100), channel_id=1, replica_groups=mesh['zh'=4,'zl'=2,'x'=4,'yh'=2,'c'=2,'mp'=2] {'yh','x','zl'}, dimensions={0} | all-to-all | bytes 786432 | tf_op jit(solution)/shard_map/all_to_all | solution.py:329
  77.9 9.4 %all_to_all.27.in_ref = f32[4,48,128]{2,1,0:T(8,128)S(1)} all-to-all(f32[4,48,128]{2,1,0:T(8,128)S(1)} %shard_map.101), channel_id=1, replica_groups=mesh['zh'=4,'zl'=2,'x'=4,'yh'=2,'c'=2,'mp'=2] {'zh'}, dimensions={0} | all-to-all | bytes 196608 | tf_op jit(solution)/shard_map/all_to_all | solution.py:329
  87.3 12.6 %all_to_all.28.mine_ref = f32[16,48,128]{2,1,0:T(8,128)S(1)} all-to-all(f32[16,48,128]{2,1,0:T(8,128)S(1)} %shard_map.102), channel_id=1, replica_groups=mesh['zh'=4,'zl'=2,'x'=4,'yh'=2,'c'=2,'mp'=2] {'yh','x','zl'}, dimensions={0} | all-to-all | bytes 786432 | tf_op jit(solution)/shard_map/all_to_all | solution.py:329
  100.0 4.5 %collective-permute-start.9 = (f32[16,48,128]{2,1,0:T(8,128)S(1)}, f32[16,48,128]{2,1,0:T(8,128)S(1)}, u32[]{:S(2)}, u32[]{:S(2)}) collective-permute-start(f32[16,48,128]{2,1,0:T(8,128)S(1)} %all_to_all.28.mine_ref), channel_id=1, source_target_pairs={{0,2},{2,0},{1,3},{3,1},{4,6},{6,4},{5,7},{7,5},{8,10},{10,8},{9,1... | collective-permute-start | bytes 1179656 | tf_op jit(solution)/shard_map/ppermute | solution.py:325
  (18 shorter events, 3.9 us)
Async XLA Ops:
  2.0 3.9 %collective-permute-start = (f32[128,128]{1,0:T(8,128)S(1)}, f32[128,128]{1,0:T(8,128)S(1)}, u32[]{:S(2)}, u32[]{:S(2)}) collective-permute-start(f32[128,128]{1,0:T(8,128)S(1)} %get-tuple-element.25.part_ref), channel_id=1, source_target_pairs={{0,1},{1,0},{2,3},{3,2},{4,5},{5,4},{6,7},{7,6},{8,9},{9,8},{10,11... | collective-permute-start | bytes 196616 | tf_op jit(solution)/shard_map/ppermute | solution.py:325
  6.7 21.5 %all-to-all-start = ((bf16[32,24,128]{2,1,0:T(8,128)(2,1)}), bf16[32,24,128]{2,1,0:T(8,128)(2,1)S(1)}, u32[]{:S(2)}, u32[]{:S(2)}) async-start(bf16[32,24,128]{2,1,0:T(8,128)(2,1)} %get-tuple-element.27), calls=%async_computation | async-start | bytes 393216 | tf_op jit(solution)/shard_map/all_to_all | solution.py:329
  18.0 5.4 %collective-permute-start.1 = (bf16[128,128]{1,0:T(8,128)(2,1)S(1)}, bf16[128,128]{1,0:T(8,128)(2,1)S(1)}, u32[]{:S(2)}, u32[]{:S(2)}) collective-permute-start(bf16[128,128]{1,0:T(8,128)(2,1)S(1)} %get-tuple-element.28.e0_ref), channel_id=1, source_target_pairs={{0,2},{2,0},{4,6},{6,4},{1,3},{3,1},{5,7},{7,5},{8,10},{10,8},{12,... | collective-permute-start | bytes 98312 | tf_op jit(solution)/shard_map/ppermute | solution.py:325
  20.1 4.3 %collective-permute-start.2 = (bf16[128,128]{1,0:T(8,128)(2,1)S(1)}, bf16[128,128]{1,0:T(8,128)(2,1)S(1)}, u32[]{:S(2)}, u32[]{:S(2)}) collective-permute-start(bf16[128,128]{1,0:T(8,128)(2,1)S(1)} %get-tuple-element.28.e0_ref), channel_id=1, source_target_pairs={{0,4},{2,6},{4,0},{6,2},{1,5},{3,7},{5,1},{7,3},{8,12},{10,14},{12... | collective-permute-start | bytes 98312 | tf_op jit(solution)/shard_map/ppermute | solution.py:325
  23.1 5.2 %collective-permute-start.3 = (bf16[128,128]{1,0:T(8,128)(2,1)S(1)}, bf16[128,128]{1,0:T(8,128)(2,1)S(1)}, u32[]{:S(2)}, u32[]{:S(2)}) collective-permute-start(bf16[128,128]{1,0:T(8,128)(2,1)S(1)} %get-tuple-element.28.e0_ref), channel_id=1, source_target_pairs={{0,6},{2,4},{4,2},{6,0},{1,7},{3,5},{5,3},{7,1},{8,14},{10,12},{12... | collective-permute-start | bytes 98312 | tf_op jit(solution)/shard_map/ppermute | solution.py:325
  49.8 4.9 %collective-permute-start.4 = (f32[2,128,128]{2,1,0:T(8,128)S(1)}, f32[2,128,128]{2,1,0:T(8,128)S(1)}, u32[]{:S(2)}, u32[]{:S(2)}) collective-permute-start(f32[2,128,128]{2,1,0:T(8,128)S(1)} %get-tuple-element.30), channel_id=1, source_target_pairs={{0,2},{2,0},{1,3},{3,1},{4,6},{6,4},{5,7},{7,5},{8,10},{10,8},{9,1... | collective-permute-start | bytes 393224 | tf_op jit(solution)/shard_map/ppermute | solution.py:325
  54.7 7.0 %copy-start = (bf16[128,512]{1,0:T(8,128)(2,1)S(1)}, bf16[128,512]{1,0:T(8,128)(2,1)}, u32[]{:S(2)}) copy-start(bf16[128,512]{1,0:T(8,128)(2,1)} %x_ref.3) | copy-start | bytes 393220
  54.7 7.0 %copy-start.1 = (bf16[256,128]{1,0:T(8,128)(2,1)S(1)}, bf16[256,128]{1,0:T(8,128)(2,1)}, u32[]{:S(2)}) copy-start(bf16[256,128]{1,0:T(8,128)(2,1)} %w_out_ref.3) | copy-start | bytes 196612
  54.8 6.9 %collective-permute-start.5 = (f32[136,128]{1,0:T(8,128)S(1)}, f32[136,128]{1,0:T(8,128)S(1)}, u32[]{:S(2)}, u32[]{:S(2)}) collective-permute-start(f32[136,128]{1,0:T(8,128)S(1)} %get-tuple-element.31.mine_ref), channel_id=1, source_target_pairs={{0,1},{1,0},{2,3},{3,2},{4,5},{5,4},{6,7},{7,6},{8,9},{9,8},{10,11... | collective-permute-start | bytes 208904 | tf_op jit(solution)/shard_map/ppermute | solution.py:325
  55.3 4.8 %collective-permute-start.6 = (f32[128,128]{1,0:T(8,128)S(1)}, f32[128,128]{1,0:T(8,128)S(1)}, u32[]{:S(2)}, u32[]{:S(2)}) collective-permute-start(f32[128,128]{1,0:T(8,128)S(1)} %get-tuple-element.32), channel_id=1, source_target_pairs={{0,4},{4,0},{1,5},{5,1},{2,6},{6,2},{3,7},{7,3},{8,12},{12,8},{9,1... | collective-permute-start | bytes 196616 | tf_op jit(solution)/shard_map/ppermute | solution.py:325
  56.8 4.9 %collective-permute-start.7 = (f32[128,128]{1,0:T(8,128)S(1)}, f32[128,128]{1,0:T(8,128)S(1)}, u32[]{:S(2)}, u32[]{:S(2)}) collective-permute-start(f32[128,128]{1,0:T(8,128)S(1)} %get-tuple-element.32), channel_id=1, source_target_pairs={{0,5},{1,4},{4,1},{5,0},{2,7},{3,6},{6,3},{7,2},{8,13},{9,12},{12,... | collective-permute-start | bytes 196616 | tf_op jit(solution)/shard_map/ppermute | solution.py:325
  62.3 3.0 %collective-permute-start.8 = (f32[16,48,128]{2,1,0:T(8,128)S(1)}, f32[16,48,128]{2,1,0:T(8,128)S(1)}, u32[]{:S(2)}, u32[]{:S(2)}) collective-permute-start(f32[16,48,128]{2,1,0:T(8,128)S(1)} %get-tuple-element.36), channel_id=1, source_target_pairs={{0,2},{2,0},{1,3},{3,1},{4,6},{6,4},{5,7},{7,5},{8,10},{10,8},{9,1... | collective-permute-start | bytes 1179656 | tf_op jit(solution)/shard_map/ppermute | solution.py:325
  100.0 5.8 %collective-permute-start.9 = (f32[16,48,128]{2,1,0:T(8,128)S(1)}, f32[16,48,128]{2,1,0:T(8,128)S(1)}, u32[]{:S(2)}, u32[]{:S(2)}) collective-permute-start(f32[16,48,128]{2,1,0:T(8,128)S(1)} %all_to_all.28.mine_ref), channel_id=1, source_target_pairs={{0,2},{2,0},{1,3},{3,1},{4,6},{6,4},{5,7},{7,5},{8,10},{10,8},{9,1... | collective-permute-start | bytes 1179656 | tf_op jit(solution)/shard_map/ppermute | solution.py:325
